TPU v7x, 512 devices: a whole 4x4x16 slice. The times are simulated.
512 devices in a mesh: blk: 8 (over z_lo), stripe: 64 (over y, x, z_hi, core).
Axes of the slice: x: 4, y: 4, z: 16 (z_hi: 2, z_lo: 8; z = z_hi * 8 + z_lo), core: 2. Of those that a mesh axis runs over, the one named last changes fastest.
Arguments:
- points: bfloat16 [262144, 64], P(('blk', 'stripe')), may hold values from -6 to 6
- coefficients: float32 [262144], P(('blk', 'stripe')), may hold values from -0.0234375 to 0.0234375
- velocity: float32 [262144], P(('blk', 'stripe')), may hold values from -0.0234375 to 0.0234375
- targets: float32 [262144], P(('blk', 'stripe')), may hold values from -6 to 6
- batch_rows: int32 [32768], P(('blk', 'stripe')), may hold values from 0 to 511
- counts: int32 [8, 64], P('blk', 'stripe'), may hold values from 1 to 64, 2048 in all within a row
Outputs:
- new_coefficients: float32 [262144], P(('blk', 'stripe'))
- new_velocity: float32 [262144], P(('blk', 'stripe'))
Inputs may be any that keep to these rules, and one draw needn't show every extreme that they name: In every index of blk, the counts of its 64 devices sum to exactly 2048, and some device's count is exactly 64. Only the first count entries of a device's slots are live. `batch_rows`: every entry, live or not, indexes the points of the device that holds it; rows may repeat.
All inputs are finite; a program needn't handle non-finite values.
Results may differ from a plain program's by a relative error of at most 0.0003.
Values may be sent and summed in bfloat16 or wider, within the bound.
A program may use at most 64 MiB of HBM per device.

v0:
```python
import math

import jax
import jax.numpy as jnp
from jax import lax
from jax.sharding import PartitionSpec as P

MOMENTUM = 0.9
STEP_SIZE = 1.0
NOISE_VAR = 8.0
KERNEL_RATE = 3.0**0.5 / 6.0


def matern_sums(row_feats, row_sq, col_points, col_coef):
    col_sq = jnp.sum(jnp.square(col_points.astype(jnp.float32)), axis=1)
    inner_prod = lax.dot_general(
        row_feats, col_points, (((1,), (1,)), ((), ())), preferred_element_type=jnp.float32
    )
    distance = jnp.sqrt(jnp.maximum(row_sq[:, None] + col_sq[None, :] - 2.0 * inner_prod, 0.0))
    scaled = KERNEL_RATE * distance
    kernel_tile = (1.0 + scaled) * jnp.exp(-scaled)
    return jnp.sum(kernel_tile * col_coef[None, :], axis=1)


def column_sums(row_feats, points, preview):
    row_sq = jnp.sum(jnp.square(row_feats.astype(jnp.float32)), axis=1)
    every_coef = lax.all_gather(preview, "blk", axis=0, tiled=True)
    zeros_init = jnp.zeros((row_feats.shape[0],), jnp.float32)
    piece_points = lax.all_gather(points, "blk", axis=0, tiled=True)
    piece_len = piece_points.shape[0]
    block_len = math.gcd(piece_len, 512)
    point_blocks = piece_points.reshape(-1, block_len, piece_points.shape[1])
    coef_blocks = every_coef.reshape(-1, block_len)

    def advance(partial_sum, column_block):
        return (
            partial_sum + matern_sums(row_feats, row_sq, column_block[0], column_block[1]),
            None,
        )

    result, unused = lax.scan(advance, zeros_init, (point_blocks, coef_blocks))
    return result


def per_device(points, coefficients, velocity, targets, batch_rows, counts):
    preview = coefficients + MOMENTUM * velocity
    slot_total = batch_rows.shape[0]
    local_size = points.shape[0]
    slot_ids = jnp.arange(slot_total, dtype=jnp.int32)
    count_here = counts.reshape((1,))
    in_count = slot_ids < count_here[0]
    picked = jnp.take(points, batch_rows, axis=0)
    group_rows = lax.all_gather(picked, "stripe", axis=0, tiled=True)
    partial_value = column_sums(group_rows, points, preview)
    kernel_rows = lax.psum_scatter(partial_value, "stripe", scatter_dimension=0, tiled=True)
    residual = jnp.where(
        in_count,
        kernel_rows + NOISE_VAR * jnp.take(preview, batch_rows) - jnp.take(targets, batch_rows),
        0.0,
    )
    scatter_rows = (batch_rows[:, None] == jnp.arange(local_size, dtype=jnp.int32)[None, :]).astype(
        jnp.float32
    )
    update_sum = jnp.dot(residual, scatter_rows, precision=lax.Precision.HIGHEST)
    new_velocity = MOMENTUM * velocity - STEP_SIZE * update_sum
    new_coefficients = coefficients + new_velocity
    return (new_coefficients, new_velocity)


def solution(mesh):
    in_specs = (
        P(("blk", "stripe"), None),
        P(("blk", "stripe")),
        P(("blk", "stripe")),
        P(("blk", "stripe")),
        P(("blk", "stripe")),
        P("blk", "stripe"),
    )
    out_specs = (P(("blk", "stripe")), P(("blk", "stripe")))
    return jax.shard_map(
        per_device, mesh=mesh, in_specs=in_specs, out_specs=out_specs, check_vma=False
    )
```

profile of v0, /device:TPU:0, one launch (start us, length us, event | category | flops | bytes accessed | tf_op | source)
XLA Modules:
  0.0 869.1 jit_solution(8727007130608261097)
XLA Ops:
  0.6 0.0 copy-start
  0.6 0.0 copy-start.1
  1.3 1.3 dynamic-slice
  3.3 0.7 compare_and_fusion
  3.9 0.7 compare_select_fusion
  4.6 0.7 multiply_add_fusion
  5.3 0.0 copy-done
  5.3 0.8 gather_fusion.2
  6.1 0.8 gather_fusion.1
  6.9 42.5 %all-gather = f32[8,1,512]{2,1,0:T(1,128)S(1)} all-gather(f32[1,1,512]{2,1,0:T(1,128)S(1)} %bitcast.38), channel_id=1, replica_groups=mesh['blk'=8,'stripe'=64] {'blk'}, dimensions={0}, use_global_device_ids=true | all-gather | bytes 18432 | tf_op jit(solution)/shard_map/all_gather | solution.py:27
  49.4 0.0 copy-done.1
  49.4 0.1 copy.12
  49.6 0.6 gather_fusion
  50.2 0.1 broadcast_select_fusion
  50.3 48.1 %all_gather.10 = bf16[4096,64]{0,1:T(8,128)(2,1)S(1)} all-gather(bf16[512,64]{0,1:T(8,128)(2,1)S(1)} %copy-done.1), channel_id=1, replica_groups=mesh['blk'=8,'stripe'=64] {'blk'}, dimensions={0}, use_global_device_ids=true | all-gather | bytes 589824 | tf_op jit(solution)/shard_map/all_gather | solution.py:29
  98.3 0.5 copy.13
  98.8 165.1 %all_gather.9 = bf16[4096,64]{1,0:T(8,128)(2,1)S(1)} all-gather(bf16[64,64]{1,0:T(8,128)(2,1)S(1)} %broadcast_select_fusion), channel_id=1, replica_groups=mesh['blk'=8,'stripe'=64] {'stripe'}, dimensions={0}, use_global_device_ids=true | all-gather | bytes 532480 | tf_op jit(solution)/shard_map/all_gather | solution.py:53
  264.0 0.6 multiply_reduce_fusion.2
  264.6 0.0 copy-start.4
  264.6 0.0 copy-start.2
  264.6 0.0 copy-start.3
  264.6 49.5 %while.11 = (s32[]{:T(128)}, f32[4096]{0:T(1024)S(1)}, f32[4096]{0:T(1024)S(1)}, bf16[8,512,64]{2,1,0:T(8,128)(2,1)S(1)}, bf16[4096,64]{1,0:T(8,128)(2,1)S(1)}, /*index=5*/f32[8,512]{1,0:T(8,128)S(1)}, s32[]{:T(128)}, s32[]{:T(128)}) while((s32[]{:T(128)}, f32[4096]{0:T(1024)S(1)}, f32[4096]{0:T(1024)S(1)}, ...), condition=%wide.region_4.5_spmd.clone, body=%wide.region_1.0_spmd.clone.sunk | while | flops 289508864 | bytes 1337459 | solution.py:41
  264.7 0.2 multiply_reduce_fusion.5
  264.8 6.0 multiply_reduce_fusion.6
  270.8 0.2 multiply_reduce_fusion.5
  271.0 6.0 multiply_reduce_fusion.6
  277.0 0.2 multiply_reduce_fusion.5
  277.2 6.0 multiply_reduce_fusion.6
  283.2 0.2 multiply_reduce_fusion.5
  283.4 6.0 multiply_reduce_fusion.6
  289.4 0.2 multiply_reduce_fusion.5
  289.6 6.0 multiply_reduce_fusion.6
  295.6 0.2 multiply_reduce_fusion.5
  295.8 6.0 multiply_reduce_fusion.6
  301.8 0.2 multiply_reduce_fusion.5
  302.0 6.0 multiply_reduce_fusion.6
  308.0 0.2 multiply_reduce_fusion.5
  308.2 6.0 multiply_reduce_fusion.6
  314.2 554.0 %all-reduce = f32[4096]{0:T(1024)S(1)} all-reduce(f32[4096]{0:T(1024)S(1)} %get-tuple-element.35), channel_id=2, replica_groups=mesh['blk'=8,'stripe'=64] {'stripe'}, use_global_device_ids=true, to_apply=%region_5.6.clone | all-reduce | flops 4096 | bytes 32768
  868.2 0.0 copy-done.4
  868.2 0.2 fusion.6
  868.5 0.0 copy-done.2
  868.5 0.0 copy-done.3
  868.5 0.6 fusion.21
  (19 shorter events, 0.1 us)
Async XLA Ops:
  0.6 4.7 copy-start
  0.6 48.8 %copy-start.1 = (bf16[512,64]{0,1:T(8,128)(2,1)S(1)}, bf16[512,64]{0,1:T(8,128)(2,1)}, u32[]{:S(2)}) copy-start(bf16[512,64]{0,1:T(8,128)(2,1)} %param.10) | copy-start | bytes 196612
  264.6 603.6 %copy-start.4 = (s32[64]{0:T(128)S(1)}, s32[64]{0:T(128)}, u32[]{:S(2)}) copy-start(s32[64]{0:T(128)} %param.14) | copy-start | bytes 772
  264.6 603.9 %copy-start.2 = (f32[512]{0:T(512)S(1)}, f32[512]{0:T(512)}, u32[]{:S(2)}) copy-start(f32[512]{0:T(512)} %param.11) | copy-start | bytes 6148
  264.6 603.8 %copy-start.3 = (f32[512]{0:T(512)S(1)}, f32[512]{0:T(512)}, u32[]{:S(2)}) copy-start(f32[512]{0:T(512)} %param.12) | copy-start | bytes 6148
where the time goes:
time: 869 us
  blocking collectives  810 us (93%)
  matrix products  48.1 us (6%)
    unnamed x1, blocking collectives  554 us
    all_gather x1, blocking collectives, per_device(): group_rows = lax.all_gather(picked, 'stripe', axis=0, tiled=True)  165 us
    all_gather x1, blocking collectives, column_sums(): piece_points = lax.all_gather(points, 'blk', axis=0, tiled=True)  48.1 us
    dot_general x8, matrix products, matern_sums(): lax.dot_general(row_feats, col_points, (((1,), (1,)), ((), ())), preferre...  47.9 us
    all_gather x1, blocking collectives, column_sums(): every_coef = lax.all_gather(preview, 'blk', axis=0, tiled=True)  42.5 us

commit v1 on v0

--- a/solution.py
+++ b/solution.py
@@ -1,8 +1,11 @@
+import functools
 import math
 
 import jax
 import jax.numpy as jnp
 from jax import lax
+from jax.experimental import pallas as pl
+from jax.experimental.pallas import tpu as pltpu
 from jax.sharding import PartitionSpec as P
 
 MOMENTUM = 0.9
@@ -10,6 +13,129 @@
 NOISE_VAR = 8.0
 KERNEL_RATE = 3.0**0.5 / 6.0
 
+MESH_ID = pl.DeviceIdType.MESH
+ANY = pl.BlockSpec(memory_space=pl.ANY)
+
+
+def gather_kernel(n_blk, n_str, picked, pts, prev, rows_out, pts_out, prev_out,
+                  row_send, row_recv, pt_send, pt_recv, pv_send, pv_recv, local_sem):
+    b = lax.axis_index("blk")
+    s = lax.axis_index("stripe")
+    own = [
+        pltpu.make_async_copy(picked, rows_out.at[s], local_sem.at[0]),
+        pltpu.make_async_copy(pts, pts_out.at[b], local_sem.at[1]),
+        pltpu.make_async_copy(prev, prev_out.at[b], local_sem.at[2]),
+    ]
+    for c in own:
+        c.start()
+
+    def row_copy(i, src):
+        peer = lax.rem(s + 1 + i, n_str)
+        return pltpu.make_async_remote_copy(
+            src_ref=picked, dst_ref=rows_out.at[src], send_sem=row_send.at[i],
+            recv_sem=row_recv.at[src], device_id=(b, peer), device_id_type=MESH_ID)
+
+    def blk_copies(i, src):
+        peer = lax.rem(b + 1 + i, n_blk)
+        return (
+            pltpu.make_async_remote_copy(
+                src_ref=pts, dst_ref=pts_out.at[src], send_sem=pt_send.at[i],
+                recv_sem=pt_recv.at[src], device_id=(peer, s), device_id_type=MESH_ID),
+            pltpu.make_async_remote_copy(
+                src_ref=prev, dst_ref=prev_out.at[src], send_sem=pv_send.at[i],
+                recv_sem=pv_recv.at[src], device_id=(peer, s), device_id_type=MESH_ID),
+        )
+
+    def start_blk(i, carry):
+        for c in blk_copies(i, b):
+            c.start()
+        return carry
+
+    def start_row(i, carry):
+        row_copy(i, s).start()
+        return carry
+
+    lax.fori_loop(0, n_blk - 1, start_blk, 0)
+    lax.fori_loop(0, n_str - 1, start_row, 0)
+
+    def wait_row(i, carry):
+        row_copy(i, s).wait_send()
+        src = lax.rem(s + 2 * n_str - 1 - i, n_str)
+        row_copy(i, src).wait_recv()
+        return carry
+
+    def wait_blk(i, carry):
+        for c in blk_copies(i, b):
+            c.wait_send()
+        src = lax.rem(b + 2 * n_blk - 1 - i, n_blk)
+        for c in blk_copies(i, src):
+            c.wait_recv()
+        return carry
+
+    lax.fori_loop(0, n_blk - 1, wait_blk, 0)
+    lax.fori_loop(0, n_str - 1, wait_row, 0)
+    for c in own:
+        c.wait()
+
+
+def gather_all(picked, pts, prev, n_blk, n_str):
+    dma = pltpu.SemaphoreType.DMA
+    return pl.pallas_call(
+        functools.partial(gather_kernel, n_blk, n_str),
+        out_shape=(
+            jax.ShapeDtypeStruct((n_str,) + picked.shape, picked.dtype),
+            jax.ShapeDtypeStruct((n_blk,) + pts.shape, pts.dtype),
+            jax.ShapeDtypeStruct((n_blk,) + prev.shape, prev.dtype),
+        ),
+        in_specs=[ANY, ANY, ANY],
+        out_specs=(ANY, ANY, ANY),
+        scratch_shapes=[
+            dma((n_str,)), dma((n_str,)), dma((n_blk,)), dma((n_blk,)),
+            dma((n_blk,)), dma((n_blk,)), dma((3,)),
+        ],
+        compiler_params=pltpu.CompilerParams(has_side_effects=True),
+    )(picked, pts, prev)
+
+
+def scatter_kernel(n_str, part, recv_out, send_sem, recv_sem, local_sem):
+    b = lax.axis_index("blk")
+    s = lax.axis_index("stripe")
+    own = pltpu.make_async_copy(part.at[s], recv_out.at[s], local_sem.at[0])
+    own.start()
+
+    def copy(i, src):
+        peer = lax.rem(s + 1 + i, n_str)
+        return pltpu.make_async_remote_copy(
+            src_ref=part.at[peer], dst_ref=recv_out.at[src], send_sem=send_sem.at[i],
+            recv_sem=recv_sem.at[src], device_id=(b, peer), device_id_type=MESH_ID)
+
+    def start(i, carry):
+        copy(i, s).start()
+        return carry
+
+    lax.fori_loop(0, n_str - 1, start, 0)
+
+    def wait(i, carry):
+        copy(i, s).wait_send()
+        src = lax.rem(s + 2 * n_str - 1 - i, n_str)
+        copy(i, src).wait_recv()
+        return carry
+
+    lax.fori_loop(0, n_str - 1, wait, 0)
+    own.wait()
+
+
+def scatter_all(part, n_str):
+    dma = pltpu.SemaphoreType.DMA
+    return pl.pallas_call(
+        functools.partial(scatter_kernel, n_str),
+        out_shape=jax.ShapeDtypeStruct(part.shape, part.dtype),
+        in_specs=[ANY],
+        out_specs=ANY,
+        scratch_shapes=[dma((n_str,)), dma((n_str,)), dma((1,))],
+        compiler_params=pltpu.CompilerParams(has_side_effects=True),
+    )(part)
+
 
 def matern_sums(row_feats, row_sq, col_points, col_coef):
     col_sq = jnp.sum(jnp.square(col_points.astype(jnp.float32)), axis=1)
@@ -22,11 +148,9 @@
     return jnp.sum(kernel_tile * col_coef[None, :], axis=1)
 
 
-def column_sums(row_feats, points, preview):
+def column_sums(row_feats, piece_points, every_coef):
     row_sq = jnp.sum(jnp.square(row_feats.astype(jnp.float32)), axis=1)
-    every_coef = lax.all_gather(preview, "blk", axis=0, tiled=True)
     zeros_init = jnp.zeros((row_feats.shape[0],), jnp.float32)
-    piece_points = lax.all_gather(points, "blk", axis=0, tiled=True)
     piece_len = piece_points.shape[0]
     block_len = math.gcd(piece_len, 512)
     point_blocks = piece_points.reshape(-1, block_len, piece_points.shape[1])
@@ -42,7 +166,7 @@
     return result
 
 
-def per_device(points, coefficients, velocity, targets, batch_rows, counts):
+def per_device(n_blk, n_str, points, coefficients, velocity, targets, batch_rows, counts):
     preview = coefficients + MOMENTUM * velocity
     slot_total = batch_rows.shape[0]
     local_size = points.shape[0]
@@ -50,9 +174,13 @@
     count_here = counts.reshape((1,))
     in_count = slot_ids < count_here[0]
     picked = jnp.take(points, batch_rows, axis=0)
-    group_rows = lax.all_gather(picked, "stripe", axis=0, tiled=True)
-    partial_value = column_sums(group_rows, points, preview)
-    kernel_rows = lax.psum_scatter(partial_value, "stripe", scatter_dimension=0, tiled=True)
+    rows_all, pts_all, prev_all = gather_all(picked, points, preview.reshape(1, -1), n_blk, n_str)
+    group_rows = rows_all.reshape(-1, points.shape[1])
+    piece_points = pts_all.reshape(-1, points.shape[1])
+    every_coef = prev_all.reshape(-1)
+    partial_value = column_sums(group_rows, piece_points, every_coef)
+    received = scatter_all(partial_value.reshape(n_str, 1, slot_total), n_str)
+    kernel_rows = jnp.sum(received.reshape(n_str, slot_total), axis=0)
     residual = jnp.where(
         in_count,
         kernel_rows + NOISE_VAR * jnp.take(preview, batch_rows) - jnp.take(targets, batch_rows),
@@ -68,6 +196,8 @@
 
 
 def solution(mesh):
+    n_blk = mesh.shape["blk"]
+    n_str = mesh.shape["stripe"]
     in_specs = (
         P(("blk", "stripe"), None),
         P(("blk", "stripe")),
@@ -78,5 +208,6 @@
     )
     out_specs = (P(("blk", "stripe")), P(("blk", "stripe")))
     return jax.shard_map(
-        per_device, mesh=mesh, in_specs=in_specs, out_specs=out_specs, check_vma=False
-    )
+        functools.partial(per_device, n_blk, n_str), mesh=mesh, in_specs=in_specs,
+        out_specs=out_specs, check_vma=False
+    )

time: 869 us -> 214 us (0.25)
  the two profiles are of different devices: /device:TPU:0 before, /device:TPU:1 now
where the time goes in v1:
time: 214 us
  Pallas kernels  153 us (71%)
  matrix products  48.3 us (23%)
  other arithmetic  6.61 us (3%)
  local copies, waits for them, and re-layouts  4.08 us (2%)
    pallas_call x1, Pallas kernels, gather_all(): pl.pallas_call(functools.partial(gather_kernel, n_blk, n_str), out_shape=...  82.2 us
    pallas_call x1, Pallas kernels, scatter_all(): pl.pallas_call(functools.partial(scatter_kernel, n_str), out_shape=jax.Sh...  71.1 us
    dot_general x8, matrix products, matern_sums(): lax.dot_general(row_feats, col_points, (((1,), (1,)), ((), ())), preferre...  48.1 us

profile of v1, /device:TPU:1, one launch (start us, length us, event | category | flops | bytes accessed | tf_op | source)
XLA Modules:
  0.0 214.0 jit_solution(17480770192345802595)
XLA Ops:
  0.6 0.0 copy-start
  0.6 0.7 compare_select_fusion
  1.3 1.0 copy.10.pts
  2.3 0.0 copy-start.2
  2.3 0.6 gather_fusion
  2.9 0.7 compare_and_fusion
  3.6 0.7 broadcast_select_fusion.picked
  4.3 1.3 multiply_add_fusion
  5.5 0.0 copy-done.2
  5.5 82.2 %shard_map.77 = (bf16[64,64,64]{2,1,0:T(8,128)(2,1)S(1)}, bf16[8,512,64]{2,1,0:T(8,128)(2,1)S(1)}, f32[8,1,512]{2,1,0:T(1,128)}) custom-call(bf16[64,64]{1,0:T(8,128)(2,1)} %broadcast_select_fusion.picked, bf16[512,64]{1,0:T(8,128)(2,1)} %copy-done.2, f32[1,512]{1,0:T(1,128)} %bitcast.37), custom_call_target="tpu_custom_call" | custom-call | tf_op jit(solution)/shard_map/pallas_call | solution.py:83
  87.8 0.0 copy-start.3
  87.8 0.6 multiply_reduce_fusion.2
  88.4 0.1 reduce_sum.39
  88.5 0.0 copy-done.3
  88.5 0.0 copy-start.1
  88.5 49.8 %while.11 = (s32[]{:T(128)}, f32[4096]{0:T(1024)S(1)}, f32[4096]{0:T(1024)S(1)}, bf16[8,512,64]{2,1,0:T(8,128)(2,1)S(1)}, bf16[4096,64]{1,0:T(8,128)(2,1)S(1)}, /*index=5*/f32[8,512]{1,0:T(8,128)S(1)}, s32[]{:T(128)}, s32[]{:T(128)}) while((s32[]{:T(128)}, f32[4096]{0:T(1024)S(1)}, f32[4096]{0:T(1024)S(1)}, ...), condition=%wide.region_4.5_spmd.clone, body=%wide.region_1.0_spmd.clone.sunk | while | flops 289508864 | bytes 1337451 | solution.py:165
  88.5 0.2 multiply_reduce_fusion.5
  88.7 6.0 %multiply_reduce_fusion.6 = f32[4096]{0:T(1024)S(1)} fusion(bf16[4096,64]{1,0:T(8,128)(2,1)S(1)} %get-tuple-element.134, f32[512]{0:T(512)S(1)} %bitcast.39, f32[512]{0:T(512)S(1)} %multiply_reduce_fusion.5, f32[4096]{0:T(1024)S(1)} %get-tuple-element.132, bf16[8,512,64]{2,1,0:T(8,128)(2,1)S(1)} %get-tuple-element.133, s32[]{:T(128)} %get-tuple-element.122), kind=kOutput, calls=%fused_computation.7.clone.1 | convolution fusion | flops 289402880 | bytes 1216516 | tf_op jit(solution)/shard_map/while/body/eval_jaxpr/dot_general | solution.py:142
  94.7 0.2 multiply_reduce_fusion.5
  94.9 6.0 %multiply_reduce_fusion.6 = f32[4096]{0:T(1024)S(1)} fusion(bf16[4096,64]{1,0:T(8,128)(2,1)S(1)} %get-tuple-element.134, f32[512]{0:T(512)S(1)} %bitcast.39, f32[512]{0:T(512)S(1)} %multiply_reduce_fusion.5, f32[4096]{0:T(1024)S(1)} %get-tuple-element.132, bf16[8,512,64]{2,1,0:T(8,128)(2,1)S(1)} %get-tuple-element.133, s32[]{:T(128)} %get-tuple-element.122), kind=kOutput, calls=%fused_computation.7.clone.1 | convolution fusion | flops 289402880 | bytes 1216516 | tf_op jit(solution)/shard_map/while/body/eval_jaxpr/dot_general | solution.py:142
  101.0 0.2 multiply_reduce_fusion.5
  101.1 6.0 %multiply_reduce_fusion.6 = f32[4096]{0:T(1024)S(1)} fusion(bf16[4096,64]{1,0:T(8,128)(2,1)S(1)} %get-tuple-element.134, f32[512]{0:T(512)S(1)} %bitcast.39, f32[512]{0:T(512)S(1)} %multiply_reduce_fusion.5, f32[4096]{0:T(1024)S(1)} %get-tuple-element.132, bf16[8,512,64]{2,1,0:T(8,128)(2,1)S(1)} %get-tuple-element.133, s32[]{:T(128)} %get-tuple-element.122), kind=kOutput, calls=%fused_computation.7.clone.1 | convolution fusion | flops 289402880 | bytes 1216516 | tf_op jit(solution)/shard_map/while/body/eval_jaxpr/dot_general | solution.py:142
  107.2 0.2 multiply_reduce_fusion.5
  107.4 6.0 %multiply_reduce_fusion.6 = f32[4096]{0:T(1024)S(1)} fusion(bf16[4096,64]{1,0:T(8,128)(2,1)S(1)} %get-tuple-element.134, f32[512]{0:T(512)S(1)} %bitcast.39, f32[512]{0:T(512)S(1)} %multiply_reduce_fusion.5, f32[4096]{0:T(1024)S(1)} %get-tuple-element.132, bf16[8,512,64]{2,1,0:T(8,128)(2,1)S(1)} %get-tuple-element.133, s32[]{:T(128)} %get-tuple-element.122), kind=kOutput, calls=%fused_computation.7.clone.1 | convolution fusion | flops 289402880 | bytes 1216516 | tf_op jit(solution)/shard_map/while/body/eval_jaxpr/dot_general | solution.py:142
  113.4 0.2 multiply_reduce_fusion.5
  113.6 6.0 %multiply_reduce_fusion.6 = f32[4096]{0:T(1024)S(1)} fusion(bf16[4096,64]{1,0:T(8,128)(2,1)S(1)} %get-tuple-element.134, f32[512]{0:T(512)S(1)} %bitcast.39, f32[512]{0:T(512)S(1)} %multiply_reduce_fusion.5, f32[4096]{0:T(1024)S(1)} %get-tuple-element.132, bf16[8,512,64]{2,1,0:T(8,128)(2,1)S(1)} %get-tuple-element.133, s32[]{:T(128)} %get-tuple-element.122), kind=kOutput, calls=%fused_computation.7.clone.1 | convolution fusion | flops 289402880 | bytes 1216516 | tf_op jit(solution)/shard_map/while/body/eval_jaxpr/dot_general | solution.py:142
  119.6 0.2 multiply_reduce_fusion.5
  119.8 6.0 %multiply_reduce_fusion.6 = f32[4096]{0:T(1024)S(1)} fusion(bf16[4096,64]{1,0:T(8,128)(2,1)S(1)} %get-tuple-element.134, f32[512]{0:T(512)S(1)} %bitcast.39, f32[512]{0:T(512)S(1)} %multiply_reduce_fusion.5, f32[4096]{0:T(1024)S(1)} %get-tuple-element.132, bf16[8,512,64]{2,1,0:T(8,128)(2,1)S(1)} %get-tuple-element.133, s32[]{:T(128)} %get-tuple-element.122), kind=kOutput, calls=%fused_computation.7.clone.1 | convolution fusion | flops 289402880 | bytes 1216516 | tf_op jit(solution)/shard_map/while/body/eval_jaxpr/dot_general | solution.py:142
  125.8 0.2 multiply_reduce_fusion.5
  126.0 6.0 %multiply_reduce_fusion.6 = f32[4096]{0:T(1024)S(1)} fusion(bf16[4096,64]{1,0:T(8,128)(2,1)S(1)} %get-tuple-element.134, f32[512]{0:T(512)S(1)} %bitcast.39, f32[512]{0:T(512)S(1)} %multiply_reduce_fusion.5, f32[4096]{0:T(1024)S(1)} %get-tuple-element.132, bf16[8,512,64]{2,1,0:T(8,128)(2,1)S(1)} %get-tuple-element.133, s32[]{:T(128)} %get-tuple-element.122), kind=kOutput, calls=%fused_computation.7.clone.1 | convolution fusion | flops 289402880 | bytes 1216516 | tf_op jit(solution)/shard_map/while/body/eval_jaxpr/dot_general | solution.py:142
  132.1 0.2 multiply_reduce_fusion.5
  132.2 6.0 %multiply_reduce_fusion.6 = f32[4096]{0:T(1024)S(1)} fusion(bf16[4096,64]{1,0:T(8,128)(2,1)S(1)} %get-tuple-element.134, f32[512]{0:T(512)S(1)} %bitcast.39, f32[512]{0:T(512)S(1)} %multiply_reduce_fusion.5, f32[4096]{0:T(1024)S(1)} %get-tuple-element.132, bf16[8,512,64]{2,1,0:T(8,128)(2,1)S(1)} %get-tuple-element.133, s32[]{:T(128)} %get-tuple-element.122), kind=kOutput, calls=%fused_computation.7.clone.1 | convolution fusion | flops 289402880 | bytes 1216516 | tf_op jit(solution)/shard_map/while/body/eval_jaxpr/dot_general | solution.py:142
  138.3 0.0 copy-start.6
  138.3 0.0 copy-start.4
  138.3 0.0 copy-start.5
  138.3 0.7 reshape.30.part
  139.0 71.1 %shard_map.78 = f32[64,1,64]{2,1,0:T(1,128)} custom-call(f32[64,1,64]{2,1,0:T(1,128)} %reshape.30.part), custom_call_target="tpu_custom_call" | custom-call | tf_op jit(solution)/shard_map/pallas_call | solution.py:130
  210.1 0.8 reduce_sum.40
  210.9 0.0 copy-done.1
  210.9 0.8 gather_fusion.1
  211.7 0.0 copy-done
  211.7 0.8 gather_fusion.2
  213.2 0.0 copy-done.6
  213.2 0.2 fusion.6
  213.4 0.0 copy-done.4
  213.4 0.0 copy-done.5
  213.4 0.6 fusion.20
  (19 shorter events, 0.1 us)
Async XLA Ops:
  0.6 211.1 %copy-start = (f32[512]{0:T(512)S(1)}, f32[512]{0:T(512)}, u32[]{:S(2)}) copy-start(f32[512]{0:T(512)} %param.13) | copy-start | bytes 6148
  2.3 3.3 %copy-start.2 = (bf16[512,64]{1,0:T(8,128)(2,1)}, bf16[512,64]{1,0:T(8,128)(2,1)S(1)}, u32[]{:S(2)}) copy-start(bf16[512,64]{1,0:T(8,128)(2,1)S(1)} %copy.10.pts) | copy-start | bytes 196612
  87.8 0.7 copy-start.3
  88.5 122.4 %copy-start.1 = (f32[512]{0:T(512)S(1)}, f32[512]{0:T(512)}, u32[]{:S(2)}) copy-start(f32[512]{0:T(512)} %multiply_add_fusion) | copy-start | bytes 6148
  138.3 74.9 %copy-start.6 = (s32[64]{0:T(128)S(1)}, s32[64]{0:T(128)}, u32[]{:S(2)}) copy-start(s32[64]{0:T(128)} %param.14) | copy-start | bytes 772
  138.3 75.1 %copy-start.4 = (f32[512]{0:T(512)S(1)}, f32[512]{0:T(512)}, u32[]{:S(2)}) copy-start(f32[512]{0:T(512)} %param.11) | copy-start | bytes 6148
  138.3 75.1 %copy-start.5 = (f32[512]{0:T(512)S(1)}, f32[512]{0:T(512)}, u32[]{:S(2)}) copy-start(f32[512]{0:T(512)} %param.12) | copy-start | bytes 6148

commit v2 on v1

--- a/solution.py
+++ b/solution.py
@@ -17,23 +17,32 @@
 ANY = pl.BlockSpec(memory_space=pl.ANY)
 
 
-def gather_kernel(n_blk, n_str, picked, pts, prev, rows_out, pts_out, prev_out,
-                  row_send, row_recv, pt_send, pt_recv, pv_send, pv_recv, local_sem):
+def gather_kernel(n_blk, n_in, n_out, picked, pts, prev, rows_out, pts_out, prev_out,
+                  in_send, in_recv, out_send, out_recv, pt_send, pt_recv, pv_send, pv_recv,
+                  local_sem):
     b = lax.axis_index("blk")
     s = lax.axis_index("stripe")
+    u = s // n_in
+    v = lax.rem(s, n_in)
     own = [
-        pltpu.make_async_copy(picked, rows_out.at[s], local_sem.at[0]),
+        pltpu.make_async_copy(picked, rows_out.at[u, v], local_sem.at[0]),
         pltpu.make_async_copy(pts, pts_out.at[b], local_sem.at[1]),
         pltpu.make_async_copy(prev, prev_out.at[b], local_sem.at[2]),
     ]
     for c in own:
         c.start()
 
-    def row_copy(i, src):
-        peer = lax.rem(s + 1 + i, n_str)
-        return pltpu.make_async_remote_copy(
-            src_ref=picked, dst_ref=rows_out.at[src], send_sem=row_send.at[i],
-            recv_sem=row_recv.at[src], device_id=(b, peer), device_id_type=MESH_ID)
+    def inner_copy(i, src):
+        peer = lax.rem(v + 1 + i, n_in)
+        return pltpu.make_async_remote_copy(
+            src_ref=picked, dst_ref=rows_out.at[u, src], send_sem=in_send.at[i],
+            recv_sem=in_recv.at[src], device_id=(b, u * n_in + peer), device_id_type=MESH_ID)
+
+    def outer_copy(i, src):
+        peer = lax.rem(u + 1 + i, n_out)
+        return pltpu.make_async_remote_copy(
+            src_ref=rows_out.at[u], dst_ref=rows_out.at[src], send_sem=out_send.at[i],
+            recv_sem=out_recv.at[src], device_id=(b, peer * n_in + v), device_id_type=MESH_ID)
 
     def blk_copies(i, src):
         peer = lax.rem(b + 1 + i, n_blk)
@@ -46,23 +55,31 @@
                 recv_sem=pv_recv.at[src], device_id=(peer, s), device_id_type=MESH_ID),
         )
 
+    def start_inner(i, carry):
+        inner_copy(i, v).start()
+        return carry
+
     def start_blk(i, carry):
         for c in blk_copies(i, b):
             c.start()
         return carry
 
-    def start_row(i, carry):
-        row_copy(i, s).start()
-        return carry
-
+    lax.fori_loop(0, n_in - 1, start_inner, 0)
     lax.fori_loop(0, n_blk - 1, start_blk, 0)
-    lax.fori_loop(0, n_str - 1, start_row, 0)
-
-    def wait_row(i, carry):
-        row_copy(i, s).wait_send()
-        src = lax.rem(s + 2 * n_str - 1 - i, n_str)
-        row_copy(i, src).wait_recv()
-        return carry
+
+    def wait_inner(i, carry):
+        inner_copy(i, v).wait_send()
+        inner_copy(i, lax.rem(v + 2 * n_in - 1 - i, n_in)).wait_recv()
+        return carry
+
+    lax.fori_loop(0, n_in - 1, wait_inner, 0)
+    own[0].wait()
+
+    def start_outer(i, carry):
+        outer_copy(i, u).start()
+        return carry
+
+    lax.fori_loop(0, n_out - 1, start_outer, 0)
 
     def wait_blk(i, carry):
         for c in blk_copies(i, b):
@@ -72,67 +89,105 @@
             c.wait_recv()
         return carry
 
+    def wait_outer(i, carry):
+        outer_copy(i, u).wait_send()
+        outer_copy(i, lax.rem(u + 2 * n_out - 1 - i, n_out)).wait_recv()
+        return carry
+
     lax.fori_loop(0, n_blk - 1, wait_blk, 0)
-    lax.fori_loop(0, n_str - 1, wait_row, 0)
-    for c in own:
-        c.wait()
-
-
-def gather_all(picked, pts, prev, n_blk, n_str):
+    lax.fori_loop(0, n_out - 1, wait_outer, 0)
+    own[1].wait()
+    own[2].wait()
+
+
+def gather_all(picked, pts, prev, n_blk, n_in, n_out):
     dma = pltpu.SemaphoreType.DMA
     return pl.pallas_call(
-        functools.partial(gather_kernel, n_blk, n_str),
+        functools.partial(gather_kernel, n_blk, n_in, n_out),
         out_shape=(
-            jax.ShapeDtypeStruct((n_str,) + picked.shape, picked.dtype),
+            jax.ShapeDtypeStruct((n_out, n_in) + picked.shape, picked.dtype),
             jax.ShapeDtypeStruct((n_blk,) + pts.shape, pts.dtype),
             jax.ShapeDtypeStruct((n_blk,) + prev.shape, prev.dtype),
         ),
         in_specs=[ANY, ANY, ANY],
         out_specs=(ANY, ANY, ANY),
         scratch_shapes=[
-            dma((n_str,)), dma((n_str,)), dma((n_blk,)), dma((n_blk,)),
-            dma((n_blk,)), dma((n_blk,)), dma((3,)),
+            dma((n_in,)), dma((n_in,)), dma((n_out,)), dma((n_out,)),
+            dma((n_blk,)), dma((n_blk,)), dma((n_blk,)), dma((n_blk,)), dma((3,)),
         ],
         compiler_params=pltpu.CompilerParams(has_side_effects=True),
     )(picked, pts, prev)
 
 
-def scatter_kernel(n_str, part, recv_out, send_sem, recv_sem, local_sem):
+def scatter_kernel(n_in, n_out, part, total_out, stage1, mid, stage2,
+                   out_send, out_recv, in_send, in_recv, local_sem):
     b = lax.axis_index("blk")
     s = lax.axis_index("stripe")
-    own = pltpu.make_async_copy(part.at[s], recv_out.at[s], local_sem.at[0])
-    own.start()
-
-    def copy(i, src):
-        peer = lax.rem(s + 1 + i, n_str)
-        return pltpu.make_async_remote_copy(
-            src_ref=part.at[peer], dst_ref=recv_out.at[src], send_sem=send_sem.at[i],
-            recv_sem=recv_sem.at[src], device_id=(b, peer), device_id_type=MESH_ID)
-
-    def start(i, carry):
-        copy(i, s).start()
-        return carry
-
-    lax.fori_loop(0, n_str - 1, start, 0)
-
-    def wait(i, carry):
-        copy(i, s).wait_send()
-        src = lax.rem(s + 2 * n_str - 1 - i, n_str)
-        copy(i, src).wait_recv()
-        return carry
-
-    lax.fori_loop(0, n_str - 1, wait, 0)
-    own.wait()
-
-
-def scatter_all(part, n_str):
+    u = s // n_in
+    v = lax.rem(s, n_in)
+    own1 = pltpu.make_async_copy(part.at[u], stage1.at[u], local_sem.at[0])
+    own1.start()
+
+    def outer_copy(i, src):
+        peer = lax.rem(u + 1 + i, n_out)
+        return pltpu.make_async_remote_copy(
+            src_ref=part.at[peer], dst_ref=stage1.at[src], send_sem=out_send.at[i],
+            recv_sem=out_recv.at[src], device_id=(b, peer * n_in + v), device_id_type=MESH_ID)
+
+    def inner_copy(i, src):
+        peer = lax.rem(v + 1 + i, n_in)
+        return pltpu.make_async_remote_copy(
+            src_ref=mid.at[peer], dst_ref=stage2.at[src], send_sem=in_send.at[i],
+            recv_sem=in_recv.at[src], device_id=(b, u * n_in + peer), device_id_type=MESH_ID)
+
+    def start_outer(i, carry):
+        outer_copy(i, u).start()
+        return carry
+
+    lax.fori_loop(0, n_out - 1, start_outer, 0)
+
+    def wait_outer(i, carry):
+        outer_copy(i, u).wait_send()
+        outer_copy(i, lax.rem(u + 2 * n_out - 1 - i, n_out)).wait_recv()
+        return carry
+
+    lax.fori_loop(0, n_out - 1, wait_outer, 0)
+    own1.wait()
+    mid[...] = jnp.sum(stage1[...], axis=0)[:, None, :]
+    own2 = pltpu.make_async_copy(mid.at[v], stage2.at[v], local_sem.at[1])
+    own2.start()
+
+    def start_inner(i, carry):
+        inner_copy(i, v).start()
+        return carry
+
+    lax.fori_loop(0, n_in - 1, start_inner, 0)
+
+    def wait_inner(i, carry):
+        inner_copy(i, v).wait_send()
+        inner_copy(i, lax.rem(v + 2 * n_in - 1 - i, n_in)).wait_recv()
+        return carry
+
+    lax.fori_loop(0, n_in - 1, wait_inner, 0)
+    own2.wait()
+    total_out[...] = jnp.sum(stage2[...], axis=0)
+
+
+def scatter_all(part, n_in, n_out):
     dma = pltpu.SemaphoreType.DMA
+    vmem = pl.BlockSpec(memory_space=pltpu.VMEM)
+    width = part.shape[-1]
     return pl.pallas_call(
-        functools.partial(scatter_kernel, n_str),
-        out_shape=jax.ShapeDtypeStruct(part.shape, part.dtype),
-        in_specs=[ANY],
-        out_specs=ANY,
-        scratch_shapes=[dma((n_str,)), dma((n_str,)), dma((1,))],
+        functools.partial(scatter_kernel, n_in, n_out),
+        out_shape=jax.ShapeDtypeStruct((1, width), part.dtype),
+        in_specs=[vmem],
+        out_specs=vmem,
+        scratch_shapes=[
+            pltpu.VMEM((n_out, n_in, width), jnp.float32),
+            pltpu.VMEM((n_in, 1, width), jnp.float32),
+            pltpu.VMEM((n_in, 1, width), jnp.float32),
+            dma((n_out,)), dma((n_out,)), dma((n_in,)), dma((n_in,)), dma((2,)),
+        ],
         compiler_params=pltpu.CompilerParams(has_side_effects=True),
     )(part)
 
@@ -174,13 +229,14 @@
     count_here = counts.reshape((1,))
     in_count = slot_ids < count_here[0]
     picked = jnp.take(points, batch_rows, axis=0)
-    rows_all, pts_all, prev_all = gather_all(picked, points, preview.reshape(1, -1), n_blk, n_str)
+    n_in = math.gcd(n_str, 8)
+    n_out = n_str // n_in
+    rows_all, pts_all, prev_all = gather_all(picked, points, preview.reshape(1, -1), n_blk, n_in, n_out)
     group_rows = rows_all.reshape(-1, points.shape[1])
     piece_points = pts_all.reshape(-1, points.shape[1])
     every_coef = prev_all.reshape(-1)
     partial_value = column_sums(group_rows, piece_points, every_coef)
-    received = scatter_all(partial_value.reshape(n_str, 1, slot_total), n_str)
-    kernel_rows = jnp.sum(received.reshape(n_str, slot_total), axis=0)
+    kernel_rows = scatter_all(partial_value.reshape(n_out, n_in, slot_total), n_in, n_out).reshape(-1)
     residual = jnp.where(
         in_count,
         kernel_rows + NOISE_VAR * jnp.take(preview, batch_rows) - jnp.take(targets, batch_rows),

time: 214 us -> 174 us (0.81)
  Pallas kernels: 153 us -> 114 us
    pallas_call x2, Pallas kernels: 153 us -> 114 us  [the longest x1 57.1 us: gather_all(): pl.pallas_call(functools.partial(gather_kernel, n_blk, n_in, n_out), out_...]
where the time goes in v2:
time: 174 us
  Pallas kernels  114 us (66%)
  matrix products  48 us (28%)
  other arithmetic  5.76 us (3%)
  local copies, waits for them, and re-layouts  4.08 us (2%)
    pallas_call x1, Pallas kernels, gather_all(): pl.pallas_call(functools.partial(gather_kernel, n_blk, n_in, n_out), out_...  57.1 us
    pallas_call x1, Pallas kernels, scatter_all(): pl.pallas_call(functools.partial(scatter_kernel, n_in, n_out), out_shape=...  56.8 us
    dot_general x8, matrix products, matern_sums(): lax.dot_general(row_feats, col_points, (((1,), (1,)), ((), ())), preferre...  47.8 us

profile of v2, /device:TPU:1, one launch (start us, length us, event | category | flops | bytes accessed | tf_op | source)
XLA Modules:
  0.0 173.5 jit_solution(8897835028380705550)
XLA Ops:
  0.6 0.0 copy-start
  0.6 0.7 compare_select_fusion
  1.3 1.0 copy.10.pts
  2.3 0.0 copy-start.2
  2.3 0.6 gather_fusion
  2.9 0.7 compare_and_fusion
  3.6 0.7 broadcast_select_fusion.picked
  4.3 1.3 multiply_add_fusion
  5.6 0.0 copy-done.2
  5.6 57.1 %shard_map.77 = (bf16[8,8,64,64]{3,2,1,0:T(8,128)(2,1)S(1)}, bf16[8,512,64]{2,1,0:T(8,128)(2,1)S(1)}, f32[8,1,512]{2,1,0:T(1,128)}) custom-call(bf16[64,64]{1,0:T(8,128)(2,1)} %broadcast_select_fusion.picked, bf16[512,64]{1,0:T(8,128)(2,1)} %copy-done.2, f32[1,512]{1,0:T(1,128)} %bitcast.44), custom_call_target="tpu_custom_call" | custom-call | tf_op jit(solution)/shard_map/pallas_call | solution.py:105
  62.7 0.0 copy-start.3
  62.7 0.6 multiply_reduce_fusion.2
  63.3 0.1 reduce_sum.30
  63.4 0.0 copy-done.3
  63.4 0.0 copy-start.1
  63.4 49.5 %while.11 = (s32[]{:T(128)}, f32[4096]{0:T(1024)S(1)}, f32[4096]{0:T(1024)S(1)}, bf16[8,512,64]{2,1,0:T(8,128)(2,1)S(1)}, bf16[4096,64]{1,0:T(8,128)(2,1)S(1)}, /*index=5*/f32[8,512]{1,0:T(8,128)S(1)}, s32[]{:T(128)}, s32[]{:T(128)}) while((s32[]{:T(128)}, f32[4096]{0:T(1024)S(1)}, f32[4096]{0:T(1024)S(1)}, ...), condition=%wide.region_4.5_spmd.clone, body=%wide.region_1.0_spmd.clone.sunk | while | flops 289508864 | bytes 1337451 | solution.py:220
  63.4 0.2 multiply_reduce_fusion.5
  63.6 6.0 %multiply_reduce_fusion.6 = f32[4096]{0:T(1024)S(1)} fusion(bf16[4096,64]{1,0:T(8,128)(2,1)S(1)} %get-tuple-element.134, f32[512]{0:T(512)S(1)} %bitcast.46, f32[512]{0:T(512)S(1)} %multiply_reduce_fusion.5, f32[4096]{0:T(1024)S(1)} %get-tuple-element.132, bf16[8,512,64]{2,1,0:T(8,128)(2,1)S(1)} %get-tuple-element.133, s32[]{:T(128)} %get-tuple-element.122), kind=kOutput, calls=%fused_computation.7.clone.1 | convolution fusion | flops 289402880 | bytes 1216516 | tf_op jit(solution)/shard_map/while/body/eval_jaxpr/dot_general | solution.py:197
  69.6 0.2 multiply_reduce_fusion.5
  69.8 6.0 %multiply_reduce_fusion.6 = f32[4096]{0:T(1024)S(1)} fusion(bf16[4096,64]{1,0:T(8,128)(2,1)S(1)} %get-tuple-element.134, f32[512]{0:T(512)S(1)} %bitcast.46, f32[512]{0:T(512)S(1)} %multiply_reduce_fusion.5, f32[4096]{0:T(1024)S(1)} %get-tuple-element.132, bf16[8,512,64]{2,1,0:T(8,128)(2,1)S(1)} %get-tuple-element.133, s32[]{:T(128)} %get-tuple-element.122), kind=kOutput, calls=%fused_computation.7.clone.1 | convolution fusion | flops 289402880 | bytes 1216516 | tf_op jit(solution)/shard_map/while/body/eval_jaxpr/dot_general | solution.py:197
  75.8 0.2 multiply_reduce_fusion.5
  76.0 6.0 %multiply_reduce_fusion.6 = f32[4096]{0:T(1024)S(1)} fusion(bf16[4096,64]{1,0:T(8,128)(2,1)S(1)} %get-tuple-element.134, f32[512]{0:T(512)S(1)} %bitcast.46, f32[512]{0:T(512)S(1)} %multiply_reduce_fusion.5, f32[4096]{0:T(1024)S(1)} %get-tuple-element.132, bf16[8,512,64]{2,1,0:T(8,128)(2,1)S(1)} %get-tuple-element.133, s32[]{:T(128)} %get-tuple-element.122), kind=kOutput, calls=%fused_computation.7.clone.1 | convolution fusion | flops 289402880 | bytes 1216516 | tf_op jit(solution)/shard_map/while/body/eval_jaxpr/dot_general | solution.py:197
  82.0 0.2 multiply_reduce_fusion.5
  82.2 6.0 %multiply_reduce_fusion.6 = f32[4096]{0:T(1024)S(1)} fusion(bf16[4096,64]{1,0:T(8,128)(2,1)S(1)} %get-tuple-element.134, f32[512]{0:T(512)S(1)} %bitcast.46, f32[512]{0:T(512)S(1)} %multiply_reduce_fusion.5, f32[4096]{0:T(1024)S(1)} %get-tuple-element.132, bf16[8,512,64]{2,1,0:T(8,128)(2,1)S(1)} %get-tuple-element.133, s32[]{:T(128)} %get-tuple-element.122), kind=kOutput, calls=%fused_computation.7.clone.1 | convolution fusion | flops 289402880 | bytes 1216516 | tf_op jit(solution)/shard_map/while/body/eval_jaxpr/dot_general | solution.py:197
  88.2 0.2 multiply_reduce_fusion.5
  88.4 6.0 %multiply_reduce_fusion.6 = f32[4096]{0:T(1024)S(1)} fusion(bf16[4096,64]{1,0:T(8,128)(2,1)S(1)} %get-tuple-element.134, f32[512]{0:T(512)S(1)} %bitcast.46, f32[512]{0:T(512)S(1)} %multiply_reduce_fusion.5, f32[4096]{0:T(1024)S(1)} %get-tuple-element.132, bf16[8,512,64]{2,1,0:T(8,128)(2,1)S(1)} %get-tuple-element.133, s32[]{:T(128)} %get-tuple-element.122), kind=kOutput, calls=%fused_computation.7.clone.1 | convolution fusion | flops 289402880 | bytes 1216516 | tf_op jit(solution)/shard_map/while/body/eval_jaxpr/dot_general | solution.py:197
  94.4 0.2 multiply_reduce_fusion.5
  94.5 6.0 %multiply_reduce_fusion.6 = f32[4096]{0:T(1024)S(1)} fusion(bf16[4096,64]{1,0:T(8,128)(2,1)S(1)} %get-tuple-element.134, f32[512]{0:T(512)S(1)} %bitcast.46, f32[512]{0:T(512)S(1)} %multiply_reduce_fusion.5, f32[4096]{0:T(1024)S(1)} %get-tuple-element.132, bf16[8,512,64]{2,1,0:T(8,128)(2,1)S(1)} %get-tuple-element.133, s32[]{:T(128)} %get-tuple-element.122), kind=kOutput, calls=%fused_computation.7.clone.1 | convolution fusion | flops 289402880 | bytes 1216516 | tf_op jit(solution)/shard_map/while/body/eval_jaxpr/dot_general | solution.py:197
  100.5 0.2 multiply_reduce_fusion.5
  100.7 6.0 %multiply_reduce_fusion.6 = f32[4096]{0:T(1024)S(1)} fusion(bf16[4096,64]{1,0:T(8,128)(2,1)S(1)} %get-tuple-element.134, f32[512]{0:T(512)S(1)} %bitcast.46, f32[512]{0:T(512)S(1)} %multiply_reduce_fusion.5, f32[4096]{0:T(1024)S(1)} %get-tuple-element.132, bf16[8,512,64]{2,1,0:T(8,128)(2,1)S(1)} %get-tuple-element.133, s32[]{:T(128)} %get-tuple-element.122), kind=kOutput, calls=%fused_computation.7.clone.1 | convolution fusion | flops 289402880 | bytes 1216516 | tf_op jit(solution)/shard_map/while/body/eval_jaxpr/dot_general | solution.py:197
  106.7 0.2 multiply_reduce_fusion.5
  106.9 6.0 %multiply_reduce_fusion.6 = f32[4096]{0:T(1024)S(1)} fusion(bf16[4096,64]{1,0:T(8,128)(2,1)S(1)} %get-tuple-element.134, f32[512]{0:T(512)S(1)} %bitcast.46, f32[512]{0:T(512)S(1)} %multiply_reduce_fusion.5, f32[4096]{0:T(1024)S(1)} %get-tuple-element.132, bf16[8,512,64]{2,1,0:T(8,128)(2,1)S(1)} %get-tuple-element.133, s32[]{:T(128)} %get-tuple-element.122), kind=kOutput, calls=%fused_computation.7.clone.1 | convolution fusion | flops 289402880 | bytes 1216516 | tf_op jit(solution)/shard_map/while/body/eval_jaxpr/dot_general | solution.py:197
  112.9 0.0 copy-start.7
  112.9 0.0 copy-start.4
  112.9 0.0 copy-start.5
  112.9 0.7 reshape.32.part
  113.6 56.8 %shard_map.78 = f32[1,64]{1,0:T(1,128)} custom-call(f32[8,8,64]{2,1,0:T(8,128)} %reshape.32.part), custom_call_target="tpu_custom_call" | custom-call | tf_op jit(solution)/shard_map/pallas_call | solution.py:180
  170.4 0.0 copy-done.1
  170.4 0.0 copy-start.6
  170.5 0.8 gather_fusion.1
  171.3 0.0 copy-done
  171.3 0.8 gather_fusion.2
  172.7 0.0 copy-done.7
  172.7 0.0 copy-done.6
  172.7 0.2 fusion.6
  173.0 0.0 copy-done.4
  173.0 0.0 copy-done.5
  173.0 0.6 fusion.21
  (19 shorter events, 0.1 us)
Async XLA Ops:
  0.6 170.6 %copy-start = (f32[512]{0:T(512)S(1)}, f32[512]{0:T(512)}, u32[]{:S(2)}) copy-start(f32[512]{0:T(512)} %param.13) | copy-start | bytes 6148
  2.3 3.3 %copy-start.2 = (bf16[512,64]{1,0:T(8,128)(2,1)}, bf16[512,64]{1,0:T(8,128)(2,1)S(1)}, u32[]{:S(2)}) copy-start(bf16[512,64]{1,0:T(8,128)(2,1)S(1)} %copy.10.pts) | copy-start | bytes 196612
  62.7 0.7 copy-start.3
  63.4 107.0 %copy-start.1 = (f32[512]{0:T(512)S(1)}, f32[512]{0:T(512)}, u32[]{:S(2)}) copy-start(f32[512]{0:T(512)} %multiply_add_fusion) | copy-start | bytes 6148
  112.9 59.8 %copy-start.7 = (s32[64]{0:T(128)S(1)}, s32[64]{0:T(128)}, u32[]{:S(2)}) copy-start(s32[64]{0:T(128)} %param.14) | copy-start | bytes 772
  112.9 60.0 %copy-start.4 = (f32[512]{0:T(512)S(1)}, f32[512]{0:T(512)}, u32[]{:S(2)}) copy-start(f32[512]{0:T(512)} %param.11) | copy-start | bytes 6148
  112.9 60.0 %copy-start.5 = (f32[512]{0:T(512)S(1)}, f32[512]{0:T(512)}, u32[]{:S(2)}) copy-start(f32[512]{0:T(512)} %param.12) | copy-start | bytes 6148
  170.4 2.3 %copy-start.6 = (f32[1,64]{1,0:T(1,128)S(1)}, f32[1,64]{1,0:T(1,128)}, u32[]{:S(2)}) copy-start(f32[1,64]{1,0:T(1,128)} %shard_map.78) | copy-start | bytes 772

commit v3 on v2

--- a/solution.py
+++ b/solution.py
@@ -24,6 +24,27 @@
     s = lax.axis_index("stripe")
     u = s // n_in
     v = lax.rem(s, n_in)
+    barrier = pltpu.get_barrier_semaphore()
+
+    def greet(i, carry):
+        pl.semaphore_signal(barrier, 1, device_id=(b, u * n_in + lax.rem(v + 1 + i, n_in)),
+                            device_id_type=MESH_ID)
+        return carry
+
+    def greet_out(i, carry):
+        pl.semaphore_signal(barrier, 1, device_id=(b, lax.rem(u + 1 + i, n_out) * n_in + v),
+                            device_id_type=MESH_ID)
+        return carry
+
+    def greet_blk(i, carry):
+        pl.semaphore_signal(barrier, 1, device_id=(lax.rem(b + 1 + i, n_blk), s),
+                            device_id_type=MESH_ID)
+        return carry
+
+    lax.fori_loop(0, n_in - 1, greet, 0)
+    lax.fori_loop(0, n_out - 1, greet_out, 0)
+    lax.fori_loop(0, n_blk - 1, greet_blk, 0)
+    pl.semaphore_wait(barrier, (n_in - 1) + (n_out - 1) + (n_blk - 1))
     own = [
         pltpu.make_async_copy(picked, rows_out.at[u, v], local_sem.at[0]),
         pltpu.make_async_copy(pts, pts_out.at[b], local_sem.at[1]),
@@ -115,7 +136,7 @@
             dma((n_in,)), dma((n_in,)), dma((n_out,)), dma((n_out,)),
             dma((n_blk,)), dma((n_blk,)), dma((n_blk,)), dma((n_blk,)), dma((3,)),
         ],
-        compiler_params=pltpu.CompilerParams(has_side_effects=True),
+        compiler_params=pltpu.CompilerParams(has_side_effects=True, collective_id=0),
     )(picked, pts, prev)
 
 
@@ -125,6 +146,21 @@
     s = lax.axis_index("stripe")
     u = s // n_in
     v = lax.rem(s, n_in)
+    barrier = pltpu.get_barrier_semaphore()
+
+    def greet(i, carry):
+        pl.semaphore_signal(barrier, 1, device_id=(b, u * n_in + lax.rem(v + 1 + i, n_in)),
+                            device_id_type=MESH_ID)
+        return carry
+
+    def greet_out(i, carry):
+        pl.semaphore_signal(barrier, 1, device_id=(b, lax.rem(u + 1 + i, n_out) * n_in + v),
+                            device_id_type=MESH_ID)
+        return carry
+
+    lax.fori_loop(0, n_in - 1, greet, 0)
+    lax.fori_loop(0, n_out - 1, greet_out, 0)
+    pl.semaphore_wait(barrier, (n_in - 1) + (n_out - 1))
     own1 = pltpu.make_async_copy(part.at[u], stage1.at[u], local_sem.at[0])
     own1.start()
 
@@ -188,7 +224,7 @@
             pltpu.VMEM((n_in, 1, width), jnp.float32),
             dma((n_out,)), dma((n_out,)), dma((n_in,)), dma((n_in,)), dma((2,)),
         ],
-        compiler_params=pltpu.CompilerParams(has_side_effects=True),
+        compiler_params=pltpu.CompilerParams(has_side_effects=True, collective_id=1),
     )(part)
 
 

time: 174 us -> 149 us (0.86)
  the two profiles are of different devices: /device:TPU:1 before, /device:TPU:96 now
where the time goes in v3:
time: 149 us
  Pallas kernels  89.2 us (60%)
  matrix products  48 us (32%)
  other arithmetic  5.76 us (4%)
  local copies, waits for them, and re-layouts  4.08 us (3%)
    pallas_call x1, Pallas kernels, gather_all(): pl.pallas_call(functools.partial(gather_kernel, n_blk, n_in, n_out), out_...  67.3 us
    dot_general x8, matrix products, matern_sums(): lax.dot_general(row_feats, col_points, (((1,), (1,)), ((), ())), preferre...  47.7 us
    pallas_call x1, Pallas kernels, scatter_all(): pl.pallas_call(functools.partial(scatter_kernel, n_in, n_out), out_shape=...  21.8 us

profile of v3, /device:TPU:96, one launch (start us, length us, event | category | flops | bytes accessed | tf_op | source)
XLA Modules:
  0.0 148.7 jit_solution(13259688857406192857)
XLA Ops:
  0.6 0.0 copy-start
  0.6 0.7 compare_select_fusion
  1.3 1.0 copy.10.pts
  2.3 0.0 copy-start.2
  2.3 0.6 gather_fusion
  2.9 0.7 compare_and_fusion
  3.6 0.7 broadcast_select_fusion.picked
  4.3 1.3 multiply_add_fusion
  5.6 0.0 copy-done.2
  5.6 67.3 %shard_map.77 = (bf16[8,8,64,64]{3,2,1,0:T(8,128)(2,1)S(1)}, bf16[8,512,64]{2,1,0:T(8,128)(2,1)S(1)}, f32[8,1,512]{2,1,0:T(1,128)}) custom-call(bf16[64,64]{1,0:T(8,128)(2,1)} %broadcast_select_fusion.picked, bf16[512,64]{1,0:T(8,128)(2,1)} %copy-done.2, f32[1,512]{1,0:T(1,128)} %bitcast.44), custom_call_target="tpu_custom_call" | custom-call | tf_op jit(solution)/shard_map/pallas_call | solution.py:126
  72.9 0.0 copy-start.3
  72.9 0.6 multiply_reduce_fusion.2
  73.5 0.1 reduce_sum.30
  73.6 0.0 copy-done.3
  73.6 0.0 copy-start.1
  73.6 49.4 %while.11 = (s32[]{:T(128)}, f32[4096]{0:T(1024)S(1)}, f32[4096]{0:T(1024)S(1)}, bf16[8,512,64]{2,1,0:T(8,128)(2,1)S(1)}, bf16[4096,64]{1,0:T(8,128)(2,1)S(1)}, /*index=5*/f32[8,512]{1,0:T(8,128)S(1)}, s32[]{:T(128)}, s32[]{:T(128)}) while((s32[]{:T(128)}, f32[4096]{0:T(1024)S(1)}, f32[4096]{0:T(1024)S(1)}, ...), condition=%wide.region_4.5_spmd.clone, body=%wide.region_1.0_spmd.clone.sunk | while | flops 289508864 | bytes 1337451 | solution.py:256
  73.6 0.2 multiply_reduce_fusion.5
  73.8 6.0 %multiply_reduce_fusion.6 = f32[4096]{0:T(1024)S(1)} fusion(bf16[4096,64]{1,0:T(8,128)(2,1)S(1)} %get-tuple-element.134, f32[512]{0:T(512)S(1)} %bitcast.46, f32[512]{0:T(512)S(1)} %multiply_reduce_fusion.5, f32[4096]{0:T(1024)S(1)} %get-tuple-element.132, bf16[8,512,64]{2,1,0:T(8,128)(2,1)S(1)} %get-tuple-element.133, s32[]{:T(128)} %get-tuple-element.122), kind=kOutput, calls=%fused_computation.7.clone.1 | convolution fusion | flops 289402880 | bytes 1216516 | tf_op jit(solution)/shard_map/while/body/eval_jaxpr/dot_general | solution.py:233
  79.8 0.2 multiply_reduce_fusion.5
  80.0 6.0 %multiply_reduce_fusion.6 = f32[4096]{0:T(1024)S(1)} fusion(bf16[4096,64]{1,0:T(8,128)(2,1)S(1)} %get-tuple-element.134, f32[512]{0:T(512)S(1)} %bitcast.46, f32[512]{0:T(512)S(1)} %multiply_reduce_fusion.5, f32[4096]{0:T(1024)S(1)} %get-tuple-element.132, bf16[8,512,64]{2,1,0:T(8,128)(2,1)S(1)} %get-tuple-element.133, s32[]{:T(128)} %get-tuple-element.122), kind=kOutput, calls=%fused_computation.7.clone.1 | convolution fusion | flops 289402880 | bytes 1216516 | tf_op jit(solution)/shard_map/while/body/eval_jaxpr/dot_general | solution.py:233
  86.0 0.2 multiply_reduce_fusion.5
  86.1 6.0 %multiply_reduce_fusion.6 = f32[4096]{0:T(1024)S(1)} fusion(bf16[4096,64]{1,0:T(8,128)(2,1)S(1)} %get-tuple-element.134, f32[512]{0:T(512)S(1)} %bitcast.46, f32[512]{0:T(512)S(1)} %multiply_reduce_fusion.5, f32[4096]{0:T(1024)S(1)} %get-tuple-element.132, bf16[8,512,64]{2,1,0:T(8,128)(2,1)S(1)} %get-tuple-element.133, s32[]{:T(128)} %get-tuple-element.122), kind=kOutput, calls=%fused_computation.7.clone.1 | convolution fusion | flops 289402880 | bytes 1216516 | tf_op jit(solution)/shard_map/while/body/eval_jaxpr/dot_general | solution.py:233
  92.2 0.2 multiply_reduce_fusion.5
  92.3 6.0 %multiply_reduce_fusion.6 = f32[4096]{0:T(1024)S(1)} fusion(bf16[4096,64]{1,0:T(8,128)(2,1)S(1)} %get-tuple-element.134, f32[512]{0:T(512)S(1)} %bitcast.46, f32[512]{0:T(512)S(1)} %multiply_reduce_fusion.5, f32[4096]{0:T(1024)S(1)} %get-tuple-element.132, bf16[8,512,64]{2,1,0:T(8,128)(2,1)S(1)} %get-tuple-element.133, s32[]{:T(128)} %get-tuple-element.122), kind=kOutput, calls=%fused_computation.7.clone.1 | convolution fusion | flops 289402880 | bytes 1216516 | tf_op jit(solution)/shard_map/while/body/eval_jaxpr/dot_general | solution.py:233
  98.3 0.2 multiply_reduce_fusion.5
  98.5 6.0 %multiply_reduce_fusion.6 = f32[4096]{0:T(1024)S(1)} fusion(bf16[4096,64]{1,0:T(8,128)(2,1)S(1)} %get-tuple-element.134, f32[512]{0:T(512)S(1)} %bitcast.46, f32[512]{0:T(512)S(1)} %multiply_reduce_fusion.5, f32[4096]{0:T(1024)S(1)} %get-tuple-element.132, bf16[8,512,64]{2,1,0:T(8,128)(2,1)S(1)} %get-tuple-element.133, s32[]{:T(128)} %get-tuple-element.122), kind=kOutput, calls=%fused_computation.7.clone.1 | convolution fusion | flops 289402880 | bytes 1216516 | tf_op jit(solution)/shard_map/while/body/eval_jaxpr/dot_general | solution.py:233
  104.5 0.2 multiply_reduce_fusion.5
  104.7 6.0 %multiply_reduce_fusion.6 = f32[4096]{0:T(1024)S(1)} fusion(bf16[4096,64]{1,0:T(8,128)(2,1)S(1)} %get-tuple-element.134, f32[512]{0:T(512)S(1)} %bitcast.46, f32[512]{0:T(512)S(1)} %multiply_reduce_fusion.5, f32[4096]{0:T(1024)S(1)} %get-tuple-element.132, bf16[8,512,64]{2,1,0:T(8,128)(2,1)S(1)} %get-tuple-element.133, s32[]{:T(128)} %get-tuple-element.122), kind=kOutput, calls=%fused_computation.7.clone.1 | convolution fusion | flops 289402880 | bytes 1216516 | tf_op jit(solution)/shard_map/while/body/eval_jaxpr/dot_general | solution.py:233
  110.7 0.2 multiply_reduce_fusion.5
  110.9 6.0 %multiply_reduce_fusion.6 = f32[4096]{0:T(1024)S(1)} fusion(bf16[4096,64]{1,0:T(8,128)(2,1)S(1)} %get-tuple-element.134, f32[512]{0:T(512)S(1)} %bitcast.46, f32[512]{0:T(512)S(1)} %multiply_reduce_fusion.5, f32[4096]{0:T(1024)S(1)} %get-tuple-element.132, bf16[8,512,64]{2,1,0:T(8,128)(2,1)S(1)} %get-tuple-element.133, s32[]{:T(128)} %get-tuple-element.122), kind=kOutput, calls=%fused_computation.7.clone.1 | convolution fusion | flops 289402880 | bytes 1216516 | tf_op jit(solution)/shard_map/while/body/eval_jaxpr/dot_general | solution.py:233
  116.9 0.2 multiply_reduce_fusion.5
  117.1 6.0 %multiply_reduce_fusion.6 = f32[4096]{0:T(1024)S(1)} fusion(bf16[4096,64]{1,0:T(8,128)(2,1)S(1)} %get-tuple-element.134, f32[512]{0:T(512)S(1)} %bitcast.46, f32[512]{0:T(512)S(1)} %multiply_reduce_fusion.5, f32[4096]{0:T(1024)S(1)} %get-tuple-element.132, bf16[8,512,64]{2,1,0:T(8,128)(2,1)S(1)} %get-tuple-element.133, s32[]{:T(128)} %get-tuple-element.122), kind=kOutput, calls=%fused_computation.7.clone.1 | convolution fusion | flops 289402880 | bytes 1216516 | tf_op jit(solution)/shard_map/while/body/eval_jaxpr/dot_general | solution.py:233
  123.1 0.0 copy-start.7
  123.1 0.0 copy-start.4
  123.1 0.0 copy-start.5
  123.1 0.7 reshape.32.part
  123.8 21.8 %shard_map.78 = f32[1,64]{1,0:T(1,128)} custom-call(f32[8,8,64]{2,1,0:T(8,128)} %reshape.32.part), custom_call_target="tpu_custom_call" | custom-call | tf_op jit(solution)/shard_map/pallas_call | solution.py:216
  145.6 0.0 copy-done.1
  145.6 0.0 copy-start.6
  145.6 0.8 gather_fusion.1
  146.4 0.0 copy-done
  146.4 0.8 gather_fusion.2
  147.9 0.0 copy-done.7
  147.9 0.0 copy-done.6
  147.9 0.2 fusion.6
  148.1 0.0 copy-done.4
  148.1 0.0 copy-done.5
  148.1 0.6 fusion.21
  (19 shorter events, 0.1 us)
Async XLA Ops:
  0.6 145.8 %copy-start = (f32[512]{0:T(512)S(1)}, f32[512]{0:T(512)}, u32[]{:S(2)}) copy-start(f32[512]{0:T(512)} %param.13) | copy-start | bytes 6148
  2.3 3.3 %copy-start.2 = (bf16[512,64]{1,0:T(8,128)(2,1)}, bf16[512,64]{1,0:T(8,128)(2,1)S(1)}, u32[]{:S(2)}) copy-start(bf16[512,64]{1,0:T(8,128)(2,1)S(1)} %copy.10.pts) | copy-start | bytes 196612
  72.9 0.7 copy-start.3
  73.6 72.0 %copy-start.1 = (f32[512]{0:T(512)S(1)}, f32[512]{0:T(512)}, u32[]{:S(2)}) copy-start(f32[512]{0:T(512)} %multiply_add_fusion) | copy-start | bytes 6148
  123.1 24.8 %copy-start.7 = (s32[64]{0:T(128)S(1)}, s32[64]{0:T(128)}, u32[]{:S(2)}) copy-start(s32[64]{0:T(128)} %param.14) | copy-start | bytes 772
  123.1 25.1 %copy-start.4 = (f32[512]{0:T(512)S(1)}, f32[512]{0:T(512)}, u32[]{:S(2)}) copy-start(f32[512]{0:T(512)} %param.11) | copy-start | bytes 6148
  123.1 25.0 %copy-start.5 = (f32[512]{0:T(512)S(1)}, f32[512]{0:T(512)}, u32[]{:S(2)}) copy-start(f32[512]{0:T(512)} %param.12) | copy-start | bytes 6148
  145.6 2.3 %copy-start.6 = (f32[1,64]{1,0:T(1,128)S(1)}, f32[1,64]{1,0:T(1,128)}, u32[]{:S(2)}) copy-start(f32[1,64]{1,0:T(1,128)} %shard_map.78) | copy-start | bytes 772

commit v4 on v2

v4 whole, which is shorter than its diff:
```python
import functools
import math

import jax
import jax.numpy as jnp
from jax import lax
from jax.experimental import pallas as pl
from jax.experimental.pallas import tpu as pltpu
from jax.sharding import PartitionSpec as P

MOMENTUM = 0.9
STEP_SIZE = 1.0
NOISE_VAR = 8.0
KERNEL_RATE = 3.0**0.5 / 6.0

MESH_ID = pl.DeviceIdType.MESH
ANY = pl.BlockSpec(memory_space=pl.ANY)


def coords():
    b = lax.axis_index("blk")
    s = lax.axis_index("stripe")
    core = lax.rem(s, 2)
    z_hi = lax.rem(s // 2, 2)
    x = lax.rem(s // 4, 4)
    y = s // 16
    c = lax.rem(b, 2) * 4 + lax.rem(x, 2) * 2 + core
    q = y * 2 + x // 2
    w = (b // 2) * 2 + z_hi
    return c, q, w


def dev(c, q, w):
    b = (w // 2) * 2 + c // 4
    z_hi = lax.rem(w, 2)
    y = q // 2
    x = lax.rem(q, 2) * 2 + lax.rem(c // 2, 2)
    core = lax.rem(c, 2)
    return (b, ((y * 4 + x) * 2 + z_hi) * 2 + core)


def greet_all(barrier, peers_of, n, total):
    def greet(i, carry):
        pl.semaphore_signal(barrier, 1, device_id=peers_of(i), device_id_type=MESH_ID)
        return carry

    lax.fori_loop(0, n, greet, 0)
    return total + n


def gather_kernel(g, picked, pts, prev, rows_out, pts_out, prev_out,
                  in_send, in_recv, out_send, out_recv, pt_send, pt_recv, pv_send, pv_recv,
                  local_sem):
    c, q, w = coords()
    barrier = pltpu.get_barrier_semaphore()
    n = greet_all(barrier, lambda i: dev(c, q, lax.rem(w + 1 + i, g)), g - 1, 0)
    n = greet_all(barrier, lambda i: dev(c, lax.rem(q + 1 + i, g), w), g - 1, n)
    n = greet_all(barrier, lambda i: dev(lax.rem(c + 1 + i, g), q, w), g - 1, n)
    pl.semaphore_wait(barrier, n)
    own = [
        pltpu.make_async_copy(picked, rows_out.at[q, w], local_sem.at[0]),
        pltpu.make_async_copy(pts, pts_out.at[c], local_sem.at[1]),
        pltpu.make_async_copy(prev, prev_out.at[c], local_sem.at[2]),
    ]
    for cp in own:
        cp.start()

    def inner_copy(i, src):
        return pltpu.make_async_remote_copy(
            src_ref=picked, dst_ref=rows_out.at[q, src], send_sem=in_send.at[i],
            recv_sem=in_recv.at[src], device_id=dev(c, q, lax.rem(w + 1 + i, g)),
            device_id_type=MESH_ID)

    def outer_copy(i, src):
        return pltpu.make_async_remote_copy(
            src_ref=rows_out.at[q], dst_ref=rows_out.at[src], send_sem=out_send.at[i],
            recv_sem=out_recv.at[src], device_id=dev(c, lax.rem(q + 1 + i, g), w),
            device_id_type=MESH_ID)

    def group_copies(i, src):
        peer = dev(lax.rem(c + 1 + i, g), q, w)
        return (
            pltpu.make_async_remote_copy(
                src_ref=pts, dst_ref=pts_out.at[src], send_sem=pt_send.at[i],
                recv_sem=pt_recv.at[src], device_id=peer, device_id_type=MESH_ID),
            pltpu.make_async_remote_copy(
                src_ref=prev, dst_ref=prev_out.at[src], send_sem=pv_send.at[i],
                recv_sem=pv_recv.at[src], device_id=peer, device_id_type=MESH_ID),
        )

    def start_inner(i, carry):
        inner_copy(i, w).start()
        return carry

    def start_group(i, carry):
        for cp in group_copies(i, c):
            cp.start()
        return carry

    lax.fori_loop(0, g - 1, start_inner, 0)
    lax.fori_loop(0, g - 1, start_group, 0)

    def wait_inner(i, carry):
        inner_copy(i, w).wait_send()
        inner_copy(i, lax.rem(w + 2 * g - 1 - i, g)).wait_recv()
        return carry

    lax.fori_loop(0, g - 1, wait_inner, 0)
    own[0].wait()

    def start_outer(i, carry):
        outer_copy(i, q).start()
        return carry

    lax.fori_loop(0, g - 1, start_outer, 0)

    def wait_group(i, carry):
        for cp in group_copies(i, c):
            cp.wait_send()
        for cp in group_copies(i, lax.rem(c + 2 * g - 1 - i, g)):
            cp.wait_recv()
        return carry

    def wait_outer(i, carry):
        outer_copy(i, q).wait_send()
        outer_copy(i, lax.rem(q + 2 * g - 1 - i, g)).wait_recv()
        return carry

    lax.fori_loop(0, g - 1, wait_group, 0)
    lax.fori_loop(0, g - 1, wait_outer, 0)
    own[1].wait()
    own[2].wait()


def gather_all(picked, pts, prev, g):
    dma = pltpu.SemaphoreType.DMA
    return pl.pallas_call(
        functools.partial(gather_kernel, g),
        out_shape=(
            jax.ShapeDtypeStruct((g, g) + picked.shape, picked.dtype),
            jax.ShapeDtypeStruct((g,) + pts.shape, pts.dtype),
            jax.ShapeDtypeStruct((g,) + prev.shape, prev.dtype),
        ),
        in_specs=[ANY, ANY, ANY],
        out_specs=(ANY, ANY, ANY),
        scratch_shapes=[dma((g,)) for _ in range(8)] + [dma((3,))],
        compiler_params=pltpu.CompilerParams(has_side_effects=True, collective_id=0),
    )(picked, pts, prev)


def scatter_kernel(g, part, total_out, stage1, mid, stage2,
                   out_send, out_recv, in_send, in_recv, local_sem):
    c, q, w = coords()
    barrier = pltpu.get_barrier_semaphore()
    n = greet_all(barrier, lambda i: dev(c, q, lax.rem(w + 1 + i, g)), g - 1, 0)
    n = greet_all(barrier, lambda i: dev(c, lax.rem(q + 1 + i, g), w), g - 1, n)
    pl.semaphore_wait(barrier, n)
    own1 = pltpu.make_async_copy(part.at[q], stage1.at[q], local_sem.at[0])
    own1.start()

    def outer_copy(i, src):
        peer = lax.rem(q + 1 + i, g)
        return pltpu.make_async_remote_copy(
            src_ref=part.at[peer], dst_ref=stage1.at[src], send_sem=out_send.at[i],
            recv_sem=out_recv.at[src], device_id=dev(c, peer, w), device_id_type=MESH_ID)

    def inner_copy(i, src):
        peer = lax.rem(w + 1 + i, g)
        return pltpu.make_async_remote_copy(
            src_ref=mid.at[peer], dst_ref=stage2.at[src], send_sem=in_send.at[i],
            recv_sem=in_recv.at[src], device_id=dev(c, q, peer), device_id_type=MESH_ID)

    def start_outer(i, carry):
        outer_copy(i, q).start()
        return carry

    lax.fori_loop(0, g - 1, start_outer, 0)

    def wait_outer(i, carry):
        outer_copy(i, q).wait_send()
        outer_copy(i, lax.rem(q + 2 * g - 1 - i, g)).wait_recv()
        return carry

    lax.fori_loop(0, g - 1, wait_outer, 0)
    own1.wait()
    mid[...] = jnp.sum(stage1[...], axis=0)[:, None, :]
    own2 = pltpu.make_async_copy(mid.at[w], stage2.at[w], local_sem.at[1])
    own2.start()

    def start_inner(i, carry):
        inner_copy(i, w).start()
        return carry

    lax.fori_loop(0, g - 1, start_inner, 0)

    def wait_inner(i, carry):
        inner_copy(i, w).wait_send()
        inner_copy(i, lax.rem(w + 2 * g - 1 - i, g)).wait_recv()
        return carry

    lax.fori_loop(0, g - 1, wait_inner, 0)
    own2.wait()
    total_out[...] = jnp.sum(stage2[...], axis=0)


def scatter_all(part, g):
    dma = pltpu.SemaphoreType.DMA
    vmem = pl.BlockSpec(memory_space=pltpu.VMEM)
    width = part.shape[-1]
    return pl.pallas_call(
        functools.partial(scatter_kernel, g),
        out_shape=jax.ShapeDtypeStruct((1, width), part.dtype),
        in_specs=[vmem],
        out_specs=vmem,
        scratch_shapes=[
            pltpu.VMEM((g, g, width), jnp.float32),
            pltpu.VMEM((g, 1, width), jnp.float32),
            pltpu.VMEM((g, 1, width), jnp.float32),
            dma((g,)), dma((g,)), dma((g,)), dma((g,)), dma((2,)),
        ],
        compiler_params=pltpu.CompilerParams(has_side_effects=True, collective_id=1),
    )(part)


def matern_sums(row_feats, row_sq, col_points, col_coef):
    col_sq = jnp.sum(jnp.square(col_points.astype(jnp.float32)), axis=1)
    inner_prod = lax.dot_general(
        row_feats, col_points, (((1,), (1,)), ((), ())), preferred_element_type=jnp.float32
    )
    distance = jnp.sqrt(jnp.maximum(row_sq[:, None] + col_sq[None, :] - 2.0 * inner_prod, 0.0))
    scaled = KERNEL_RATE * distance
    kernel_tile = (1.0 + scaled) * jnp.exp(-scaled)
    return jnp.sum(kernel_tile * col_coef[None, :], axis=1)


def column_sums(row_feats, piece_points, every_coef):
    row_sq = jnp.sum(jnp.square(row_feats.astype(jnp.float32)), axis=1)
    zeros_init = jnp.zeros((row_feats.shape[0],), jnp.float32)
    piece_len = piece_points.shape[0]
    block_len = math.gcd(piece_len, 512)
    point_blocks = piece_points.reshape(-1, block_len, piece_points.shape[1])
    coef_blocks = every_coef.reshape(-1, block_len)

    def advance(partial_sum, column_block):
        return (
            partial_sum + matern_sums(row_feats, row_sq, column_block[0], column_block[1]),
            None,
        )

    result, unused = lax.scan(advance, zeros_init, (point_blocks, coef_blocks))
    return result


def per_device(n_blk, n_str, points, coefficients, velocity, targets, batch_rows, counts):
    preview = coefficients + MOMENTUM * velocity
    slot_total = batch_rows.shape[0]
    local_size = points.shape[0]
    slot_ids = jnp.arange(slot_total, dtype=jnp.int32)
    count_here = counts.reshape((1,))
    in_count = slot_ids < count_here[0]
    picked = jnp.take(points, batch_rows, axis=0)
    g = 8
    rows_all, pts_all, prev_all = gather_all(picked, points, preview.reshape(1, -1), g)
    group_rows = rows_all.reshape(-1, points.shape[1])
    piece_points = pts_all.reshape(-1, points.shape[1])
    every_coef = prev_all.reshape(-1)
    partial_value = column_sums(group_rows, piece_points, every_coef)
    kernel_rows = scatter_all(partial_value.reshape(g, g, slot_total), g).reshape(-1)
    residual = jnp.where(
        in_count,
        kernel_rows + NOISE_VAR * jnp.take(preview, batch_rows) - jnp.take(targets, batch_rows),
        0.0,
    )
    scatter_rows = (batch_rows[:, None] == jnp.arange(local_size, dtype=jnp.int32)[None, :]).astype(
        jnp.float32
    )
    update_sum = jnp.dot(residual, scatter_rows, precision=lax.Precision.HIGHEST)
    new_velocity = MOMENTUM * velocity - STEP_SIZE * update_sum
    new_coefficients = coefficients + new_velocity
    return (new_coefficients, new_velocity)


def solution(mesh):
    n_blk = mesh.shape["blk"]
    n_str = mesh.shape["stripe"]
    in_specs = (
        P(("blk", "stripe"), None),
        P(("blk", "stripe")),
        P(("blk", "stripe")),
        P(("blk", "stripe")),
        P(("blk", "stripe")),
        P("blk", "stripe"),
    )
    out_specs = (P(("blk", "stripe")), P(("blk", "stripe")))
    return jax.shard_map(
        functools.partial(per_device, n_blk, n_str), mesh=mesh, in_specs=in_specs,
        out_specs=out_specs, check_vma=False
    )
```

time: 174 us -> 125 us (0.72)
  the two profiles are of different devices: /device:TPU:1 before, /device:TPU:8 now
where the time goes in v4:
time: 125 us
  Pallas kernels  65.2 us (52%)
  matrix products  48 us (38%)
  other arithmetic  5.76 us (5%)
  local copies, waits for them, and re-layouts  4.08 us (3%)
  between operations  1.4 us (1%)
    dot_general x8, matrix products, matern_sums(): lax.dot_general(row_feats, col_points, (((1,), (1,)), ((), ())), preferre...  47.7 us
    pallas_call x1, Pallas kernels, gather_all(): pl.pallas_call(functools.partial(gather_kernel, g), out_shape=(jax.ShapeD...  41.7 us
    pallas_call x1, Pallas kernels, scatter_all(): pl.pallas_call(functools.partial(scatter_kernel, g), out_shape=jax.ShapeD...  23.5 us

profile of v4, /device:TPU:8, one launch (start us, length us, event | category | flops | bytes accessed | tf_op | source)
XLA Modules:
  0.0 124.8 jit_solution(15829292364604249816)
XLA Ops:
  0.6 0.0 copy-start
  0.6 0.7 compare_select_fusion
  1.3 1.0 copy.10.pts
  2.3 0.0 copy-start.2
  2.3 0.6 gather_fusion
  2.9 0.7 compare_and_fusion
  3.6 0.7 broadcast_select_fusion.picked
  4.3 1.3 %multiply_add_fusion = f32[512]{0:T(512)} fusion(f32[512]{0:T(512)} %param.11, f32[512]{0:T(512)} %param.12), kind=kLoop, calls=%fused_computation.25 | loop fusion | flops 1024 | bytes 6144 | tf_op jit(solution)/shard_map/add | solution.py:255
  5.6 0.0 copy-done.2
  5.6 41.7 %shard_map.77 = (bf16[8,8,64,64]{3,2,1,0:T(8,128)(2,1)S(1)}, bf16[8,512,64]{2,1,0:T(8,128)(2,1)S(1)}, f32[8,1,512]{2,1,0:T(1,128)}) custom-call(bf16[64,64]{1,0:T(8,128)(2,1)} %broadcast_select_fusion.picked, bf16[512,64]{1,0:T(8,128)(2,1)} %copy-done.2, f32[1,512]{1,0:T(1,128)} %bitcast.44), custom_call_target="tpu_custom_call" | custom-call | tf_op jit(solution)/shard_map/pallas_call | solution.py:137
  47.3 0.0 copy-start.3
  47.3 0.6 multiply_reduce_fusion.2
  47.9 0.1 reduce_sum.30
  48.0 0.0 copy-done.3
  48.0 0.0 copy-start.1
  48.0 49.4 %while.11 = (s32[]{:T(128)}, f32[4096]{0:T(1024)S(1)}, f32[4096]{0:T(1024)S(1)}, bf16[8,512,64]{2,1,0:T(8,128)(2,1)S(1)}, bf16[4096,64]{1,0:T(8,128)(2,1)S(1)}, /*index=5*/f32[8,512]{1,0:T(8,128)S(1)}, s32[]{:T(128)}, s32[]{:T(128)}) while((s32[]{:T(128)}, f32[4096]{0:T(1024)S(1)}, f32[4096]{0:T(1024)S(1)}, ...), condition=%wide.region_4.5_spmd.clone, body=%wide.region_1.0_spmd.clone.sunk | while | flops 289508864 | bytes 1337451 | solution.py:250
  48.0 0.2 multiply_reduce_fusion.5
  48.2 6.0 %multiply_reduce_fusion.6 = f32[4096]{0:T(1024)S(1)} fusion(bf16[4096,64]{1,0:T(8,128)(2,1)S(1)} %get-tuple-element.134, f32[512]{0:T(512)S(1)} %bitcast.46, f32[512]{0:T(512)S(1)} %multiply_reduce_fusion.5, f32[4096]{0:T(1024)S(1)} %get-tuple-element.132, bf16[8,512,64]{2,1,0:T(8,128)(2,1)S(1)} %get-tuple-element.133, s32[]{:T(128)} %get-tuple-element.122), kind=kOutput, calls=%fused_computation.7.clone.1 | convolution fusion | flops 289402880 | bytes 1216516 | tf_op jit(solution)/shard_map/while/body/eval_jaxpr/dot_general | solution.py:227
  54.2 0.2 multiply_reduce_fusion.5
  54.4 6.0 %multiply_reduce_fusion.6 = f32[4096]{0:T(1024)S(1)} fusion(bf16[4096,64]{1,0:T(8,128)(2,1)S(1)} %get-tuple-element.134, f32[512]{0:T(512)S(1)} %bitcast.46, f32[512]{0:T(512)S(1)} %multiply_reduce_fusion.5, f32[4096]{0:T(1024)S(1)} %get-tuple-element.132, bf16[8,512,64]{2,1,0:T(8,128)(2,1)S(1)} %get-tuple-element.133, s32[]{:T(128)} %get-tuple-element.122), kind=kOutput, calls=%fused_computation.7.clone.1 | convolution fusion | flops 289402880 | bytes 1216516 | tf_op jit(solution)/shard_map/while/body/eval_jaxpr/dot_general | solution.py:227
  60.4 0.2 multiply_reduce_fusion.5
  60.5 6.0 %multiply_reduce_fusion.6 = f32[4096]{0:T(1024)S(1)} fusion(bf16[4096,64]{1,0:T(8,128)(2,1)S(1)} %get-tuple-element.134, f32[512]{0:T(512)S(1)} %bitcast.46, f32[512]{0:T(512)S(1)} %multiply_reduce_fusion.5, f32[4096]{0:T(1024)S(1)} %get-tuple-element.132, bf16[8,512,64]{2,1,0:T(8,128)(2,1)S(1)} %get-tuple-element.133, s32[]{:T(128)} %get-tuple-element.122), kind=kOutput, calls=%fused_computation.7.clone.1 | convolution fusion | flops 289402880 | bytes 1216516 | tf_op jit(solution)/shard_map/while/body/eval_jaxpr/dot_general | solution.py:227
  66.5 0.2 multiply_reduce_fusion.5
  66.7 6.0 %multiply_reduce_fusion.6 = f32[4096]{0:T(1024)S(1)} fusion(bf16[4096,64]{1,0:T(8,128)(2,1)S(1)} %get-tuple-element.134, f32[512]{0:T(512)S(1)} %bitcast.46, f32[512]{0:T(512)S(1)} %multiply_reduce_fusion.5, f32[4096]{0:T(1024)S(1)} %get-tuple-element.132, bf16[8,512,64]{2,1,0:T(8,128)(2,1)S(1)} %get-tuple-element.133, s32[]{:T(128)} %get-tuple-element.122), kind=kOutput, calls=%fused_computation.7.clone.1 | convolution fusion | flops 289402880 | bytes 1216516 | tf_op jit(solution)/shard_map/while/body/eval_jaxpr/dot_general | solution.py:227
  72.7 0.2 multiply_reduce_fusion.5
  72.9 6.0 %multiply_reduce_fusion.6 = f32[4096]{0:T(1024)S(1)} fusion(bf16[4096,64]{1,0:T(8,128)(2,1)S(1)} %get-tuple-element.134, f32[512]{0:T(512)S(1)} %bitcast.46, f32[512]{0:T(512)S(1)} %multiply_reduce_fusion.5, f32[4096]{0:T(1024)S(1)} %get-tuple-element.132, bf16[8,512,64]{2,1,0:T(8,128)(2,1)S(1)} %get-tuple-element.133, s32[]{:T(128)} %get-tuple-element.122), kind=kOutput, calls=%fused_computation.7.clone.1 | convolution fusion | flops 289402880 | bytes 1216516 | tf_op jit(solution)/shard_map/while/body/eval_jaxpr/dot_general | solution.py:227
  78.9 0.2 multiply_reduce_fusion.5
  79.1 6.0 %multiply_reduce_fusion.6 = f32[4096]{0:T(1024)S(1)} fusion(bf16[4096,64]{1,0:T(8,128)(2,1)S(1)} %get-tuple-element.134, f32[512]{0:T(512)S(1)} %bitcast.46, f32[512]{0:T(512)S(1)} %multiply_reduce_fusion.5, f32[4096]{0:T(1024)S(1)} %get-tuple-element.132, bf16[8,512,64]{2,1,0:T(8,128)(2,1)S(1)} %get-tuple-element.133, s32[]{:T(128)} %get-tuple-element.122), kind=kOutput, calls=%fused_computation.7.clone.1 | convolution fusion | flops 289402880 | bytes 1216516 | tf_op jit(solution)/shard_map/while/body/eval_jaxpr/dot_general | solution.py:227
  85.1 0.2 multiply_reduce_fusion.5
  85.3 6.0 %multiply_reduce_fusion.6 = f32[4096]{0:T(1024)S(1)} fusion(bf16[4096,64]{1,0:T(8,128)(2,1)S(1)} %get-tuple-element.134, f32[512]{0:T(512)S(1)} %bitcast.46, f32[512]{0:T(512)S(1)} %multiply_reduce_fusion.5, f32[4096]{0:T(1024)S(1)} %get-tuple-element.132, bf16[8,512,64]{2,1,0:T(8,128)(2,1)S(1)} %get-tuple-element.133, s32[]{:T(128)} %get-tuple-element.122), kind=kOutput, calls=%fused_computation.7.clone.1 | convolution fusion | flops 289402880 | bytes 1216516 | tf_op jit(solution)/shard_map/while/body/eval_jaxpr/dot_general | solution.py:227
  91.3 0.2 multiply_reduce_fusion.5
  91.4 6.0 %multiply_reduce_fusion.6 = f32[4096]{0:T(1024)S(1)} fusion(bf16[4096,64]{1,0:T(8,128)(2,1)S(1)} %get-tuple-element.134, f32[512]{0:T(512)S(1)} %bitcast.46, f32[512]{0:T(512)S(1)} %multiply_reduce_fusion.5, f32[4096]{0:T(1024)S(1)} %get-tuple-element.132, bf16[8,512,64]{2,1,0:T(8,128)(2,1)S(1)} %get-tuple-element.133, s32[]{:T(128)} %get-tuple-element.122), kind=kOutput, calls=%fused_computation.7.clone.1 | convolution fusion | flops 289402880 | bytes 1216516 | tf_op jit(solution)/shard_map/while/body/eval_jaxpr/dot_general | solution.py:227
  97.4 0.0 copy-start.7
  97.5 0.0 copy-start.4
  97.5 0.0 copy-start.5
  97.5 0.7 reshape.32.part
  98.1 23.5 %shard_map.78 = f32[1,64]{1,0:T(1,128)} custom-call(f32[8,8,64]{2,1,0:T(8,128)} %reshape.32.part), custom_call_target="tpu_custom_call" | custom-call | tf_op jit(solution)/shard_map/pallas_call | solution.py:210
  121.7 0.0 copy-done.1
  121.7 0.0 copy-start.6
  121.7 0.8 gather_fusion.1
  122.5 0.0 copy-done
  122.5 0.8 gather_fusion.2
  123.9 0.0 copy-done.7
  124.0 0.0 copy-done.6
  124.0 0.2 fusion.6
  124.2 0.0 copy-done.4
  124.2 0.0 copy-done.5
  124.2 0.6 fusion.21
  (19 shorter events, 0.1 us)
Async XLA Ops:
  0.6 121.9 %copy-start = (f32[512]{0:T(512)S(1)}, f32[512]{0:T(512)}, u32[]{:S(2)}) copy-start(f32[512]{0:T(512)} %param.13) | copy-start | bytes 6148
  2.3 3.3 %copy-start.2 = (bf16[512,64]{1,0:T(8,128)(2,1)}, bf16[512,64]{1,0:T(8,128)(2,1)S(1)}, u32[]{:S(2)}) copy-start(bf16[512,64]{1,0:T(8,128)(2,1)S(1)} %copy.10.pts) | copy-start | bytes 196612
  47.3 0.7 copy-start.3
  48.0 73.7 %copy-start.1 = (f32[512]{0:T(512)S(1)}, f32[512]{0:T(512)}, u32[]{:S(2)}) copy-start(f32[512]{0:T(512)} %multiply_add_fusion) | copy-start | bytes 6148
  97.4 26.5 %copy-start.7 = (s32[64]{0:T(128)S(1)}, s32[64]{0:T(128)}, u32[]{:S(2)}) copy-start(s32[64]{0:T(128)} %param.14) | copy-start | bytes 772
  97.5 26.7 %copy-start.4 = (f32[512]{0:T(512)S(1)}, f32[512]{0:T(512)}, u32[]{:S(2)}) copy-start(f32[512]{0:T(512)} %param.11) | copy-start | bytes 6148
  97.5 26.7 %copy-start.5 = (f32[512]{0:T(512)S(1)}, f32[512]{0:T(512)}, u32[]{:S(2)}) copy-start(f32[512]{0:T(512)} %param.12) | copy-start | bytes 6148
  121.7 2.3 %copy-start.6 = (f32[1,64]{1,0:T(1,128)S(1)}, f32[1,64]{1,0:T(1,128)}, u32[]{:S(2)}) copy-start(f32[1,64]{1,0:T(1,128)} %shard_map.78) | copy-start | bytes 772

commit v5 on v4

--- a/solution.py
+++ b/solution.py
@@ -222,33 +222,55 @@
     )(part)
 
 
-def matern_sums(row_feats, row_sq, col_points, col_coef):
-    col_sq = jnp.sum(jnp.square(col_points.astype(jnp.float32)), axis=1)
-    inner_prod = lax.dot_general(
-        row_feats, col_points, (((1,), (1,)), ((), ())), preferred_element_type=jnp.float32
-    )
-    distance = jnp.sqrt(jnp.maximum(row_sq[:, None] + col_sq[None, :] - 2.0 * inner_prod, 0.0))
-    scaled = KERNEL_RATE * distance
-    kernel_tile = (1.0 + scaled) * jnp.exp(-scaled)
-    return jnp.sum(kernel_tile * col_coef[None, :], axis=1)
+def tile_kernel(rows_ref, pts_ref, rs_ref, cs_ref, coef_ref, out_ref):
+    row_chunk, col_chunk, lanes = 64, 512, 128
+    n_cols = pts_ref.shape[0]
+
+    def body(r, carry):
+        r0 = pl.multiple_of(r * row_chunk, row_chunk)
+        rows = rows_ref[pl.ds(r0, row_chunk), :]
+        rs = rs_ref[pl.ds(r0, row_chunk), :]
+        acc = jnp.zeros((row_chunk, lanes), jnp.float32)
+        for cj in range(n_cols // col_chunk):
+            cols = slice(cj * col_chunk, (cj + 1) * col_chunk)
+            neg_two_dot = lax.dot_general(
+                rows, pts_ref[cols, :], (((1,), (1,)), ((), ())),
+                preferred_element_type=jnp.float32)
+            sq = (rs + cs_ref[:, cols]) + neg_two_dot
+            m = jnp.sqrt(jnp.maximum(sq, 0.0)) * (-KERNEL_RATE)
+            term = ((1.0 - m) * jnp.exp(m)) * coef_ref[:, cols]
+            for l in range(col_chunk // lanes):
+                acc = acc + term[:, l * lanes:(l + 1) * lanes]
+        out_ref[pl.ds(r0, row_chunk), :] = jnp.sum(acc, axis=1, keepdims=True)
+        return carry
+
+    lax.fori_loop(0, rows_ref.shape[0] // row_chunk, body, 0)
 
 
 def column_sums(row_feats, piece_points, every_coef):
-    row_sq = jnp.sum(jnp.square(row_feats.astype(jnp.float32)), axis=1)
-    zeros_init = jnp.zeros((row_feats.shape[0],), jnp.float32)
-    piece_len = piece_points.shape[0]
-    block_len = math.gcd(piece_len, 512)
-    point_blocks = piece_points.reshape(-1, block_len, piece_points.shape[1])
-    coef_blocks = every_coef.reshape(-1, block_len)
-
-    def advance(partial_sum, column_block):
-        return (
-            partial_sum + matern_sums(row_feats, row_sq, column_block[0], column_block[1]),
-            None,
-        )
-
-    result, unused = lax.scan(advance, zeros_init, (point_blocks, coef_blocks))
-    return result
+    n_rows, n_cols = row_feats.shape[0], piece_points.shape[0]
+    row_sq = jnp.sum(jnp.square(row_feats.astype(jnp.float32)), axis=1, keepdims=True)
+    col_sq = jnp.sum(jnp.square(piece_points.astype(jnp.float32)), axis=1)[None, :]
+    neg_two_rows = row_feats * jnp.asarray(-2.0, row_feats.dtype)
+    block = math.gcd(n_rows, 512)
+    full = lambda i: (0, 0)
+    return pl.pallas_call(
+        tile_kernel,
+        out_shape=jax.ShapeDtypeStruct((n_rows, 1), jnp.float32),
+        grid=(n_rows // block,),
+        in_specs=[
+            pl.BlockSpec((block, row_feats.shape[1]), lambda i: (i, 0)),
+            pl.BlockSpec(piece_points.shape, full),
+            pl.BlockSpec((block, 1), lambda i: (i, 0)),
+            pl.BlockSpec((1, n_cols), full),
+            pl.BlockSpec((1, n_cols), full),
+        ],
+        out_specs=pl.BlockSpec((block, 1), lambda i: (i, 0)),
+        cost_estimate=pl.CostEstimate(
+            flops=n_rows * n_cols * (2 * row_feats.shape[1] + 10),
+            transcendentals=2 * n_rows * n_cols,
+            bytes_accessed=2 * (n_rows + n_cols) * row_feats.shape[1] + 12 * (n_rows + n_cols)),
+    )(neg_two_rows, piece_points, row_sq, col_sq, every_coef[None, :]).reshape(-1)
 
 
 def per_device(n_blk, n_str, points, coefficients, velocity, targets, batch_rows, counts):

time: 125 us -> 147 us (1.18)
  Pallas kernels: 65.2 us -> 126 us
  matrix products: 48 us -> 0.85 us
  other arithmetic: 5.76 us -> 10.4 us
  local copies, waits for them, and re-layouts: 4.08 us -> 7.95 us
    pallas_call x0 -> x1, Pallas kernels: none -> 60.3 us  [column_sums(): pl.pallas_call(tile_kernel, out_shape=jax.ShapeDtypeStruct((n_rows, 1), j...]
    dot_general x8 -> x0, matrix products: 47.7 us -> none  [matern_sums(): lax.dot_general(row_feats, col_points, (((1,), (1,)), ((), ())), preferre...]
    broadcast_in_dim x0 -> x1, local copies, waits for them, and re-layouts: none -> 3.44 us  [column_sums(): jnp.sum(jnp.square(row_feats.astype(jnp.float32)), axis=1, keepdims=True)]
    pallas_call x0 -> x1, other arithmetic: none -> 2.23 us  [column_sums(): pl.pallas_call(tile_kernel, out_shape=jax.ShapeDtypeStruct((n_rows, 1), j...]
    reduce_sum x9 -> x2, other arithmetic: 1.83 us -> 3.76 us  [the longest x1 1.93 us: column_sums(): jnp.sum(jnp.square(piece_points.astype(jnp.float32)), axis=1)[None, :]]
where the time goes in v5:
time: 147 us; the launch traced here: 146 us
  Pallas kernels  126 us (86%)
  other arithmetic  10.4 us (7%)
  local copies, waits for them, and re-layouts  7.95 us (5%)
    pallas_call x1, Pallas kernels, column_sums(): pl.pallas_call(tile_kernel, out_shape=jax.ShapeDtypeStruct((n_rows, 1), j...  60.3 us
    pallas_call x1, Pallas kernels, gather_all(): pl.pallas_call(functools.partial(gather_kernel, g), out_shape=(jax.ShapeD...  41.8 us
    pallas_call x1, Pallas kernels, scatter_all(): pl.pallas_call(functools.partial(scatter_kernel, g), out_shape=jax.ShapeD...  23.8 us
    broadcast_in_dim x1, local copies, waits for them, and re-layouts, column_sums(): jnp.sum(jnp.square(row_feats.astype(jnp.float32)), axis=1, keepdims=True)  3.44 us

profile of v5, /device:TPU:8, one launch (start us, length us, event | category | flops | bytes accessed | tf_op | source)
XLA Modules:
  0.0 146.4 jit_solution(5002206907005805739)
XLA Ops:
  0.6 0.0 copy-start
  1.3 0.7 compare_and_fusion
  2.0 0.7 compare_select_fusion
  2.6 0.7 multiply_add_fusion
  3.3 0.0 copy-start.1
  3.3 0.0 copy-done
  3.3 0.8 gather_fusion.2
  4.1 0.8 gather_fusion.1
  4.9 1.0 copy.10.pts
  5.9 0.0 copy-start.3
  5.9 0.6 gather_fusion
  6.5 0.7 broadcast_select_fusion.picked
  7.2 0.0 copy-done.1
  7.2 0.0 copy-done.3
  7.2 41.8 %shard_map.77 = (bf16[8,8,64,64]{3,2,1,0:T(8,128)(2,1)}, bf16[8,512,64]{2,1,0:T(8,128)(2,1)}, f32[8,1,512]{2,1,0:T(1,128)}) custom-call(bf16[64,64]{1,0:T(8,128)(2,1)} %broadcast_select_fusion.picked, bf16[512,64]{1,0:T(8,128)(2,1)} %copy-done.3, f32[1,512]{1,0:T(1,128)} %bitcast.20), custom_call_target="tpu_custom_call" | custom-call | tf_op jit(solution)/shard_map/pallas_call | solution.py:137
  49.0 0.0 copy-start.2
  49.0 1.9 %multiply_reduce_fusion = f32[8,512]{1,0:T(8,128)S(1)} fusion(bf16[8,512,64]{2,1,0:T(8,128)(2,1)} %get-tuple-element.7), kind=kLoop, calls=%fused_computation.3 | loop fusion | flops 782336 | bytes 540672 | tf_op jit(solution)/shard_map/reduce_sum | solution.py:253
  51.0 0.6 copy.13
  51.6 1.8 %multiply_reduce_fusion.1 = f32[8,8,64]{2,1,0:T(8,128)S(1)} fusion(bf16[8,8,64,64]{3,2,1,0:T(8,128)(2,1)} %get-tuple-element.6), kind=kLoop, calls=%fused_computation.4 | loop fusion | flops 782336 | bytes 540672 | tf_op jit(solution)/shard_map/reduce_sum | solution.py:252
  53.4 0.0 copy-done.2
  53.4 1.1 broadcast_multiply_fusion
  54.5 3.4 %broadcast_in_dim.40.rs_ref = f32[4096,1]{1,0:T(8,128)} reshape(f32[8,8,64]{2,1,0:T(8,128)S(1)} %multiply_reduce_fusion.1) | data formatting | bytes 32768 | tf_op jit(solution)/shard_map/broadcast_in_dim | solution.py:252
  58.0 60.3 %shard_map.78 = f32[4096,1]{1,0:T(8,128)} custom-call(bf16[4096,64]{1,0:T(8,128)(2,1)} %bitcast.22, bf16[4096,64]{1,0:T(8,128)(2,1)} %bitcast.21, f32[4096,1]{1,0:T(8,128)} %broadcast_in_dim.40.rs_ref, f32[1,4096]{1,0:T(1,128)} %bitcast.24, f32[1,4096]{1,0:T(1,128)} %bitcast.26), custom_call_target="tpu_custom_call" | custom-call | flops 2315255808 | bytes 1146880 | tf_op jit(solution)/shard_map/pallas_call | solution.py:257
  118.2 0.0 copy-start.6
  118.2 0.0 copy-start.4
  118.2 0.0 copy-start.5
  118.3 2.2 %reduce.2 = f32[4096]{0:T(1024)S(1)} reduce(f32[4096,1]{1,0:T(8,128)} %shard_map.78, f32[]{:T(128)} %constant.36), dimensions={1}, to_apply=%pallas_call.16.reduce_sub_computation | reduce | bytes 32772 | tf_op jit(solution)/shard_map/pallas_call | solution.py:257
  120.5 0.7 reshape_reshape.3.part
  121.2 23.8 %shard_map.79 = f32[1,64]{1,0:T(1,128)} custom-call(f32[8,8,64]{2,1,0:T(8,128)} %reshape_reshape.3.part), custom_call_target="tpu_custom_call" | custom-call | tf_op jit(solution)/shard_map/pallas_call | solution.py:210
  145.0 0.0 copy-done.6
  145.0 0.9 fusion
  145.8 0.0 copy-done.4
  145.8 0.0 copy-done.5
  145.9 0.6 fusion.15
  (1 shorter events, 0.0 us)
Async XLA Ops:
  0.6 2.7 %copy-start = (f32[512]{0:T(512)S(1)}, f32[512]{0:T(512)}, u32[]{:S(2)}) copy-start(f32[512]{0:T(512)} %param.11) | copy-start | bytes 6148
  3.3 3.9 %copy-start.1 = (f32[512]{0:T(512)}, f32[512]{0:T(512)S(1)}, u32[]{:S(2)}) copy-start(f32[512]{0:T(512)S(1)} %multiply_add_fusion) | copy-start | bytes 6148
  5.9 1.3 copy-start.3
  49.0 4.4 %copy-start.2 = (bf16[8,8,64,64]{3,2,1,0:T(8,128)(2,1)S(1)}, bf16[8,8,64,64]{3,2,1,0:T(8,128)(2,1)}, u32[]{:S(2)}) copy-start(bf16[8,8,64,64]{3,2,1,0:T(8,128)(2,1)} %get-tuple-element.6) | copy-start | bytes 1572868
  118.2 26.7 %copy-start.6 = (s32[64]{0:T(128)S(1)}, s32[64]{0:T(128)}, u32[]{:S(2)}) copy-start(s32[64]{0:T(128)} %param.12) | copy-start | bytes 772
  118.2 27.6 %copy-start.4 = (f32[512]{0:T(512)S(1)}, f32[512]{0:T(512)}, u32[]{:S(2)}) copy-start(f32[512]{0:T(512)} %param.9) | copy-start | bytes 6148
  118.2 27.6 %copy-start.5 = (f32[512]{0:T(512)S(1)}, f32[512]{0:T(512)}, u32[]{:S(2)}) copy-start(f32[512]{0:T(512)} %param.10) | copy-start | bytes 6148

commit v6 on v5

--- a/solution.py
+++ b/solution.py
@@ -222,55 +222,58 @@
     )(part)
 
 
-def tile_kernel(rows_ref, pts_ref, rs_ref, cs_ref, coef_ref, out_ref):
-    row_chunk, col_chunk, lanes = 64, 512, 128
-    n_cols = pts_ref.shape[0]
-
-    def body(r, carry):
-        r0 = pl.multiple_of(r * row_chunk, row_chunk)
-        rows = rows_ref[pl.ds(r0, row_chunk), :]
-        rs = rs_ref[pl.ds(r0, row_chunk), :]
-        acc = jnp.zeros((row_chunk, lanes), jnp.float32)
-        for cj in range(n_cols // col_chunk):
-            cols = slice(cj * col_chunk, (cj + 1) * col_chunk)
-            neg_two_dot = lax.dot_general(
-                rows, pts_ref[cols, :], (((1,), (1,)), ((), ())),
-                preferred_element_type=jnp.float32)
-            sq = (rs + cs_ref[:, cols]) + neg_two_dot
+def tile_kernel(pts_ref, rows_t_ref, rs_ref, cs_ref, coef_ref, out_ref):
+    pt_chunk, lanes, sub = 256, 128, 8
+    n_pts = pts_ref.shape[0]
+
+    def lane_tile(t, carry):
+        c0 = pl.multiple_of(t * lanes, lanes)
+        rows_t = rows_t_ref[:, pl.ds(c0, lanes)]
+        rs = jnp.broadcast_to(rs_ref[:, pl.ds(c0, lanes)], (pt_chunk, lanes))
+
+        def chunk(p, acc):
+            p0 = pl.multiple_of(p * pt_chunk, pt_chunk)
+            neg_two_dot = jnp.dot(pts_ref[pl.ds(p0, pt_chunk), :], rows_t,
+                                  preferred_element_type=jnp.float32)
+            sq = (rs + cs_ref[pl.ds(p0, pt_chunk), :]) + neg_two_dot
             m = jnp.sqrt(jnp.maximum(sq, 0.0)) * (-KERNEL_RATE)
-            term = ((1.0 - m) * jnp.exp(m)) * coef_ref[:, cols]
-            for l in range(col_chunk // lanes):
-                acc = acc + term[:, l * lanes:(l + 1) * lanes]
-        out_ref[pl.ds(r0, row_chunk), :] = jnp.sum(acc, axis=1, keepdims=True)
-        return carry
-
-    lax.fori_loop(0, rows_ref.shape[0] // row_chunk, body, 0)
+            term = ((1.0 - m) * jnp.exp(m)) * coef_ref[pl.ds(p0, pt_chunk), :]
+            return acc + jnp.sum(term.reshape(pt_chunk // sub, sub, lanes), axis=0)
+
+        acc = lax.fori_loop(0, n_pts // pt_chunk, chunk, jnp.zeros((sub, lanes), jnp.float32))
+        out_ref[:, pl.ds(c0, lanes)] = jnp.sum(acc, axis=0, keepdims=True)
+        return carry
+
+    lax.fori_loop(0, out_ref.shape[1] // lanes, lane_tile, 0)
 
 
 def column_sums(row_feats, piece_points, every_coef):
-    n_rows, n_cols = row_feats.shape[0], piece_points.shape[0]
-    row_sq = jnp.sum(jnp.square(row_feats.astype(jnp.float32)), axis=1, keepdims=True)
-    col_sq = jnp.sum(jnp.square(piece_points.astype(jnp.float32)), axis=1)[None, :]
-    neg_two_rows = row_feats * jnp.asarray(-2.0, row_feats.dtype)
+    n_rows, n_pts = row_feats.shape[0], piece_points.shape[0]
+    lanes = 128
+    row_sq = jnp.sum(jnp.square(row_feats.astype(jnp.float32)), axis=1)[None, :]
+    col_sq = jnp.sum(jnp.square(piece_points.astype(jnp.float32)), axis=1)
+    col_sq = jnp.broadcast_to(col_sq[:, None], (n_pts, lanes))
+    coef = jnp.broadcast_to(every_coef[:, None], (n_pts, lanes))
+    neg_two_rows_t = (row_feats * jnp.asarray(-2.0, row_feats.dtype)).T
     block = math.gcd(n_rows, 512)
     full = lambda i: (0, 0)
     return pl.pallas_call(
         tile_kernel,
-        out_shape=jax.ShapeDtypeStruct((n_rows, 1), jnp.float32),
+        out_shape=jax.ShapeDtypeStruct((1, n_rows), jnp.float32),
         grid=(n_rows // block,),
         in_specs=[
-            pl.BlockSpec((block, row_feats.shape[1]), lambda i: (i, 0)),
             pl.BlockSpec(piece_points.shape, full),
-            pl.BlockSpec((block, 1), lambda i: (i, 0)),
-            pl.BlockSpec((1, n_cols), full),
-            pl.BlockSpec((1, n_cols), full),
+            pl.BlockSpec((row_feats.shape[1], block), lambda i: (0, i)),
+            pl.BlockSpec((1, block), lambda i: (0, i)),
+            pl.BlockSpec((n_pts, lanes), full),
+            pl.BlockSpec((n_pts, lanes), full),
         ],
-        out_specs=pl.BlockSpec((block, 1), lambda i: (i, 0)),
+        out_specs=pl.BlockSpec((1, block), lambda i: (0, i)),
         cost_estimate=pl.CostEstimate(
-            flops=n_rows * n_cols * (2 * row_feats.shape[1] + 10),
-            transcendentals=2 * n_rows * n_cols,
-            bytes_accessed=2 * (n_rows + n_cols) * row_feats.shape[1] + 12 * (n_rows + n_cols)),
-    )(neg_two_rows, piece_points, row_sq, col_sq, every_coef[None, :]).reshape(-1)
+            flops=n_rows * n_pts * (2 * row_feats.shape[1] + 10),
+            transcendentals=2 * n_rows * n_pts,
+            bytes_accessed=2 * (n_rows + n_pts) * row_feats.shape[1] + 1024 * n_pts),
+    )(piece_points, neg_two_rows_t, row_sq, col_sq, coef).reshape(-1)
 
 
 def per_device(n_blk, n_str, points, coefficients, velocity, targets, batch_rows, counts):

time: 147 us -> 199 us (1.35)
  Pallas kernels: 126 us -> 177 us
  local copies, waits for them, and re-layouts: 7.95 us -> 10.1 us
    pallas_call x1, Pallas kernels: 60.3 us -> 112 us  [column_sums(): pl.pallas_call(tile_kernel, out_shape=jax.ShapeDtypeStruct((1, n_rows), j...]
    broadcast_in_dim x1 -> x3, local copies, waits for them, and re-layouts: 3.44 us -> 4.55 us  [the longest x1 1.95 us: column_sums(): col_sq = jnp.broadcast_to(col_sq[:, None], (n_pts, lanes))]
where the time goes in v6:
time: 199 us; the launch traced here: 198 us
  Pallas kernels  177 us (89%)
  local copies, waits for them, and re-layouts  10.1 us (5%)
  other arithmetic  8.53 us (4%)
    pallas_call x1, Pallas kernels, column_sums(): pl.pallas_call(tile_kernel, out_shape=jax.ShapeDtypeStruct((1, n_rows), j...  112 us
    pallas_call x1, Pallas kernels, gather_all(): pl.pallas_call(functools.partial(gather_kernel, g), out_shape=(jax.ShapeD...  41.8 us
    pallas_call x1, Pallas kernels, scatter_all(): pl.pallas_call(functools.partial(scatter_kernel, g), out_shape=jax.ShapeD...  23.8 us

profile of v6, /device:TPU:8, one launch (start us, length us, event | category | flops | bytes accessed | tf_op | source)
XLA Modules:
  0.0 198.1 jit_solution(3223748799155204844)
XLA Ops:
  0.6 0.0 copy-start
  1.3 0.7 compare_and_fusion
  2.0 0.7 compare_select_fusion
  2.6 0.7 multiply_add_fusion
  3.3 0.0 copy-start.1
  3.3 0.0 copy-done
  3.3 0.8 gather_fusion.2
  4.1 0.8 gather_fusion.1
  4.9 1.0 copy.11.pts
  5.9 0.0 copy-start.3
  5.9 0.6 gather_fusion
  6.5 0.7 broadcast_select_fusion.picked
  7.2 0.0 copy-done.1
  7.2 0.0 copy-done.3
  7.2 41.8 %shard_map.77 = (bf16[8,8,64,64]{3,2,1,0:T(8,128)(2,1)}, bf16[8,512,64]{2,1,0:T(8,128)(2,1)}, f32[8,1,512]{2,1,0:T(1,128)}) custom-call(bf16[64,64]{1,0:T(8,128)(2,1)} %broadcast_select_fusion.picked, bf16[512,64]{1,0:T(8,128)(2,1)} %copy-done.3, f32[1,512]{1,0:T(1,128)} %bitcast.20), custom_call_target="tpu_custom_call" | custom-call | tf_op jit(solution)/shard_map/pallas_call | solution.py:137
  49.0 0.0 copy-start.2
  49.0 1.9 multiply_reduce_fusion
  51.0 1.8 multiply_reduce_fusion.1
  52.8 0.7 broadcast_in_dim.45.rs_ref
  53.5 0.0 copy-done.2
  53.5 0.1 broadcast_multiply_fusion
  53.6 0.0 copy-start.4
  53.6 1.2 copy.14
  54.8 2.0 broadcast_in_dim.47.cs_ref
  56.7 0.0 copy-done.4
  56.7 1.9 broadcast_in_dim.49.coef_ref
  58.6 0.0 copy-start.7
  58.6 0.0 copy-start.5
  58.6 0.0 copy-start.6
  58.6 111.5 %shard_map.78 = f32[1,4096]{1,0:T(1,128)} custom-call(bf16[4096,64]{1,0:T(8,128)(2,1)} %bitcast.22, bf16[64,4096]{1,0:T(8,128)(2,1)} %bitcast.23, f32[1,4096]{1,0:T(1,128)} %broadcast_in_dim.45.rs_ref, f32[4096,128]{1,0:T(8,128)} %broadcast_in_dim.47.cs_ref, f32[4096,128]{1,0:T(8,128)} %broadcast_in_dim.49.coef_ref), custom_call_target="tpu_custom_call" | custom-call | flops 2315255808 | bytes 5242880 | tf_op jit(solution)/shard_map/pallas_call | solution.py:260
  170.1 0.5 broadcast.25
  170.6 1.4 reduce.5
  172.1 0.7 reshape_reshape.3.part
  172.7 23.8 %shard_map.79 = f32[1,64]{1,0:T(1,128)} custom-call(f32[8,8,64]{2,1,0:T(8,128)} %reshape_reshape.3.part), custom_call_target="tpu_custom_call" | custom-call | tf_op jit(solution)/shard_map/pallas_call | solution.py:210
  196.6 0.0 copy-done.7
  196.6 0.9 fusion
  197.5 0.0 copy-done.5
  197.5 0.0 copy-done.6
  197.5 0.6 fusion.15
  (2 shorter events, 0.0 us)
Async XLA Ops:
  0.6 2.7 %copy-start = (f32[512]{0:T(512)S(1)}, f32[512]{0:T(512)}, u32[]{:S(2)}) copy-start(f32[512]{0:T(512)} %param.11) | copy-start | bytes 6148
  3.3 3.9 %copy-start.1 = (f32[512]{0:T(512)}, f32[512]{0:T(512)S(1)}, u32[]{:S(2)}) copy-start(f32[512]{0:T(512)S(1)} %multiply_add_fusion) | copy-start | bytes 6148
  5.9 1.3 copy-start.3
  49.0 4.5 %copy-start.2 = (bf16[8,8,64,64]{3,2,1,0:T(8,128)(2,1)S(1)}, bf16[8,8,64,64]{3,2,1,0:T(8,128)(2,1)}, u32[]{:S(2)}) copy-start(bf16[8,8,64,64]{3,2,1,0:T(8,128)(2,1)} %get-tuple-element.7) | copy-start | bytes 1572868
  53.6 3.1 %copy-start.4 = (f32[8,1,512]{2,1,0:T(1,128)S(1)}, f32[8,1,512]{2,1,0:T(1,128)}, u32[]{:S(2)}) copy-start(f32[8,1,512]{2,1,0:T(1,128)} %get-tuple-element.8) | copy-start | bytes 49156
  58.6 138.0 %copy-start.7 = (s32[64]{0:T(128)S(1)}, s32[64]{0:T(128)}, u32[]{:S(2)}) copy-start(s32[64]{0:T(128)} %param.12) | copy-start | bytes 772
  58.6 138.9 %copy-start.5 = (f32[512]{0:T(512)S(1)}, f32[512]{0:T(512)}, u32[]{:S(2)}) copy-start(f32[512]{0:T(512)} %param.9) | copy-start | bytes 6148
  58.6 138.9 %copy-start.6 = (f32[512]{0:T(512)S(1)}, f32[512]{0:T(512)}, u32[]{:S(2)}) copy-start(f32[512]{0:T(512)} %param.10) | copy-start | bytes 6148

commit v7 on v5

--- a/solution.py
+++ b/solution.py
@@ -222,22 +222,21 @@
     )(part)
 
 
-def tile_kernel(rows_ref, pts_ref, rs_ref, cs_ref, coef_ref, out_ref):
+def tile_kernel(rows_ref, pts_ref, coef_ref, out_ref):
     row_chunk, col_chunk, lanes = 64, 512, 128
     n_cols = pts_ref.shape[0]
 
     def body(r, carry):
         r0 = pl.multiple_of(r * row_chunk, row_chunk)
         rows = rows_ref[pl.ds(r0, row_chunk), :]
-        rs = rs_ref[pl.ds(r0, row_chunk), :]
         acc = jnp.zeros((row_chunk, lanes), jnp.float32)
         for cj in range(n_cols // col_chunk):
             cols = slice(cj * col_chunk, (cj + 1) * col_chunk)
-            neg_two_dot = lax.dot_general(
+            sq = lax.dot_general(
                 rows, pts_ref[cols, :], (((1,), (1,)), ((), ())),
                 preferred_element_type=jnp.float32)
-            sq = (rs + cs_ref[:, cols]) + neg_two_dot
-            m = jnp.sqrt(jnp.maximum(sq, 0.0)) * (-KERNEL_RATE)
+            dist = jnp.where(sq > 0.0, sq * lax.rsqrt(sq), 0.0)
+            m = dist * (-KERNEL_RATE)
             term = ((1.0 - m) * jnp.exp(m)) * coef_ref[:, cols]
             for l in range(col_chunk // lanes):
                 acc = acc + term[:, l * lanes:(l + 1) * lanes]
@@ -247,11 +246,27 @@
     lax.fori_loop(0, rows_ref.shape[0] // row_chunk, body, 0)
 
 
+def split3(v):
+    hi = lax.reduce_precision(v, exponent_bits=8, mantissa_bits=7)
+    rest = v - hi
+    mid = lax.reduce_precision(rest, exponent_bits=8, mantissa_bits=7)
+    lo = rest - mid
+    return jnp.stack([hi, mid, lo], axis=1).astype(jnp.bfloat16)
+
+
 def column_sums(row_feats, piece_points, every_coef):
     n_rows, n_cols = row_feats.shape[0], piece_points.shape[0]
-    row_sq = jnp.sum(jnp.square(row_feats.astype(jnp.float32)), axis=1, keepdims=True)
-    col_sq = jnp.sum(jnp.square(piece_points.astype(jnp.float32)), axis=1)[None, :]
-    neg_two_rows = row_feats * jnp.asarray(-2.0, row_feats.dtype)
+    depth = row_feats.shape[1]
+    width = 128 * ((depth + 6 + 127) // 128)
+    row_sq = jnp.sum(jnp.square(row_feats.astype(jnp.float32)), axis=1)
+    col_sq = jnp.sum(jnp.square(piece_points.astype(jnp.float32)), axis=1)
+    one = jnp.bfloat16
+    rows_aug = jnp.concatenate([
+        row_feats * jnp.asarray(-2.0, one), jnp.ones((n_rows, 3), one), split3(row_sq),
+        jnp.zeros((n_rows, width - depth - 6), one)], axis=1)
+    pts_aug = jnp.concatenate([
+        piece_points, split3(col_sq), jnp.ones((n_cols, 3), one),
+        jnp.zeros((n_cols, width - depth - 6), one)], axis=1)
     block = math.gcd(n_rows, 512)
     full = lambda i: (0, 0)
     return pl.pallas_call(
@@ -259,18 +274,16 @@
         out_shape=jax.ShapeDtypeStruct((n_rows, 1), jnp.float32),
         grid=(n_rows // block,),
         in_specs=[
-            pl.BlockSpec((block, row_feats.shape[1]), lambda i: (i, 0)),
-            pl.BlockSpec(piece_points.shape, full),
-            pl.BlockSpec((block, 1), lambda i: (i, 0)),
-            pl.BlockSpec((1, n_cols), full),
+            pl.BlockSpec((block, width), lambda i: (i, 0)),
+            pl.BlockSpec((n_cols, width), full),
             pl.BlockSpec((1, n_cols), full),
         ],
         out_specs=pl.BlockSpec((block, 1), lambda i: (i, 0)),
         cost_estimate=pl.CostEstimate(
-            flops=n_rows * n_cols * (2 * row_feats.shape[1] + 10),
+            flops=n_rows * n_cols * (2 * width + 10),
             transcendentals=2 * n_rows * n_cols,
-            bytes_accessed=2 * (n_rows + n_cols) * row_feats.shape[1] + 12 * (n_rows + n_cols)),
-    )(neg_two_rows, piece_points, row_sq, col_sq, every_coef[None, :]).reshape(-1)
+            bytes_accessed=2 * (n_rows + n_cols) * width + 4 * (n_rows + n_cols)),
+    )(rows_aug, pts_aug, every_coef[None, :]).reshape(-1)
 
 
 def per_device(n_blk, n_str, points, coefficients, velocity, targets, batch_rows, counts):

time: 147 us -> 161 us (1.095)
  local copies, waits for them, and re-layouts: 7.95 us -> 26.2 us
  Pallas kernels: 126 us -> 112 us
  other arithmetic: 10.4 us -> 19.5 us
    concatenate x0 -> x2, local copies, waits for them, and re-layouts: none -> 13.5 us  [the longest x1 6.76 us: column_sums(): jnp.concatenate([row_feats * jnp.asarray(-2.0, one), jnp.ones((n_rows, 3)...]
    pallas_call x1, Pallas kernels: 60.3 us -> 46.9 us  [column_sums(): pl.pallas_call(tile_kernel, out_shape=jax.ShapeDtypeStruct((n_rows, 1), j...]
    another operation x0 -> x2, other arithmetic: none -> 7.37 us
    reduce_sum x0 -> x3, local copies, waits for them, and re-layouts: none -> 4.06 us  [the longest x2 2.07 us: column_sums(): row_sq = jnp.sum(jnp.square(row_feats.astype(jnp.float32)), axis=1)]
    broadcast_in_dim x1 -> x0, local copies, waits for them, and re-layouts: 3.44 us -> none  [column_sums(): jnp.sum(jnp.square(row_feats.astype(jnp.float32)), axis=1, keepdims=True)]
    reduce_precision x0 -> x2, local copies, waits for them, and re-layouts: none -> 2.6 us  [split3(): hi = lax.reduce_precision(v, exponent_bits=8, mantissa_bits=7)]
    another operation x0 -> x4, local copies, waits for them, and re-layouts: none -> 2.17 us
where the time goes in v7:
time: 161 us; the launch traced here: 160 us
  Pallas kernels  112 us (70%)
  local copies, waits for them, and re-layouts  26.2 us (16%)
  other arithmetic  19.5 us (12%)
    pallas_call x1, Pallas kernels, column_sums(): pl.pallas_call(tile_kernel, out_shape=jax.ShapeDtypeStruct((n_rows, 1), j...  46.9 us
    pallas_call x1, Pallas kernels, gather_all(): pl.pallas_call(functools.partial(gather_kernel, g), out_shape=(jax.ShapeD...  41.8 us
    pallas_call x1, Pallas kernels, scatter_all(): pl.pallas_call(functools.partial(scatter_kernel, g), out_shape=jax.ShapeD...  23.8 us
    another operation x2, other arithmetic  7.37 us
    concatenate x1, local copies, waits for them, and re-layouts, column_sums(): jnp.concatenate([row_feats * jnp.asarray(-2.0, one), jnp.ones((n_rows, 3)...  6.76 us
    concatenate x1, local copies, waits for them, and re-layouts, column_sums(): jnp.concatenate([piece_points, split3(col_sq), jnp.ones((n_cols, 3), one)...  6.72 us

profile of v7, /device:TPU:8, one launch (start us, length us, event | category | flops | bytes accessed | tf_op | source)
XLA Modules:
  0.0 160.5 jit_solution(16676819607030111487)
XLA Ops:
  0.6 0.0 copy-start
  0.6 0.7 compare_select_fusion
  1.3 1.0 copy.16.pts
  2.3 0.0 copy-start.3
  2.3 0.6 gather_fusion
  2.9 0.7 compare_and_fusion
  3.6 0.7 broadcast_select_fusion.picked
  4.3 1.3 multiply_add_fusion
  5.5 0.0 copy-done.3
  5.5 41.8 %shard_map.77 = (bf16[8,8,64,64]{3,2,1,0:T(8,128)(2,1)}, bf16[8,512,64]{2,1,0:T(8,128)(2,1)}, f32[8,1,512]{2,1,0:T(1,128)}) custom-call(bf16[64,64]{1,0:T(8,128)(2,1)} %broadcast_select_fusion.picked, bf16[512,64]{1,0:T(8,128)(2,1)} %copy-done.3, f32[1,512]{1,0:T(1,128)} %bitcast.21), custom_call_target="tpu_custom_call" | custom-call | tf_op jit(solution)/shard_map/pallas_call | solution.py:137
  47.3 1.8 %multiply_reduce_fusion = f32[8,512]{1,0:T(8,128)S(1)} fusion(bf16[8,512,64]{2,1,0:T(8,128)(2,1)} %get-tuple-element.7), kind=kLoop, calls=%fused_computation.9 | loop fusion | flops 782336 | bytes 540672 | tf_op jit(solution)/shard_map/reduce_sum | solution.py:262
  49.2 0.6 copy.22
  49.9 2.0 %copy.21 = f32[4096,1]{1,0:T(8,128)} copy(f32[4096,1]{0,1:T(1,128)S(1)} %bitcast.25) | data formatting | bytes 32768 | tf_op jit(solution)/shard_map/reduce_sum | solution.py:262
  51.9 3.4 %fusion.1 = (bf16[4096,1]{1,0:T(8,128)(2,1)}, bf16[4096,1]{1,0:T(8,128)(2,1)}) fusion(f32[4096,1]{1,0:T(8,128)} %copy.21, f32[4096,1]{1,0:T(8,128)S(1)} %copy.22), kind=kLoop, calls=%fused_computation.8 | loop fusion | flops 20480 | bytes 49152 | tf_op jit(solution)/shard_map/convert.2
  55.3 0.0 copy-start.2
  55.3 1.4 copy.23
  56.7 0.1 broadcast.18
  56.8 0.1 broadcast.19
  57.0 0.0 copy-done.2
  57.0 6.7 %concatenate.9.pts_ref = bf16[4096,128]{1,0:T(8,128)(2,1)} concatenate(bf16[4096,64]{1,0:T(8,128)(2,1)S(1)} %bitcast.22, bf16[4096,1]{1,0:T(8,128)(2,1)} %copy.23, bf16[4096,1]{1,0:T(8,128)(2,1)} %get-tuple-element.12, bf16[4096,1]{1,0:T(8,128)(2,1)} %get-tuple-element.11, bf16[4096,3]{1,0:T(8,128)(2,1)S(1)} %broadcast.18, bf16[4096,58]{1,0:T(8,128)(2,1)S(1)} %broadcast.19), dimensions={1} | concatenate | bytes 2097152 | tf_op jit(solution)/shard_map/concatenate | solution.py:267
  63.7 1.8 %multiply_reduce_fusion.1 = f32[8,8,64]{2,1,0:T(8,128)S(1)} fusion(bf16[8,8,64,64]{3,2,1,0:T(8,128)(2,1)} %get-tuple-element.6), kind=kLoop, calls=%fused_computation.10 | loop fusion | flops 782336 | bytes 540672 | tf_op jit(solution)/shard_map/reduce_sum | solution.py:261
  65.5 0.1 reduce_sum.23
  65.7 2.0 %copy.19 = f32[4096,1]{1,0:T(8,128)} copy(f32[4096,1]{0,1:T(1,128)S(1)} %get-tuple-element.17) | data formatting | bytes 32768 | tf_op jit(solution)/shard_map/reduce_precision | solution.py:250
  67.6 2.0 %copy.18 = f32[4096,1]{1,0:T(8,128)} copy(f32[4096,1]{0,1:T(1,128)S(1)} %reduce_sum.23) | data formatting | bytes 32768 | tf_op jit(solution)/shard_map/reduce_sum | solution.py:261
  69.6 3.9 %fusion = (bf16[4096,1]{1,0:T(8,128)(2,1)}, bf16[4096,1]{1,0:T(8,128)(2,1)}) fusion(f32[4096,1]{1,0:T(8,128)} %copy.18, f32[4096,1]{1,0:T(8,128)} %copy.19), kind=kLoop, calls=%fused_computation.7 | loop fusion | flops 20480 | bytes 49152 | tf_op jit(solution)/shard_map/convert.5
  73.6 0.5 copy.20
  74.1 2.3 %broadcast_multiply_fusion = bf16[8,8,64,64]{3,2,1,0:T(8,128)(2,1)} fusion(bf16[8,8,64,64]{3,2,1,0:T(8,128)(2,1)} %get-tuple-element.6), kind=kLoop, calls=%fused_computation.11 | loop fusion | flops 262144 | bytes 1048576 | tf_op jit(solution)/shard_map/mul | solution.py:265
  76.4 6.8 %concatenate.8.rows_ref = bf16[4096,128]{1,0:T(8,128)(2,1)} concatenate(bf16[4096,64]{1,0:T(8,128)(2,1)} %bitcast.23, bf16[4096,3]{1,0:T(8,128)(2,1)S(1)} %broadcast.18, bf16[4096,1]{1,0:T(8,128)(2,1)S(1)} %copy.20, bf16[4096,1]{1,0:T(8,128)(2,1)} %get-tuple-element.14, bf16[4096,1]{1,0:T(8,128)(2,1)} %get-tuple-element.13, bf16[4096,58]{1,0:T(8,128)(2,1)S(1)} %broadcast.19), dimensions={1} | concatenate | bytes 2097152 | tf_op jit(solution)/shard_map/concatenate | solution.py:264
  83.1 46.9 %shard_map.78 = f32[4096,1]{1,0:T(8,128)} custom-call(bf16[4096,128]{1,0:T(8,128)(2,1)} %concatenate.8.rows_ref, bf16[4096,128]{1,0:T(8,128)(2,1)} %concatenate.9.pts_ref, f32[1,4096]{1,0:T(1,128)} %bitcast.28), custom_call_target="tpu_custom_call" | custom-call | flops 4462739456 | bytes 2129920 | tf_op jit(solution)/shard_map/pallas_call | solution.py:272
  130.0 0.0 copy-start.1
  130.0 0.0 copy-start.6
  130.0 0.0 copy-start.4
  130.0 0.0 copy-start.5
  130.1 2.2 %reduce.2 = f32[4096]{0:T(1024)S(1)} reduce(f32[4096,1]{1,0:T(8,128)} %shard_map.78, f32[]{:T(128)} %constant.40), dimensions={1}, to_apply=%pallas_call.16.reduce_sub_computation | reduce | bytes 32772 | tf_op jit(solution)/shard_map/pallas_call | solution.py:272
  132.3 0.7 reshape_reshape.3.part
  133.0 23.8 %shard_map.79 = f32[1,64]{1,0:T(1,128)} custom-call(f32[8,8,64]{2,1,0:T(8,128)} %reshape_reshape.3.part), custom_call_target="tpu_custom_call" | custom-call | tf_op jit(solution)/shard_map/pallas_call | solution.py:210
  156.8 0.0 copy-done.1
  156.8 0.8 gather_fusion.1
  157.6 0.0 copy-done
  157.6 0.8 gather_fusion.2
  159.0 0.0 copy-done.6
  159.0 0.8 fusion.2
  159.9 0.0 copy-done.4
  159.9 0.0 copy-done.5
  159.9 0.6 fusion.17
  (4 shorter events, 0.1 us)
Async XLA Ops:
  0.6 156.9 %copy-start = (f32[512]{0:T(512)S(1)}, f32[512]{0:T(512)}, u32[]{:S(2)}) copy-start(f32[512]{0:T(512)} %param.11) | copy-start | bytes 6148
  2.3 3.3 %copy-start.3 = (bf16[512,64]{1,0:T(8,128)(2,1)}, bf16[512,64]{1,0:T(8,128)(2,1)S(1)}, u32[]{:S(2)}) copy-start(bf16[512,64]{1,0:T(8,128)(2,1)S(1)} %copy.16.pts) | copy-start | bytes 196612
  55.3 1.7 %copy-start.2 = (bf16[8,512,64]{2,1,0:T(8,128)(2,1)S(1)}, bf16[8,512,64]{2,1,0:T(8,128)(2,1)}, u32[]{:S(2)}) copy-start(bf16[8,512,64]{2,1,0:T(8,128)(2,1)} %get-tuple-element.7) | copy-start | bytes 1572868
  130.0 26.7 %copy-start.1 = (f32[512]{0:T(512)S(1)}, f32[512]{0:T(512)}, u32[]{:S(2)}) copy-start(f32[512]{0:T(512)} %multiply_add_fusion) | copy-start | bytes 6148
  130.0 29.0 %copy-start.6 = (s32[64]{0:T(128)S(1)}, s32[64]{0:T(128)}, u32[]{:S(2)}) copy-start(s32[64]{0:T(128)} %param.12) | copy-start | bytes 772
  130.0 29.8 %copy-start.4 = (f32[512]{0:T(512)S(1)}, f32[512]{0:T(512)}, u32[]{:S(2)}) copy-start(f32[512]{0:T(512)} %param.9) | copy-start | bytes 6148
  130.0 29.8 %copy-start.5 = (f32[512]{0:T(512)S(1)}, f32[512]{0:T(512)}, u32[]{:S(2)}) copy-start(f32[512]{0:T(512)} %param.10) | copy-start | bytes 6148

commit v8 on v4

--- a/solution.py
+++ b/solution.py
@@ -260,7 +260,10 @@
     in_count = slot_ids < count_here[0]
     picked = jnp.take(points, batch_rows, axis=0)
     g = 8
-    rows_all, pts_all, prev_all = gather_all(picked, points, preview.reshape(1, -1), g)
+    lanes = 128
+    dense = lambda a: a.reshape(-1, lanes)
+    rows_all, pts_all, prev_all = gather_all(
+        dense(picked), dense(points), preview.reshape(1, -1), g)
     group_rows = rows_all.reshape(-1, points.shape[1])
     piece_points = pts_all.reshape(-1, points.shape[1])
     every_coef = prev_all.reshape(-1)

time: 125 us -> 116 us (0.928)
  Pallas kernels: 65.2 us -> 52.7 us
  local copies, waits for them, and re-layouts: 4.08 us -> 7.53 us
    pallas_call x1, Pallas kernels: 41.7 us -> 33.1 us  [gather_all(): pl.pallas_call(functools.partial(gather_kernel, g), out_shape=(jax.ShapeD...]
    pallas_call x1, Pallas kernels: 23.5 us -> 19.5 us  [scatter_all(): pl.pallas_call(functools.partial(scatter_kernel, g), out_shape=jax.ShapeD...]
    reshape x0 -> x2, local copies, waits for them, and re-layouts: none -> 2.45 us  [the longest x1 1.71 us: per_device(): group_rows = rows_all.reshape(-1, points.shape[1])]
where the time goes in v8:
time: 116 us
  Pallas kernels  52.7 us (45%)
  matrix products  48.2 us (42%)
  local copies, waits for them, and re-layouts  7.53 us (6%)
  other arithmetic  5.69 us (5%)
  between operations  1.45 us (1%)
    dot_general x8, matrix products, matern_sums(): lax.dot_general(row_feats, col_points, (((1,), (1,)), ((), ())), preferre...  48 us
    pallas_call x1, Pallas kernels, gather_all(): pl.pallas_call(functools.partial(gather_kernel, g), out_shape=(jax.ShapeD...  33.1 us
    pallas_call x1, Pallas kernels, scatter_all(): pl.pallas_call(functools.partial(scatter_kernel, g), out_shape=jax.ShapeD...  19.5 us

profile of v8, /device:TPU:8, one launch (start us, length us, event | category | flops | bytes accessed | tf_op | source)
XLA Modules:
  0.0 115.9 jit_solution(16614062769719964802)
XLA Ops:
  0.6 0.0 copy-start
  0.6 0.7 compare_select_fusion
  1.3 1.0 copy.10
  2.3 0.6 gather_fusion
  2.9 0.1 gather.10
  3.0 0.7 compare_and_fusion
  3.7 0.1 broadcast_in_dim.35
  3.8 0.1 broadcast_in_dim.36
  3.9 0.1 broadcast_in_dim.37
  4.0 0.6 broadcast_select_fusion.picked
  4.6 0.7 reshape.37.pts
  5.3 1.3 %multiply_add_fusion = f32[512]{0:T(512)} fusion(f32[512]{0:T(512)} %param.11, f32[512]{0:T(512)} %param.12), kind=kLoop, calls=%fused_computation.25 | loop fusion | flops 1024 | bytes 6144 | tf_op jit(solution)/shard_map/add | solution.py:255
  6.6 33.1 %shard_map.77 = (bf16[8,8,32,128]{3,2,1,0:T(8,128)(2,1)}, bf16[8,256,128]{2,1,0:T(8,128)(2,1)}, f32[8,1,512]{2,1,0:T(1,128)}) custom-call(bf16[32,128]{1,0:T(8,128)(2,1)} %broadcast_select_fusion.picked, bf16[256,128]{1,0:T(8,128)(2,1)} %reshape.37.pts, f32[1,512]{1,0:T(1,128)} %bitcast.45), custom_call_target="tpu_custom_call" | custom-call | tf_op jit(solution)/shard_map/pallas_call | solution.py:137
  39.8 0.0 copy-start.2
  39.8 1.7 %reshape.39 = bf16[4096,64]{1,0:T(8,128)(2,1)S(1)} reshape(bf16[8,8,32,128]{3,2,1,0:T(8,128)(2,1)} %get-tuple-element.38) | data formatting | bytes 1048576 | tf_op jit(solution)/shard_map/reshape | solution.py:267
  41.5 0.6 multiply_reduce_fusion.2
  42.1 0.0 copy-start.3
  42.1 0.0 copy-done.2
  42.1 0.4 reshape_reshape.6
  42.5 0.3 copy-done.3
  42.8 49.7 %while.11 = (s32[]{:T(128)}, f32[4096]{0:T(1024)S(1)}, f32[4096]{0:T(1024)S(1)}, bf16[8,512,64]{2,1,0:T(8,128)(2,1)S(1)}, bf16[4096,64]{1,0:T(8,128)(2,1)S(1)}, /*index=5*/f32[8,512]{1,0:T(8,128)S(1)}, s32[]{:T(128)}, s32[]{:T(128)}) while((s32[]{:T(128)}, f32[4096]{0:T(1024)S(1)}, f32[4096]{0:T(1024)S(1)}, ...), condition=%wide.region_4.5_spmd.clone, body=%wide.region_1.0_spmd.clone.sunk | while | flops 289508864 | bytes 1337451 | solution.py:250
  42.8 0.1 multiply_reduce_fusion.5
  43.0 6.0 %multiply_reduce_fusion.6 = f32[4096]{0:T(1024)S(1)} fusion(bf16[4096,64]{1,0:T(8,128)(2,1)S(1)} %get-tuple-element.134, f32[512]{0:T(512)S(1)} %bitcast.46, f32[512]{0:T(512)S(1)} %multiply_reduce_fusion.5, f32[4096]{0:T(1024)S(1)} %get-tuple-element.132, bf16[8,512,64]{2,1,0:T(8,128)(2,1)S(1)} %get-tuple-element.133, s32[]{:T(128)} %get-tuple-element.122), kind=kOutput, calls=%fused_computation.7.clone.1 | convolution fusion | flops 289402880 | bytes 1216516 | tf_op jit(solution)/shard_map/while/body/eval_jaxpr/dot_general | solution.py:227
  49.0 0.2 multiply_reduce_fusion.5
  49.2 6.0 %multiply_reduce_fusion.6 = f32[4096]{0:T(1024)S(1)} fusion(bf16[4096,64]{1,0:T(8,128)(2,1)S(1)} %get-tuple-element.134, f32[512]{0:T(512)S(1)} %bitcast.46, f32[512]{0:T(512)S(1)} %multiply_reduce_fusion.5, f32[4096]{0:T(1024)S(1)} %get-tuple-element.132, bf16[8,512,64]{2,1,0:T(8,128)(2,1)S(1)} %get-tuple-element.133, s32[]{:T(128)} %get-tuple-element.122), kind=kOutput, calls=%fused_computation.7.clone.1 | convolution fusion | flops 289402880 | bytes 1216516 | tf_op jit(solution)/shard_map/while/body/eval_jaxpr/dot_general | solution.py:227
  55.3 0.2 multiply_reduce_fusion.5
  55.4 6.0 %multiply_reduce_fusion.6 = f32[4096]{0:T(1024)S(1)} fusion(bf16[4096,64]{1,0:T(8,128)(2,1)S(1)} %get-tuple-element.134, f32[512]{0:T(512)S(1)} %bitcast.46, f32[512]{0:T(512)S(1)} %multiply_reduce_fusion.5, f32[4096]{0:T(1024)S(1)} %get-tuple-element.132, bf16[8,512,64]{2,1,0:T(8,128)(2,1)S(1)} %get-tuple-element.133, s32[]{:T(128)} %get-tuple-element.122), kind=kOutput, calls=%fused_computation.7.clone.1 | convolution fusion | flops 289402880 | bytes 1216516 | tf_op jit(solution)/shard_map/while/body/eval_jaxpr/dot_general | solution.py:227
  61.5 0.2 multiply_reduce_fusion.5
  61.6 6.0 %multiply_reduce_fusion.6 = f32[4096]{0:T(1024)S(1)} fusion(bf16[4096,64]{1,0:T(8,128)(2,1)S(1)} %get-tuple-element.134, f32[512]{0:T(512)S(1)} %bitcast.46, f32[512]{0:T(512)S(1)} %multiply_reduce_fusion.5, f32[4096]{0:T(1024)S(1)} %get-tuple-element.132, bf16[8,512,64]{2,1,0:T(8,128)(2,1)S(1)} %get-tuple-element.133, s32[]{:T(128)} %get-tuple-element.122), kind=kOutput, calls=%fused_computation.7.clone.1 | convolution fusion | flops 289402880 | bytes 1216516 | tf_op jit(solution)/shard_map/while/body/eval_jaxpr/dot_general | solution.py:227
  67.7 0.2 multiply_reduce_fusion.5
  67.9 6.0 %multiply_reduce_fusion.6 = f32[4096]{0:T(1024)S(1)} fusion(bf16[4096,64]{1,0:T(8,128)(2,1)S(1)} %get-tuple-element.134, f32[512]{0:T(512)S(1)} %bitcast.46, f32[512]{0:T(512)S(1)} %multiply_reduce_fusion.5, f32[4096]{0:T(1024)S(1)} %get-tuple-element.132, bf16[8,512,64]{2,1,0:T(8,128)(2,1)S(1)} %get-tuple-element.133, s32[]{:T(128)} %get-tuple-element.122), kind=kOutput, calls=%fused_computation.7.clone.1 | convolution fusion | flops 289402880 | bytes 1216516 | tf_op jit(solution)/shard_map/while/body/eval_jaxpr/dot_general | solution.py:227
  73.9 0.2 multiply_reduce_fusion.5
  74.1 6.0 %multiply_reduce_fusion.6 = f32[4096]{0:T(1024)S(1)} fusion(bf16[4096,64]{1,0:T(8,128)(2,1)S(1)} %get-tuple-element.134, f32[512]{0:T(512)S(1)} %bitcast.46, f32[512]{0:T(512)S(1)} %multiply_reduce_fusion.5, f32[4096]{0:T(1024)S(1)} %get-tuple-element.132, bf16[8,512,64]{2,1,0:T(8,128)(2,1)S(1)} %get-tuple-element.133, s32[]{:T(128)} %get-tuple-element.122), kind=kOutput, calls=%fused_computation.7.clone.1 | convolution fusion | flops 289402880 | bytes 1216516 | tf_op jit(solution)/shard_map/while/body/eval_jaxpr/dot_general | solution.py:227
  80.1 0.2 multiply_reduce_fusion.5
  80.3 6.0 %multiply_reduce_fusion.6 = f32[4096]{0:T(1024)S(1)} fusion(bf16[4096,64]{1,0:T(8,128)(2,1)S(1)} %get-tuple-element.134, f32[512]{0:T(512)S(1)} %bitcast.46, f32[512]{0:T(512)S(1)} %multiply_reduce_fusion.5, f32[4096]{0:T(1024)S(1)} %get-tuple-element.132, bf16[8,512,64]{2,1,0:T(8,128)(2,1)S(1)} %get-tuple-element.133, s32[]{:T(128)} %get-tuple-element.122), kind=kOutput, calls=%fused_computation.7.clone.1 | convolution fusion | flops 289402880 | bytes 1216516 | tf_op jit(solution)/shard_map/while/body/eval_jaxpr/dot_general | solution.py:227
  86.3 0.2 multiply_reduce_fusion.5
  86.5 6.0 %multiply_reduce_fusion.6 = f32[4096]{0:T(1024)S(1)} fusion(bf16[4096,64]{1,0:T(8,128)(2,1)S(1)} %get-tuple-element.134, f32[512]{0:T(512)S(1)} %bitcast.46, f32[512]{0:T(512)S(1)} %multiply_reduce_fusion.5, f32[4096]{0:T(1024)S(1)} %get-tuple-element.132, bf16[8,512,64]{2,1,0:T(8,128)(2,1)S(1)} %get-tuple-element.133, s32[]{:T(128)} %get-tuple-element.122), kind=kOutput, calls=%fused_computation.7.clone.1 | convolution fusion | flops 289402880 | bytes 1216516 | tf_op jit(solution)/shard_map/while/body/eval_jaxpr/dot_general | solution.py:227
  92.5 0.0 copy-start.7
  92.6 0.0 copy-start.4
  92.6 0.0 copy-start.5
  92.6 0.7 reshape.40.part
  93.3 19.5 %shard_map.78 = f32[1,64]{1,0:T(1,128)} custom-call(f32[8,8,64]{2,1,0:T(8,128)} %reshape.40.part), custom_call_target="tpu_custom_call" | custom-call | tf_op jit(solution)/shard_map/pallas_call | solution.py:210
  112.8 0.0 copy-done.1
  112.8 0.8 gather_fusion.1
  113.6 0.8 gather_fusion.2
  115.1 0.2 fusion.6
  115.3 0.0 copy-done.5
  115.3 0.6 fusion.21
  (25 shorter events, 0.2 us)
Async XLA Ops:
  0.6 113.0 %copy-start = (f32[512]{0:T(512)S(1)}, f32[512]{0:T(512)}, u32[]{:S(2)}) copy-start(f32[512]{0:T(512)} %param.13) | copy-start | bytes 6148
  39.8 2.4 %copy-start.2 = (bf16[8,256,128]{2,1,0:T(8,128)(2,1)S(1)}, bf16[8,256,128]{2,1,0:T(8,128)(2,1)}, u32[]{:S(2)}) copy-start(bf16[8,256,128]{2,1,0:T(8,128)(2,1)} %get-tuple-element.39) | copy-start | bytes 1572868
  42.1 0.7 copy-start.3
  42.8 70.0 %copy-start.1 = (f32[512]{0:T(512)S(1)}, f32[512]{0:T(512)}, u32[]{:S(2)}) copy-start(f32[512]{0:T(512)} %multiply_add_fusion) | copy-start | bytes 6148
  92.5 22.5 %copy-start.7 = (s32[64]{0:T(128)S(1)}, s32[64]{0:T(128)}, u32[]{:S(2)}) copy-start(s32[64]{0:T(128)} %param.14) | copy-start | bytes 772
  92.6 22.8 %copy-start.4 = (f32[512]{0:T(512)S(1)}, f32[512]{0:T(512)}, u32[]{:S(2)}) copy-start(f32[512]{0:T(512)} %param.11) | copy-start | bytes 6148
  92.6 22.7 %copy-start.5 = (f32[512]{0:T(512)S(1)}, f32[512]{0:T(512)}, u32[]{:S(2)}) copy-start(f32[512]{0:T(512)} %param.12) | copy-start | bytes 6148
  112.8 2.3 %copy-start.6 = (f32[1,64]{1,0:T(1,128)S(1)}, f32[1,64]{1,0:T(1,128)}, u32[]{:S(2)}) copy-start(f32[1,64]{1,0:T(1,128)} %shard_map.78) | copy-start | bytes 772

commit v9 on v8

--- a/solution.py
+++ b/solution.py
@@ -222,19 +222,21 @@
     )(part)
 
 
-def matern_sums(row_feats, row_sq, col_points, col_coef):
+def matern_sums(neg_two_rows, row_sq, col_points, col_coef):
     col_sq = jnp.sum(jnp.square(col_points.astype(jnp.float32)), axis=1)
-    inner_prod = lax.dot_general(
-        row_feats, col_points, (((1,), (1,)), ((), ())), preferred_element_type=jnp.float32
-    )
-    distance = jnp.sqrt(jnp.maximum(row_sq[:, None] + col_sq[None, :] - 2.0 * inner_prod, 0.0))
-    scaled = KERNEL_RATE * distance
-    kernel_tile = (1.0 + scaled) * jnp.exp(-scaled)
+    neg_two_dot = lax.dot_general(
+        neg_two_rows, col_points, (((1,), (1,)), ((), ())), preferred_element_type=jnp.float32
+    )
+    sq = (row_sq[:, None] + col_sq[None, :]) + neg_two_dot
+    distance = jnp.where(sq > 0.0, sq * lax.rsqrt(sq), 0.0)
+    m = distance * (-KERNEL_RATE)
+    kernel_tile = (1.0 - m) * jnp.exp(m)
     return jnp.sum(kernel_tile * col_coef[None, :], axis=1)
 
 
 def column_sums(row_feats, piece_points, every_coef):
     row_sq = jnp.sum(jnp.square(row_feats.astype(jnp.float32)), axis=1)
+    neg_two_rows = row_feats * jnp.asarray(-2.0, row_feats.dtype)
     zeros_init = jnp.zeros((row_feats.shape[0],), jnp.float32)
     piece_len = piece_points.shape[0]
     block_len = math.gcd(piece_len, 512)
@@ -243,7 +245,7 @@
 
     def advance(partial_sum, column_block):
         return (
-            partial_sum + matern_sums(row_feats, row_sq, column_block[0], column_block[1]),
+            partial_sum + matern_sums(neg_two_rows, row_sq, column_block[0], column_block[1]),
             None,
         )
 

time: 116 us -> 105 us (0.905)
  matrix products: 48.2 us -> 36.2 us
  other arithmetic: 5.69 us -> 6.89 us
    dot_general x8, matrix products: 48 us -> 35.3 us  [matern_sums(): lax.dot_general(neg_two_rows, col_points, (((1,), (1,)), ((), ())), prefe...]
    reshape x1 -> x0, local copies, waits for them, and re-layouts: 1.71 us -> none  [per_device(): group_rows = rows_all.reshape(-1, points.shape[1])]
    square x0 -> x1, other arithmetic: none -> 1.17 us  [column_sums(): row_sq = jnp.sum(jnp.square(row_feats.astype(jnp.float32)), axis=1)]
where the time goes in v9:
time: 105 us; the launch traced here: 104 us
  Pallas kernels  52.7 us (50%)
  matrix products  36.2 us (34%)
  other arithmetic  6.89 us (7%)
  local copies, waits for them, and re-layouts  6.69 us (6%)
  between operations  1.48 us (1%)
    dot_general x8, matrix products, matern_sums(): lax.dot_general(neg_two_rows, col_points, (((1,), (1,)), ((), ())), prefe...  35.3 us
    pallas_call x1, Pallas kernels, gather_all(): pl.pallas_call(functools.partial(gather_kernel, g), out_shape=(jax.ShapeD...  33.1 us
    pallas_call x1, Pallas kernels, scatter_all(): pl.pallas_call(functools.partial(scatter_kernel, g), out_shape=jax.ShapeD...  19.5 us

profile of v9, /device:TPU:8, one launch (start us, length us, event | category | flops | bytes accessed | tf_op | source)
XLA Modules:
  0.0 104.3 jit_solution(17683599109109759316)
XLA Ops:
  0.6 0.0 copy-start
  0.6 0.7 compare_select_fusion
  1.3 1.0 copy.10
  2.3 0.6 gather_fusion
  2.9 0.1 gather.10
  3.0 0.7 compare_and_fusion
  3.7 0.1 broadcast_in_dim.37
  3.8 0.1 broadcast_in_dim.38
  3.9 0.1 broadcast_in_dim.39
  4.0 0.6 broadcast_select_fusion.picked
  4.6 0.7 reshape.39.pts
  5.3 1.3 %multiply_add_fusion = f32[512]{0:T(512)} fusion(f32[512]{0:T(512)} %param.11, f32[512]{0:T(512)} %param.12), kind=kLoop, calls=%fused_computation.26 | loop fusion | flops 1024 | bytes 6144 | tf_op jit(solution)/shard_map/add | solution.py:257
  6.6 33.1 %shard_map.77 = (bf16[8,8,32,128]{3,2,1,0:T(8,128)(2,1)}, bf16[8,256,128]{2,1,0:T(8,128)(2,1)}, f32[8,1,512]{2,1,0:T(1,128)}) custom-call(bf16[32,128]{1,0:T(8,128)(2,1)} %broadcast_select_fusion.picked, bf16[256,128]{1,0:T(8,128)(2,1)} %reshape.39.pts, f32[1,512]{1,0:T(1,128)} %bitcast.41), custom_call_target="tpu_custom_call" | custom-call | tf_op jit(solution)/shard_map/pallas_call | solution.py:137
  39.8 1.2 %convert_multiply_fusion = f32[8,8,32,128]{3,2,1,0:T(8,128)S(1)} fusion(bf16[8,8,32,128]{3,2,1,0:T(8,128)(2,1)} %get-tuple-element.38), kind=kLoop, calls=%fused_computation.14 | loop fusion | flops 524288 | bytes 1572864 | tf_op jit(solution)/shard_map/square | solution.py:238
  40.9 0.3 square.10
  41.3 0.0 copy-start.2
  41.3 0.0 copy-start.3
  41.3 0.6 reduce_sum.27
  41.9 0.4 copy-done.2
  42.4 0.4 mul.41
  42.8 0.4 reshape_reshape.6
  43.2 0.0 copy-start.1
  43.2 0.0 copy-start.7
  43.3 0.0 copy-start.5
  43.3 0.0 copy-start.6
  43.3 37.0 %while.11 = (s32[]{:T(128)}, f32[4096]{0:T(1024)S(1)}, f32[4096]{0:T(1024)S(1)}, bf16[8,512,64]{2,1,0:T(8,128)(2,1)S(1)}, bf16[4096,64]{1,0:T(8,128)(2,1)S(1)}, /*index=5*/f32[8,512]{1,0:T(8,128)S(1)}, s32[]{:T(128)}, s32[]{:T(128)}) while((s32[]{:T(128)}, f32[4096]{0:T(1024)S(1)}, f32[4096]{0:T(1024)S(1)}, ...), condition=%wide.region_4.5_spmd.clone, body=%wide.region_1.0_spmd.clone.sunk | while | flops 289508864 | bytes 1337451 | solution.py:252
  43.3 0.2 multiply_reduce_fusion.4
  43.5 4.4 %multiply_reduce_fusion.5 = f32[4096]{0:T(1024)S(1)} fusion(bf16[4096,64]{1,0:T(8,128)(2,1)S(1)} %get-tuple-element.134, f32[512]{0:T(512)S(1)} %bitcast.42, f32[512]{0:T(512)S(1)} %multiply_reduce_fusion.4, f32[4096]{0:T(1024)S(1)} %get-tuple-element.132, bf16[8,512,64]{2,1,0:T(8,128)(2,1)S(1)} %get-tuple-element.133, s32[]{:T(128)} %get-tuple-element.122), kind=kOutput, calls=%fused_computation.7.clone.1 | convolution fusion | flops 289402880 | bytes 1216516 | tf_op jit(solution)/shard_map/while/body/eval_jaxpr/dot_general | solution.py:227
  47.9 0.2 multiply_reduce_fusion.4
  48.1 4.4 %multiply_reduce_fusion.5 = f32[4096]{0:T(1024)S(1)} fusion(bf16[4096,64]{1,0:T(8,128)(2,1)S(1)} %get-tuple-element.134, f32[512]{0:T(512)S(1)} %bitcast.42, f32[512]{0:T(512)S(1)} %multiply_reduce_fusion.4, f32[4096]{0:T(1024)S(1)} %get-tuple-element.132, bf16[8,512,64]{2,1,0:T(8,128)(2,1)S(1)} %get-tuple-element.133, s32[]{:T(128)} %get-tuple-element.122), kind=kOutput, calls=%fused_computation.7.clone.1 | convolution fusion | flops 289402880 | bytes 1216516 | tf_op jit(solution)/shard_map/while/body/eval_jaxpr/dot_general | solution.py:227
  52.6 0.2 multiply_reduce_fusion.4
  52.7 4.4 %multiply_reduce_fusion.5 = f32[4096]{0:T(1024)S(1)} fusion(bf16[4096,64]{1,0:T(8,128)(2,1)S(1)} %get-tuple-element.134, f32[512]{0:T(512)S(1)} %bitcast.42, f32[512]{0:T(512)S(1)} %multiply_reduce_fusion.4, f32[4096]{0:T(1024)S(1)} %get-tuple-element.132, bf16[8,512,64]{2,1,0:T(8,128)(2,1)S(1)} %get-tuple-element.133, s32[]{:T(128)} %get-tuple-element.122), kind=kOutput, calls=%fused_computation.7.clone.1 | convolution fusion | flops 289402880 | bytes 1216516 | tf_op jit(solution)/shard_map/while/body/eval_jaxpr/dot_general | solution.py:227
  57.2 0.2 multiply_reduce_fusion.4
  57.4 4.4 %multiply_reduce_fusion.5 = f32[4096]{0:T(1024)S(1)} fusion(bf16[4096,64]{1,0:T(8,128)(2,1)S(1)} %get-tuple-element.134, f32[512]{0:T(512)S(1)} %bitcast.42, f32[512]{0:T(512)S(1)} %multiply_reduce_fusion.4, f32[4096]{0:T(1024)S(1)} %get-tuple-element.132, bf16[8,512,64]{2,1,0:T(8,128)(2,1)S(1)} %get-tuple-element.133, s32[]{:T(128)} %get-tuple-element.122), kind=kOutput, calls=%fused_computation.7.clone.1 | convolution fusion | flops 289402880 | bytes 1216516 | tf_op jit(solution)/shard_map/while/body/eval_jaxpr/dot_general | solution.py:227
  61.8 0.2 multiply_reduce_fusion.4
  62.0 4.4 %multiply_reduce_fusion.5 = f32[4096]{0:T(1024)S(1)} fusion(bf16[4096,64]{1,0:T(8,128)(2,1)S(1)} %get-tuple-element.134, f32[512]{0:T(512)S(1)} %bitcast.42, f32[512]{0:T(512)S(1)} %multiply_reduce_fusion.4, f32[4096]{0:T(1024)S(1)} %get-tuple-element.132, bf16[8,512,64]{2,1,0:T(8,128)(2,1)S(1)} %get-tuple-element.133, s32[]{:T(128)} %get-tuple-element.122), kind=kOutput, calls=%fused_computation.7.clone.1 | convolution fusion | flops 289402880 | bytes 1216516 | tf_op jit(solution)/shard_map/while/body/eval_jaxpr/dot_general | solution.py:227
  66.5 0.2 multiply_reduce_fusion.4
  66.6 4.4 %multiply_reduce_fusion.5 = f32[4096]{0:T(1024)S(1)} fusion(bf16[4096,64]{1,0:T(8,128)(2,1)S(1)} %get-tuple-element.134, f32[512]{0:T(512)S(1)} %bitcast.42, f32[512]{0:T(512)S(1)} %multiply_reduce_fusion.4, f32[4096]{0:T(1024)S(1)} %get-tuple-element.132, bf16[8,512,64]{2,1,0:T(8,128)(2,1)S(1)} %get-tuple-element.133, s32[]{:T(128)} %get-tuple-element.122), kind=kOutput, calls=%fused_computation.7.clone.1 | convolution fusion | flops 289402880 | bytes 1216516 | tf_op jit(solution)/shard_map/while/body/eval_jaxpr/dot_general | solution.py:227
  71.1 0.2 multiply_reduce_fusion.4
  71.3 4.4 %multiply_reduce_fusion.5 = f32[4096]{0:T(1024)S(1)} fusion(bf16[4096,64]{1,0:T(8,128)(2,1)S(1)} %get-tuple-element.134, f32[512]{0:T(512)S(1)} %bitcast.42, f32[512]{0:T(512)S(1)} %multiply_reduce_fusion.4, f32[4096]{0:T(1024)S(1)} %get-tuple-element.132, bf16[8,512,64]{2,1,0:T(8,128)(2,1)S(1)} %get-tuple-element.133, s32[]{:T(128)} %get-tuple-element.122), kind=kOutput, calls=%fused_computation.7.clone.1 | convolution fusion | flops 289402880 | bytes 1216516 | tf_op jit(solution)/shard_map/while/body/eval_jaxpr/dot_general | solution.py:227
  75.7 0.2 multiply_reduce_fusion.4
  75.9 4.4 %multiply_reduce_fusion.5 = f32[4096]{0:T(1024)S(1)} fusion(bf16[4096,64]{1,0:T(8,128)(2,1)S(1)} %get-tuple-element.134, f32[512]{0:T(512)S(1)} %bitcast.42, f32[512]{0:T(512)S(1)} %multiply_reduce_fusion.4, f32[4096]{0:T(1024)S(1)} %get-tuple-element.132, bf16[8,512,64]{2,1,0:T(8,128)(2,1)S(1)} %get-tuple-element.133, s32[]{:T(128)} %get-tuple-element.122), kind=kOutput, calls=%fused_computation.7.clone.1 | convolution fusion | flops 289402880 | bytes 1216516 | tf_op jit(solution)/shard_map/while/body/eval_jaxpr/dot_general | solution.py:227
  80.3 0.7 reshape.41.part
  81.0 19.5 %shard_map.78 = f32[1,64]{1,0:T(1,128)} custom-call(f32[8,8,64]{2,1,0:T(8,128)} %reshape.41.part), custom_call_target="tpu_custom_call" | custom-call | tf_op jit(solution)/shard_map/pallas_call | solution.py:210
  100.6 0.8 gather_fusion.1
  101.4 0.8 gather_fusion.2
  102.8 0.9 fusion.5
  103.7 0.6 fusion.20
  (28 shorter events, 0.2 us)
Async XLA Ops:
  0.6 100.7 %copy-start = (f32[512]{0:T(512)S(1)}, f32[512]{0:T(512)}, u32[]{:S(2)}) copy-start(f32[512]{0:T(512)} %param.13) | copy-start | bytes 6148
  41.3 1.0 %copy-start.2 = (bf16[8,8,32,128]{3,2,1,0:T(8,128)(2,1)S(1)}, bf16[8,8,32,128]{3,2,1,0:T(8,128)(2,1)}, u32[]{:S(2)}) copy-start(bf16[8,8,32,128]{3,2,1,0:T(8,128)(2,1)} %get-tuple-element.38) | copy-start | bytes 1572868
  41.3 1.5 %copy-start.3 = (bf16[8,256,128]{2,1,0:T(8,128)(2,1)S(1)}, bf16[8,256,128]{2,1,0:T(8,128)(2,1)}, u32[]{:S(2)}) copy-start(bf16[8,256,128]{2,1,0:T(8,128)(2,1)} %get-tuple-element.39) | copy-start | bytes 1572868
  42.3 0.9 copy-start.4
  43.2 57.3 %copy-start.1 = (f32[512]{0:T(512)S(1)}, f32[512]{0:T(512)}, u32[]{:S(2)}) copy-start(f32[512]{0:T(512)} %multiply_add_fusion) | copy-start | bytes 6148
  43.2 59.6 %copy-start.7 = (s32[64]{0:T(128)S(1)}, s32[64]{0:T(128)}, u32[]{:S(2)}) copy-start(s32[64]{0:T(128)} %param.14) | copy-start | bytes 772
  43.3 60.4 %copy-start.5 = (f32[512]{0:T(512)S(1)}, f32[512]{0:T(512)}, u32[]{:S(2)}) copy-start(f32[512]{0:T(512)} %param.11) | copy-start | bytes 6148
  43.3 60.4 %copy-start.6 = (f32[512]{0:T(512)S(1)}, f32[512]{0:T(512)}, u32[]{:S(2)}) copy-start(f32[512]{0:T(512)} %param.12) | copy-start | bytes 6148

commit v10 on v9

--- a/solution.py
+++ b/solution.py
@@ -98,7 +98,6 @@
         return carry
 
     lax.fori_loop(0, g - 1, start_inner, 0)
-    lax.fori_loop(0, g - 1, start_group, 0)
 
     def wait_inner(i, carry):
         inner_copy(i, w).wait_send()
@@ -113,6 +112,7 @@
         return carry
 
     lax.fori_loop(0, g - 1, start_outer, 0)
+    lax.fori_loop(0, g - 1, start_group, 0)
 
     def wait_group(i, carry):
         for cp in group_copies(i, c):

time: 105 us -> 107 us (1.019)
  Pallas kernels: 52.7 us -> 54.8 us
    pallas_call x1, Pallas kernels: 19.5 us -> 20.9 us  [scatter_all(): pl.pallas_call(functools.partial(scatter_kernel, g), out_shape=jax.ShapeD...]
where the time goes in v10:
time: 107 us; the launch traced here: 106 us
  Pallas kernels  54.8 us (51%)
  matrix products  36.2 us (34%)
  other arithmetic  6.89 us (6%)
  local copies, waits for them, and re-layouts  6.69 us (6%)
  between operations  1.48 us (1%)
    dot_general x8, matrix products, matern_sums(): lax.dot_general(neg_two_rows, col_points, (((1,), (1,)), ((), ())), prefe...  35.3 us
    pallas_call x1, Pallas kernels, gather_all(): pl.pallas_call(functools.partial(gather_kernel, g), out_shape=(jax.ShapeD...  33.9 us
    pallas_call x1, Pallas kernels, scatter_all(): pl.pallas_call(functools.partial(scatter_kernel, g), out_shape=jax.ShapeD...  20.9 us

profile of v10, /device:TPU:8, one launch (start us, length us, event | category | flops | bytes accessed | tf_op | source)
XLA Modules:
  0.0 106.5 jit_solution(16179273286894497962)
XLA Ops:
  0.6 0.0 copy-start
  0.6 0.7 compare_select_fusion
  1.3 1.0 copy.10
  2.3 0.6 gather_fusion
  2.9 0.1 gather.10
  3.0 0.7 compare_and_fusion
  3.7 0.1 broadcast_in_dim.37
  3.8 0.1 broadcast_in_dim.38
  3.9 0.1 broadcast_in_dim.39
  4.0 0.6 broadcast_select_fusion.picked
  4.6 0.7 reshape.39.pts
  5.3 1.3 %multiply_add_fusion = f32[512]{0:T(512)} fusion(f32[512]{0:T(512)} %param.11, f32[512]{0:T(512)} %param.12), kind=kLoop, calls=%fused_computation.26 | loop fusion | flops 1024 | bytes 6144 | tf_op jit(solution)/shard_map/add | solution.py:257
  6.6 33.9 %shard_map.77 = (bf16[8,8,32,128]{3,2,1,0:T(8,128)(2,1)}, bf16[8,256,128]{2,1,0:T(8,128)(2,1)}, f32[8,1,512]{2,1,0:T(1,128)}) custom-call(bf16[32,128]{1,0:T(8,128)(2,1)} %broadcast_select_fusion.picked, bf16[256,128]{1,0:T(8,128)(2,1)} %reshape.39.pts, f32[1,512]{1,0:T(1,128)} %bitcast.41), custom_call_target="tpu_custom_call" | custom-call | tf_op jit(solution)/shard_map/pallas_call | solution.py:137
  40.6 1.2 %convert_multiply_fusion = f32[8,8,32,128]{3,2,1,0:T(8,128)S(1)} fusion(bf16[8,8,32,128]{3,2,1,0:T(8,128)(2,1)} %get-tuple-element.38), kind=kLoop, calls=%fused_computation.14 | loop fusion | flops 524288 | bytes 1572864 | tf_op jit(solution)/shard_map/square | solution.py:238
  41.7 0.3 square.10
  42.1 0.0 copy-start.2
  42.1 0.6 reduce_sum.27
  42.7 0.4 copy-done.2
  43.2 0.4 mul.41
  43.6 0.4 reshape_reshape.6
  44.0 0.0 copy-start.1
  44.0 0.0 copy-start.7
  44.1 0.0 copy-start.5
  44.1 0.0 copy-start.6
  44.1 37.1 %while.11 = (s32[]{:T(128)}, f32[4096]{0:T(1024)S(1)}, f32[4096]{0:T(1024)S(1)}, bf16[8,512,64]{2,1,0:T(8,128)(2,1)S(1)}, bf16[4096,64]{1,0:T(8,128)(2,1)S(1)}, /*index=5*/f32[8,512]{1,0:T(8,128)S(1)}, s32[]{:T(128)}, s32[]{:T(128)}) while((s32[]{:T(128)}, f32[4096]{0:T(1024)S(1)}, f32[4096]{0:T(1024)S(1)}, ...), condition=%wide.region_4.5_spmd.clone, body=%wide.region_1.0_spmd.clone.sunk | while | flops 289508864 | bytes 1337451 | solution.py:252
  44.1 0.2 multiply_reduce_fusion.4
  44.3 4.4 %multiply_reduce_fusion.5 = f32[4096]{0:T(1024)S(1)} fusion(bf16[4096,64]{1,0:T(8,128)(2,1)S(1)} %get-tuple-element.134, f32[512]{0:T(512)S(1)} %bitcast.42, f32[512]{0:T(512)S(1)} %multiply_reduce_fusion.4, f32[4096]{0:T(1024)S(1)} %get-tuple-element.132, bf16[8,512,64]{2,1,0:T(8,128)(2,1)S(1)} %get-tuple-element.133, s32[]{:T(128)} %get-tuple-element.122), kind=kOutput, calls=%fused_computation.7.clone.1 | convolution fusion | flops 289402880 | bytes 1216516 | tf_op jit(solution)/shard_map/while/body/eval_jaxpr/dot_general | solution.py:227
  48.7 0.2 multiply_reduce_fusion.4
  48.9 4.4 %multiply_reduce_fusion.5 = f32[4096]{0:T(1024)S(1)} fusion(bf16[4096,64]{1,0:T(8,128)(2,1)S(1)} %get-tuple-element.134, f32[512]{0:T(512)S(1)} %bitcast.42, f32[512]{0:T(512)S(1)} %multiply_reduce_fusion.4, f32[4096]{0:T(1024)S(1)} %get-tuple-element.132, bf16[8,512,64]{2,1,0:T(8,128)(2,1)S(1)} %get-tuple-element.133, s32[]{:T(128)} %get-tuple-element.122), kind=kOutput, calls=%fused_computation.7.clone.1 | convolution fusion | flops 289402880 | bytes 1216516 | tf_op jit(solution)/shard_map/while/body/eval_jaxpr/dot_general | solution.py:227
  53.4 0.2 multiply_reduce_fusion.4
  53.5 4.4 %multiply_reduce_fusion.5 = f32[4096]{0:T(1024)S(1)} fusion(bf16[4096,64]{1,0:T(8,128)(2,1)S(1)} %get-tuple-element.134, f32[512]{0:T(512)S(1)} %bitcast.42, f32[512]{0:T(512)S(1)} %multiply_reduce_fusion.4, f32[4096]{0:T(1024)S(1)} %get-tuple-element.132, bf16[8,512,64]{2,1,0:T(8,128)(2,1)S(1)} %get-tuple-element.133, s32[]{:T(128)} %get-tuple-element.122), kind=kOutput, calls=%fused_computation.7.clone.1 | convolution fusion | flops 289402880 | bytes 1216516 | tf_op jit(solution)/shard_map/while/body/eval_jaxpr/dot_general | solution.py:227
  58.0 0.2 multiply_reduce_fusion.4
  58.2 4.4 %multiply_reduce_fusion.5 = f32[4096]{0:T(1024)S(1)} fusion(bf16[4096,64]{1,0:T(8,128)(2,1)S(1)} %get-tuple-element.134, f32[512]{0:T(512)S(1)} %bitcast.42, f32[512]{0:T(512)S(1)} %multiply_reduce_fusion.4, f32[4096]{0:T(1024)S(1)} %get-tuple-element.132, bf16[8,512,64]{2,1,0:T(8,128)(2,1)S(1)} %get-tuple-element.133, s32[]{:T(128)} %get-tuple-element.122), kind=kOutput, calls=%fused_computation.7.clone.1 | convolution fusion | flops 289402880 | bytes 1216516 | tf_op jit(solution)/shard_map/while/body/eval_jaxpr/dot_general | solution.py:227
  62.6 0.2 multiply_reduce_fusion.4
  62.8 4.4 %multiply_reduce_fusion.5 = f32[4096]{0:T(1024)S(1)} fusion(bf16[4096,64]{1,0:T(8,128)(2,1)S(1)} %get-tuple-element.134, f32[512]{0:T(512)S(1)} %bitcast.42, f32[512]{0:T(512)S(1)} %multiply_reduce_fusion.4, f32[4096]{0:T(1024)S(1)} %get-tuple-element.132, bf16[8,512,64]{2,1,0:T(8,128)(2,1)S(1)} %get-tuple-element.133, s32[]{:T(128)} %get-tuple-element.122), kind=kOutput, calls=%fused_computation.7.clone.1 | convolution fusion | flops 289402880 | bytes 1216516 | tf_op jit(solution)/shard_map/while/body/eval_jaxpr/dot_general | solution.py:227
  67.2 0.2 multiply_reduce_fusion.4
  67.4 4.4 %multiply_reduce_fusion.5 = f32[4096]{0:T(1024)S(1)} fusion(bf16[4096,64]{1,0:T(8,128)(2,1)S(1)} %get-tuple-element.134, f32[512]{0:T(512)S(1)} %bitcast.42, f32[512]{0:T(512)S(1)} %multiply_reduce_fusion.4, f32[4096]{0:T(1024)S(1)} %get-tuple-element.132, bf16[8,512,64]{2,1,0:T(8,128)(2,1)S(1)} %get-tuple-element.133, s32[]{:T(128)} %get-tuple-element.122), kind=kOutput, calls=%fused_computation.7.clone.1 | convolution fusion | flops 289402880 | bytes 1216516 | tf_op jit(solution)/shard_map/while/body/eval_jaxpr/dot_general | solution.py:227
  71.9 0.2 multiply_reduce_fusion.4
  72.1 4.4 %multiply_reduce_fusion.5 = f32[4096]{0:T(1024)S(1)} fusion(bf16[4096,64]{1,0:T(8,128)(2,1)S(1)} %get-tuple-element.134, f32[512]{0:T(512)S(1)} %bitcast.42, f32[512]{0:T(512)S(1)} %multiply_reduce_fusion.4, f32[4096]{0:T(1024)S(1)} %get-tuple-element.132, bf16[8,512,64]{2,1,0:T(8,128)(2,1)S(1)} %get-tuple-element.133, s32[]{:T(128)} %get-tuple-element.122), kind=kOutput, calls=%fused_computation.7.clone.1 | convolution fusion | flops 289402880 | bytes 1216516 | tf_op jit(solution)/shard_map/while/body/eval_jaxpr/dot_general | solution.py:227
  76.5 0.2 multiply_reduce_fusion.4
  76.7 4.4 %multiply_reduce_fusion.5 = f32[4096]{0:T(1024)S(1)} fusion(bf16[4096,64]{1,0:T(8,128)(2,1)S(1)} %get-tuple-element.134, f32[512]{0:T(512)S(1)} %bitcast.42, f32[512]{0:T(512)S(1)} %multiply_reduce_fusion.4, f32[4096]{0:T(1024)S(1)} %get-tuple-element.132, bf16[8,512,64]{2,1,0:T(8,128)(2,1)S(1)} %get-tuple-element.133, s32[]{:T(128)} %get-tuple-element.122), kind=kOutput, calls=%fused_computation.7.clone.1 | convolution fusion | flops 289402880 | bytes 1216516 | tf_op jit(solution)/shard_map/while/body/eval_jaxpr/dot_general | solution.py:227
  81.1 0.7 reshape.41.part
  81.8 20.9 %shard_map.78 = f32[1,64]{1,0:T(1,128)} custom-call(f32[8,8,64]{2,1,0:T(8,128)} %reshape.41.part), custom_call_target="tpu_custom_call" | custom-call | tf_op jit(solution)/shard_map/pallas_call | solution.py:210
  102.7 0.8 gather_fusion.1
  103.5 0.0 copy-done
  103.5 0.8 gather_fusion.2
  105.0 0.9 fusion.5
  105.9 0.6 fusion.20
  (28 shorter events, 0.2 us)
Async XLA Ops:
  0.6 102.9 %copy-start = (f32[512]{0:T(512)S(1)}, f32[512]{0:T(512)}, u32[]{:S(2)}) copy-start(f32[512]{0:T(512)} %param.13) | copy-start | bytes 6148
  42.1 1.0 copy-start.2
  42.1 1.5 %copy-start.3 = (bf16[8,256,128]{2,1,0:T(8,128)(2,1)S(1)}, bf16[8,256,128]{2,1,0:T(8,128)(2,1)}, u32[]{:S(2)}) copy-start(bf16[8,256,128]{2,1,0:T(8,128)(2,1)} %get-tuple-element.39) | copy-start | bytes 1572868
  43.1 0.9 copy-start.4
  44.0 58.7 %copy-start.1 = (f32[512]{0:T(512)S(1)}, f32[512]{0:T(512)}, u32[]{:S(2)}) copy-start(f32[512]{0:T(512)} %multiply_add_fusion) | copy-start | bytes 6148
  44.0 61.0 %copy-start.7 = (s32[64]{0:T(128)S(1)}, s32[64]{0:T(128)}, u32[]{:S(2)}) copy-start(s32[64]{0:T(128)} %param.14) | copy-start | bytes 772
  44.1 61.8 %copy-start.5 = (f32[512]{0:T(512)S(1)}, f32[512]{0:T(512)}, u32[]{:S(2)}) copy-start(f32[512]{0:T(512)} %param.11) | copy-start | bytes 6148
  44.1 61.8 %copy-start.6 = (f32[512]{0:T(512)S(1)}, f32[512]{0:T(512)}, u32[]{:S(2)}) copy-start(f32[512]{0:T(512)} %param.12) | copy-start | bytes 6148

commit v11 on v9

--- a/solution.py
+++ b/solution.py
@@ -239,7 +239,7 @@
     neg_two_rows = row_feats * jnp.asarray(-2.0, row_feats.dtype)
     zeros_init = jnp.zeros((row_feats.shape[0],), jnp.float32)
     piece_len = piece_points.shape[0]
-    block_len = math.gcd(piece_len, 512)
+    block_len = math.gcd(piece_len, 2048)
     point_blocks = piece_points.reshape(-1, block_len, piece_points.shape[1])
     coef_blocks = every_coef.reshape(-1, block_len)
 

time: 105 us -> 104 us (level)
    dot_general x8 -> x2, matrix products: 35.3 us -> 35.2 us  [matern_sums(): lax.dot_general(neg_two_rows, col_points, (((1,), (1,)), ((), ())), prefe...]
where the time goes in v11:
time: 104 us
  Pallas kernels  52.7 us (51%)
  matrix products  36.1 us (35%)
  local copies, waits for them, and re-layouts  6.89 us (7%)
  other arithmetic  6.37 us (6%)
  between operations  1.5 us (1%)
    dot_general x2, matrix products, matern_sums(): lax.dot_general(neg_two_rows, col_points, (((1,), (1,)), ((), ())), prefe...  35.2 us
    pallas_call x1, Pallas kernels, gather_all(): pl.pallas_call(functools.partial(gather_kernel, g), out_shape=(jax.ShapeD...  33.1 us
    pallas_call x1, Pallas kernels, scatter_all(): pl.pallas_call(functools.partial(scatter_kernel, g), out_shape=jax.ShapeD...  19.5 us

profile of v11, /device:TPU:8, one launch (start us, length us, event | category | flops | bytes accessed | tf_op | source)
XLA Modules:
  0.0 103.6 jit_solution(8408095928834301696)
XLA Ops:
  0.6 0.0 copy-start
  0.6 0.7 compare_select_fusion
  1.3 0.0 copy-start.7
  1.3 1.0 copy.10
  2.3 0.0 copy-done.7
  2.3 0.6 gather_fusion
  2.9 0.1 gather.10
  3.0 0.7 compare_and_fusion
  3.7 0.1 broadcast_in_dim.37
  3.8 0.1 broadcast_in_dim.38
  3.9 0.1 broadcast_in_dim.39
  4.0 0.6 broadcast_select_fusion.picked
  4.6 0.7 reshape.39.pts
  5.3 1.3 %multiply_add_fusion = f32[512]{0:T(512)} fusion(f32[512]{0:T(512)} %param.11, f32[512]{0:T(512)} %param.12), kind=kLoop, calls=%fused_computation.25 | loop fusion | flops 1024 | bytes 6144 | tf_op jit(solution)/shard_map/add | solution.py:257
  6.6 33.1 %shard_map.77 = (bf16[8,8,32,128]{3,2,1,0:T(8,128)(2,1)}, bf16[8,256,128]{2,1,0:T(8,128)(2,1)}, f32[8,1,512]{2,1,0:T(1,128)}) custom-call(bf16[32,128]{1,0:T(8,128)(2,1)} %broadcast_select_fusion.picked, bf16[256,128]{1,0:T(8,128)(2,1)} %reshape.39.pts, f32[1,512]{1,0:T(1,128)} %bitcast.38), custom_call_target="tpu_custom_call" | custom-call | tf_op jit(solution)/shard_map/pallas_call | solution.py:137
  39.8 1.2 %convert_multiply_fusion = f32[8,8,32,128]{3,2,1,0:T(8,128)S(1)} fusion(bf16[8,8,32,128]{3,2,1,0:T(8,128)(2,1)} %get-tuple-element.38), kind=kLoop, calls=%fused_computation.14 | loop fusion | flops 524288 | bytes 1572864 | tf_op jit(solution)/shard_map/square | solution.py:238
  40.9 0.3 square.10
  41.3 0.0 copy-start.2
  41.3 0.0 copy-start.3
  41.3 0.6 reduce_sum.27
  41.9 0.4 copy-done.2
  42.3 0.0 copy-start.4
  42.4 0.4 mul.41
  42.8 0.0 copy-done.3
  42.8 0.4 reshape_reshape.6
  43.2 0.0 copy-done.4
  43.3 0.0 copy-start.1
  43.3 0.0 copy-start.8
  43.3 0.0 copy-start.5
  43.3 0.0 copy-start.6
  43.3 36.0 %while.11 = (s32[]{:T(128)}, f32[4096]{0:T(1024)S(1)}, f32[4096]{0:T(1024)S(1)}, bf16[2,2048,64]{2,1,0:T(8,128)(2,1)S(1)}, bf16[4096,64]{1,0:T(8,128)(2,1)S(1)},...) while((s32[]{:T(128)}, f32[4096]{0:T(1024)S(1)}, f32[4096]{0:T(1024)S(1)}, ...), condition=%wide.region_4.5_spmd.clone, body=%wide.region_1.0_spmd.clone.sunk | while | flops 1158023168 | bytes 1957995 | solution.py:252
  43.4 0.3 multiply_reduce_fusion.4
  43.7 17.6 %multiply_reduce_fusion.5 = f32[4096]{0:T(1024)S(1)} fusion(bf16[4096,64]{1,0:T(8,128)(2,1)S(1)} %get-tuple-element.134, f32[2048]{0:T(1024)S(1)} %bitcast.39, f32[2048]{0:T(1024)S(1)} %multiply_reduce_fusion.4, f32[4096]{0:T(1024)S(1)} %get-tuple-element.132, bf16[2,2048,64]{2,1,0:T(8,128)(2,1)S(1)} %get-tuple-element.133, s32[]{:T(128)} %get-tuple-element.122), kind=kOutput, calls=%fused_computation.7.clone.1 | convolution fusion | flops 1157623808 | bytes 1622020 | tf_op jit(solution)/shard_map/while/body/eval_jaxpr/dot_general | solution.py:227
  61.4 0.3 multiply_reduce_fusion.4
  61.8 17.6 %multiply_reduce_fusion.5 = f32[4096]{0:T(1024)S(1)} fusion(bf16[4096,64]{1,0:T(8,128)(2,1)S(1)} %get-tuple-element.134, f32[2048]{0:T(1024)S(1)} %bitcast.39, f32[2048]{0:T(1024)S(1)} %multiply_reduce_fusion.4, f32[4096]{0:T(1024)S(1)} %get-tuple-element.132, bf16[2,2048,64]{2,1,0:T(8,128)(2,1)S(1)} %get-tuple-element.133, s32[]{:T(128)} %get-tuple-element.122), kind=kOutput, calls=%fused_computation.7.clone.1 | convolution fusion | flops 1157623808 | bytes 1622020 | tf_op jit(solution)/shard_map/while/body/eval_jaxpr/dot_general | solution.py:227
  79.4 0.7 reshape.41.part
  80.1 19.5 %shard_map.78 = f32[1,64]{1,0:T(1,128)} custom-call(f32[8,8,64]{2,1,0:T(8,128)} %reshape.41.part), custom_call_target="tpu_custom_call" | custom-call | tf_op jit(solution)/shard_map/pallas_call | solution.py:210
  99.6 0.0 copy-done.1
  99.6 0.9 gather_fusion.1
  100.5 0.0 copy-done
  100.5 0.9 gather_fusion.2
  102.1 0.0 copy-done.8
  102.1 0.9 fusion.5
  103.0 0.0 copy-done.5
  103.0 0.0 copy-done.6
  103.0 0.6 fusion.20
  (9 shorter events, 0.1 us)
Async XLA Ops:
  0.6 99.9 %copy-start = (f32[512]{0:T(512)S(1)}, f32[512]{0:T(512)}, u32[]{:S(2)}) copy-start(f32[512]{0:T(512)} %param.13) | copy-start | bytes 6148
  1.3 1.0 copy-start.7
  41.3 1.0 %copy-start.2 = (bf16[8,8,32,128]{3,2,1,0:T(8,128)(2,1)S(1)}, bf16[8,8,32,128]{3,2,1,0:T(8,128)(2,1)}, u32[]{:S(2)}) copy-start(bf16[8,8,32,128]{3,2,1,0:T(8,128)(2,1)} %get-tuple-element.38) | copy-start | bytes 1572868
  41.3 1.5 %copy-start.3 = (bf16[8,256,128]{2,1,0:T(8,128)(2,1)S(1)}, bf16[8,256,128]{2,1,0:T(8,128)(2,1)}, u32[]{:S(2)}) copy-start(bf16[8,256,128]{2,1,0:T(8,128)(2,1)} %get-tuple-element.39) | copy-start | bytes 1572868
  42.3 0.9 copy-start.4
  43.3 56.3 %copy-start.1 = (f32[512]{0:T(512)S(1)}, f32[512]{0:T(512)}, u32[]{:S(2)}) copy-start(f32[512]{0:T(512)} %multiply_add_fusion) | copy-start | bytes 6148
  43.3 58.8 %copy-start.8 = (s32[64]{0:T(128)S(1)}, s32[64]{0:T(128)}, u32[]{:S(2)}) copy-start(s32[64]{0:T(128)} %param.14) | copy-start | bytes 772
  43.3 59.7 %copy-start.5 = (f32[512]{0:T(512)S(1)}, f32[512]{0:T(512)}, u32[]{:S(2)}) copy-start(f32[512]{0:T(512)} %param.11) | copy-start | bytes 6148
  43.3 59.6 %copy-start.6 = (f32[512]{0:T(512)S(1)}, f32[512]{0:T(512)}, u32[]{:S(2)}) copy-start(f32[512]{0:T(512)} %param.12) | copy-start | bytes 6148

commit v12 on v11

--- a/solution.py
+++ b/solution.py
@@ -257,15 +257,16 @@
     preview = coefficients + MOMENTUM * velocity
     slot_total = batch_rows.shape[0]
     local_size = points.shape[0]
-    slot_ids = jnp.arange(slot_total, dtype=jnp.int32)
-    count_here = counts.reshape((1,))
-    in_count = slot_ids < count_here[0]
-    picked = jnp.take(points, batch_rows, axis=0)
+    picked = points.at[batch_rows].get(mode="promise_in_bounds")
     g = 8
     lanes = 128
     dense = lambda a: a.reshape(-1, lanes)
     rows_all, pts_all, prev_all = gather_all(
         dense(picked), dense(points), preview.reshape(1, -1), g)
+    rows_all, batch_rows, counts = lax.optimization_barrier((rows_all, batch_rows, counts))
+    slot_ids = jnp.arange(slot_total, dtype=jnp.int32)
+    count_here = counts.reshape((1,))
+    in_count = slot_ids < count_here[0]
     group_rows = rows_all.reshape(-1, points.shape[1])
     piece_points = pts_all.reshape(-1, points.shape[1])
     every_coef = prev_all.reshape(-1)
@@ -273,7 +274,7 @@
     kernel_rows = scatter_all(partial_value.reshape(g, g, slot_total), g).reshape(-1)
     residual = jnp.where(
         in_count,
-        kernel_rows + NOISE_VAR * jnp.take(preview, batch_rows) - jnp.take(targets, batch_rows),
+        kernel_rows + NOISE_VAR * preview.at[batch_rows].get(mode="promise_in_bounds") - targets.at[batch_rows].get(mode="promise_in_bounds"),
         0.0,
     )
     scatter_rows = (batch_rows[:, None] == jnp.arange(local_size, dtype=jnp.int32)[None, :]).astype(

time: 104 us -> 103 us (level)
  other arithmetic: 6.37 us -> 5.11 us
    gather x4 -> x3, local copies, waits for them, and re-layouts: 2.56 us -> 2.23 us  [the longest x1 0.8 us: per_device(): preview.at[batch_rows].get(mode='promise_in_bounds')]
where the time goes in v12:
time: 103 us; the launch traced here: 102 us
  Pallas kernels  52.7 us (51%)
  matrix products  36.1 us (35%)
  local copies, waits for them, and re-layouts  6.94 us (7%)
  other arithmetic  5.11 us (5%)
  between operations  1.49 us (1%)
    dot_general x2, matrix products, matern_sums(): lax.dot_general(neg_two_rows, col_points, (((1,), (1,)), ((), ())), prefe...  35.2 us
    pallas_call x1, Pallas kernels, gather_all(): pl.pallas_call(functools.partial(gather_kernel, g), out_shape=(jax.ShapeD...  33.1 us
    pallas_call x1, Pallas kernels, scatter_all(): pl.pallas_call(functools.partial(scatter_kernel, g), out_shape=jax.ShapeD...  19.5 us

profile of v12, /device:TPU:8, one launch (start us, length us, event | category | flops | bytes accessed | tf_op | source)
XLA Modules:
  0.0 102.4 jit_solution(3018002059076244763)
XLA Ops:
  0.6 0.0 copy-start
  0.6 1.0 copy.10
  1.6 0.7 reshape.28.pts
  2.4 0.7 compare_select_fusion.1
  3.0 0.6 gather_fusion
  3.7 0.7 reshape.27.picked
  4.3 1.3 %multiply_add_fusion = f32[512]{0:T(512)} fusion(f32[512]{0:T(512)} %param.9, f32[512]{0:T(512)} %param.10), kind=kLoop, calls=%fused_computation.25 | loop fusion | flops 1024 | bytes 6144 | tf_op jit(solution)/shard_map/add | solution.py:257
  5.6 33.1 %shard_map.77 = (bf16[8,8,32,128]{3,2,1,0:T(8,128)(2,1)}, bf16[8,256,128]{2,1,0:T(8,128)(2,1)}, f32[8,1,512]{2,1,0:T(1,128)}) custom-call(bf16[32,128]{1,0:T(8,128)(2,1)} %reshape.27.picked, bf16[256,128]{1,0:T(8,128)(2,1)} %reshape.28.pts, f32[1,512]{1,0:T(1,128)} %bitcast.38), custom_call_target="tpu_custom_call" | custom-call | tf_op jit(solution)/shard_map/pallas_call | solution.py:137
  38.8 1.2 %convert_multiply_fusion = f32[8,8,32,128]{3,2,1,0:T(8,128)S(1)} fusion(bf16[8,8,32,128]{3,2,1,0:T(8,128)(2,1)} %get-tuple-element.42), kind=kLoop, calls=%fused_computation.14 | loop fusion | flops 524288 | bytes 1572864 | tf_op jit(solution)/shard_map/square | solution.py:238
  39.9 0.3 square.10
  40.3 0.0 copy-start.2
  40.3 0.0 copy-start.3
  40.3 0.6 reduce_sum.27
  40.9 0.4 copy-done.2
  41.3 0.0 copy-start.4
  41.4 0.4 mul.41
  41.8 0.0 copy-done.3
  41.8 0.4 reshape_reshape.6
  42.2 0.0 copy-done.4
  42.3 0.0 copy-start.7
  42.3 0.0 copy-start.1
  42.3 0.0 copy-start.5
  42.3 0.0 copy-start.6
  42.3 36.1 %while.11 = (s32[]{:T(128)}, f32[4096]{0:T(1024)S(1)}, f32[4096]{0:T(1024)S(1)}, bf16[2,2048,64]{2,1,0:T(8,128)(2,1)S(1)}, bf16[4096,64]{1,0:T(8,128)(2,1)S(1)},...) while((s32[]{:T(128)}, f32[4096]{0:T(1024)S(1)}, f32[4096]{0:T(1024)S(1)}, ...), condition=%wide.region_4.5_spmd.clone, body=%wide.region_1.4_spmd.clone.sunk | while | flops 1158023168 | bytes 1957995 | solution.py:252
  42.4 0.3 multiply_reduce_fusion.4
  42.7 17.6 %multiply_reduce_fusion.5 = f32[4096]{0:T(1024)S(1)} fusion(bf16[4096,64]{1,0:T(8,128)(2,1)S(1)} %get-tuple-element.139, f32[2048]{0:T(1024)S(1)} %bitcast.39, f32[2048]{0:T(1024)S(1)} %multiply_reduce_fusion.4, f32[4096]{0:T(1024)S(1)} %get-tuple-element.137, bf16[2,2048,64]{2,1,0:T(8,128)(2,1)S(1)} %get-tuple-element.138, s32[]{:T(128)} %get-tuple-element.127), kind=kOutput, calls=%fused_computation.7.clone.1 | convolution fusion | flops 1157623808 | bytes 1622020 | tf_op jit(solution)/shard_map/while/body/eval_jaxpr/dot_general | solution.py:227
  60.4 0.3 multiply_reduce_fusion.4
  60.8 17.6 %multiply_reduce_fusion.5 = f32[4096]{0:T(1024)S(1)} fusion(bf16[4096,64]{1,0:T(8,128)(2,1)S(1)} %get-tuple-element.139, f32[2048]{0:T(1024)S(1)} %bitcast.39, f32[2048]{0:T(1024)S(1)} %multiply_reduce_fusion.4, f32[4096]{0:T(1024)S(1)} %get-tuple-element.137, bf16[2,2048,64]{2,1,0:T(8,128)(2,1)S(1)} %get-tuple-element.138, s32[]{:T(128)} %get-tuple-element.127), kind=kOutput, calls=%fused_computation.7.clone.1 | convolution fusion | flops 1157623808 | bytes 1622020 | tf_op jit(solution)/shard_map/while/body/eval_jaxpr/dot_general | solution.py:227
  78.4 0.7 reshape.30.part
  79.1 19.5 %shard_map.78 = f32[1,64]{1,0:T(1,128)} custom-call(f32[8,8,64]{2,1,0:T(8,128)} %reshape.30.part), custom_call_target="tpu_custom_call" | custom-call | tf_op jit(solution)/shard_map/pallas_call | solution.py:210
  98.6 0.0 copy-done.7
  98.6 0.0 copy-done.1
  98.7 0.8 gather_fusion.1
  99.5 0.0 copy-done
  99.5 0.8 gather_fusion.2
  100.9 0.9 fusion.5
  101.8 0.0 copy-done.5
  101.8 0.0 copy-done.6
  101.8 0.6 fusion.18
  (11 shorter events, 0.2 us)
Async XLA Ops:
  0.6 98.8 %copy-start = (f32[512]{0:T(512)S(1)}, f32[512]{0:T(512)}, u32[]{:S(2)}) copy-start(f32[512]{0:T(512)} %param.11) | copy-start | bytes 6148
  40.3 1.0 %copy-start.2 = (bf16[8,8,32,128]{3,2,1,0:T(8,128)(2,1)S(1)}, bf16[8,8,32,128]{3,2,1,0:T(8,128)(2,1)}, u32[]{:S(2)}) copy-start(bf16[8,8,32,128]{3,2,1,0:T(8,128)(2,1)} %get-tuple-element.42) | copy-start | bytes 1572868
  40.3 1.5 %copy-start.3 = (bf16[8,256,128]{2,1,0:T(8,128)(2,1)S(1)}, bf16[8,256,128]{2,1,0:T(8,128)(2,1)}, u32[]{:S(2)}) copy-start(bf16[8,256,128]{2,1,0:T(8,128)(2,1)} %get-tuple-element.43) | copy-start | bytes 1572868
  41.3 0.9 copy-start.4
  42.3 56.3 %copy-start.7 = (s32[64]{0:T(128)S(1)}, s32[64]{0:T(128)}, u32[]{:S(2)}) copy-start(s32[64]{0:T(128)} %param.12) | copy-start | bytes 772
  42.3 56.3 %copy-start.1 = (f32[512]{0:T(512)S(1)}, f32[512]{0:T(512)}, u32[]{:S(2)}) copy-start(f32[512]{0:T(512)} %multiply_add_fusion) | copy-start | bytes 6148
  42.3 59.4 %copy-start.5 = (f32[512]{0:T(512)S(1)}, f32[512]{0:T(512)}, u32[]{:S(2)}) copy-start(f32[512]{0:T(512)} %param.9) | copy-start | bytes 6148
  42.3 59.4 %copy-start.6 = (f32[512]{0:T(512)S(1)}, f32[512]{0:T(512)}, u32[]{:S(2)}) copy-start(f32[512]{0:T(512)} %param.10) | copy-start | bytes 6148

commit v13 on v12

--- a/solution.py
+++ b/solution.py
@@ -48,9 +48,8 @@
     return total + n
 
 
-def gather_kernel(g, picked, pts, prev, rows_out, pts_out, prev_out,
-                  in_send, in_recv, out_send, out_recv, pt_send, pt_recv, pv_send, pv_recv,
-                  local_sem):
+def gather_kernel(g, picked, pts, rows_out, pts_out,
+                  in_send, in_recv, out_send, out_recv, pt_send, pt_recv, local_sem):
     c, q, w = coords()
     barrier = pltpu.get_barrier_semaphore()
     n = greet_all(barrier, lambda i: dev(c, q, lax.rem(w + 1 + i, g)), g - 1, 0)
@@ -60,7 +59,6 @@
     own = [
         pltpu.make_async_copy(picked, rows_out.at[q, w], local_sem.at[0]),
         pltpu.make_async_copy(pts, pts_out.at[c], local_sem.at[1]),
-        pltpu.make_async_copy(prev, prev_out.at[c], local_sem.at[2]),
     ]
     for cp in own:
         cp.start()
@@ -83,9 +81,6 @@
             pltpu.make_async_remote_copy(
                 src_ref=pts, dst_ref=pts_out.at[src], send_sem=pt_send.at[i],
                 recv_sem=pt_recv.at[src], device_id=peer, device_id_type=MESH_ID),
-            pltpu.make_async_remote_copy(
-                src_ref=prev, dst_ref=prev_out.at[src], send_sem=pv_send.at[i],
-                recv_sem=pv_recv.at[src], device_id=peer, device_id_type=MESH_ID),
         )
 
     def start_inner(i, carry):
@@ -129,23 +124,29 @@
     lax.fori_loop(0, g - 1, wait_group, 0)
     lax.fori_loop(0, g - 1, wait_outer, 0)
     own[1].wait()
-    own[2].wait()
-
-
-def gather_all(picked, pts, prev, g):
+
+
+def gather_all(picked, pts, g):
     dma = pltpu.SemaphoreType.DMA
     return pl.pallas_call(
         functools.partial(gather_kernel, g),
         out_shape=(
             jax.ShapeDtypeStruct((g, g) + picked.shape, picked.dtype),
             jax.ShapeDtypeStruct((g,) + pts.shape, pts.dtype),
-            jax.ShapeDtypeStruct((g,) + prev.shape, prev.dtype),
         ),
-        in_specs=[ANY, ANY, ANY],
-        out_specs=(ANY, ANY, ANY),
-        scratch_shapes=[dma((g,)) for _ in range(8)] + [dma((3,))],
+        in_specs=[ANY, ANY],
+        out_specs=(ANY, ANY),
+        scratch_shapes=[dma((g,)) for _ in range(6)] + [dma((2,))],
         compiler_params=pltpu.CompilerParams(has_side_effects=True, collective_id=0),
-    )(picked, pts, prev)
+    )(picked, pts)
+
+
+def split3(v):
+    hi = lax.reduce_precision(v, exponent_bits=8, mantissa_bits=7)
+    rest = v - hi
+    mid = lax.reduce_precision(rest, exponent_bits=8, mantissa_bits=7)
+    lo = rest - mid
+    return jnp.stack([hi, mid, lo]).astype(jnp.bfloat16)
 
 
 def scatter_kernel(g, part, total_out, stage1, mid, stage2,
@@ -261,9 +262,18 @@
     g = 8
     lanes = 128
     dense = lambda a: a.reshape(-1, lanes)
-    rows_all, pts_all, prev_all = gather_all(
-        dense(picked), dense(points), preview.reshape(1, -1), g)
+    pt_rows = points.size // lanes
+    pieces = split3(preview).reshape(-1, lanes)
+    pad = (-(pt_rows + pieces.shape[0])) % 16
+    block = jnp.concatenate(
+        [dense(points), pieces, jnp.zeros((pad, lanes), points.dtype)], axis=0)
+    rows_all, pts_all = gather_all(dense(picked), block, g)
     rows_all, batch_rows, counts = lax.optimization_barrier((rows_all, batch_rows, counts))
+    prev_all = pts_all[:, pt_rows:pt_rows + pieces.shape[0], :].astype(jnp.float32)
+    prev_all = prev_all.reshape(g, 3, -1)
+    prev_all = (prev_all[:, 0] + prev_all[:, 1]) + prev_all[:, 2]
+    pts_all = pts_all[:, :pt_rows, :]
+    adjust = NOISE_VAR * preview - targets
     slot_ids = jnp.arange(slot_total, dtype=jnp.int32)
     count_here = counts.reshape((1,))
     in_count = slot_ids < count_here[0]
@@ -274,7 +284,7 @@
     kernel_rows = scatter_all(partial_value.reshape(g, g, slot_total), g).reshape(-1)
     residual = jnp.where(
         in_count,
-        kernel_rows + NOISE_VAR * preview.at[batch_rows].get(mode="promise_in_bounds") - targets.at[batch_rows].get(mode="promise_in_bounds"),
+        kernel_rows + adjust.at[batch_rows].get(mode="promise_in_bounds"),
         0.0,
     )
     scatter_rows = (batch_rows[:, None] == jnp.arange(local_size, dtype=jnp.int32)[None, :]).astype(

time: 103 us -> 102 us (level)
  local copies, waits for them, and re-layouts: 6.94 us -> 5.66 us
    sub x0 -> x1, other arithmetic: none -> 1.3 us  [per_device(): adjust = NOISE_VAR * preview - targets]
    add x1, other arithmetic: 1.28 us -> 0.06 us  [per_device(): prev_all = prev_all[:, 0] + prev_all[:, 1] + prev_all[:, 2]]
where the time goes in v13:
time: 102 us
  Pallas kernels  52.6 us (52%)
  matrix products  36 us (35%)
  other arithmetic  5.93 us (6%)
  local copies, waits for them, and re-layouts  5.66 us (6%)
  between operations  1.53 us (2%)
    dot_general x2, matrix products, matern_sums(): lax.dot_general(neg_two_rows, col_points, (((1,), (1,)), ((), ())), prefe...  35.2 us
    pallas_call x1, Pallas kernels, gather_all(): pl.pallas_call(functools.partial(gather_kernel, g), out_shape=(jax.ShapeD...  33.1 us
    pallas_call x1, Pallas kernels, scatter_all(): pl.pallas_call(functools.partial(scatter_kernel, g), out_shape=jax.ShapeD...  19.5 us

profile of v13, /device:TPU:8, one launch (start us, length us, event | category | flops | bytes accessed | tf_op | source)
XLA Modules:
  0.0 101.8 jit_solution(12652590977033934136)
XLA Ops:
  0.6 1.3 %multiply_subtract_fusion = (f32[512]{0:T(512)}, f32[512]{0:T(512)S(1)}) fusion(f32[512]{0:T(512)} %param.11, f32[512]{0:T(512)} %param.9, f32[512]{0:T(512)} %param.10), kind=kLoop, calls=%fused_computation.33 | loop fusion | flops 2048 | bytes 10240 | tf_op jit(solution)/shard_map/sub | solution.py:276
  2.0 1.0 copy.10
  3.0 0.1 reshape.39
  3.1 0.1 pad.2.clone
  3.2 0.7 maximum_maximum_fusion.pts
  3.9 0.7 compare_select_fusion.1
  4.6 0.6 gather_fusion
  5.2 0.7 reshape.38.picked
  5.9 33.1 %shard_map.77 = (bf16[8,8,32,128]{3,2,1,0:T(8,128)(2,1)}, bf16[8,272,128]{2,1,0:T(8,128)(2,1)}) custom-call(bf16[32,128]{1,0:T(8,128)(2,1)} %reshape.38.picked, bf16[272,128]{1,0:T(8,128)(2,1)} %maximum_maximum_fusion.pts), custom_call_target="tpu_custom_call" | custom-call | tf_op jit(solution)/shard_map/pallas_call | solution.py:131
  39.0 1.2 %convert_multiply_fusion = f32[8,8,32,128]{3,2,1,0:T(8,128)S(1)} fusion(bf16[8,8,32,128]{3,2,1,0:T(8,128)(2,1)} %get-tuple-element.41), kind=kLoop, calls=%fused_computation.13 | loop fusion | flops 524288 | bytes 1572864 | tf_op jit(solution)/shard_map/square | solution.py:239
  40.2 0.3 square.10
  40.5 0.0 copy-start.1
  40.5 0.0 copy-start.2
  40.5 0.6 reduce_sum.27
  41.2 0.4 copy-done.1
  41.6 0.4 mul.41
  42.0 0.0 copy-done.2
  42.1 0.4 reshape_reshape.4
  42.5 0.1 fusion.7
  42.6 0.0 copy-start.5
  42.6 0.0 copy-start
  42.7 0.0 copy-start.3
  42.7 0.0 copy-start.4
  42.7 36.0 %while.11 = (s32[]{:T(128)}, f32[4096]{0:T(1024)S(1)}, f32[4096]{0:T(1024)S(1)}, bf16[2,2048,64]{2,1,0:T(8,128)(2,1)S(1)}, bf16[4096,64]{1,0:T(8,128)(2,1)S(1)},...) while((s32[]{:T(128)}, f32[4096]{0:T(1024)S(1)}, f32[4096]{0:T(1024)S(1)}, ...), condition=%wide.region_4.5_spmd.clone, body=%wide.region_1.4_spmd.clone.sunk | while | flops 1158023168 | bytes 1957995 | solution.py:253
  42.7 0.3 multiply_reduce_fusion.4
  43.1 17.6 %multiply_reduce_fusion.5 = f32[4096]{0:T(1024)S(1)} fusion(bf16[4096,64]{1,0:T(8,128)(2,1)S(1)} %get-tuple-element.142, f32[2048]{0:T(1024)S(1)} %bitcast.35, f32[2048]{0:T(1024)S(1)} %multiply_reduce_fusion.4, f32[4096]{0:T(1024)S(1)} %get-tuple-element.140, bf16[2,2048,64]{2,1,0:T(8,128)(2,1)S(1)} %get-tuple-element.141, s32[]{:T(128)} %get-tuple-element.130), kind=kOutput, calls=%fused_computation.6.clone.1 | convolution fusion | flops 1157623808 | bytes 1622020 | tf_op jit(solution)/shard_map/while/body/eval_jaxpr/dot_general | solution.py:228
  60.7 0.3 multiply_reduce_fusion.4
  61.1 17.6 %multiply_reduce_fusion.5 = f32[4096]{0:T(1024)S(1)} fusion(bf16[4096,64]{1,0:T(8,128)(2,1)S(1)} %get-tuple-element.142, f32[2048]{0:T(1024)S(1)} %bitcast.35, f32[2048]{0:T(1024)S(1)} %multiply_reduce_fusion.4, f32[4096]{0:T(1024)S(1)} %get-tuple-element.140, bf16[2,2048,64]{2,1,0:T(8,128)(2,1)S(1)} %get-tuple-element.141, s32[]{:T(128)} %get-tuple-element.130), kind=kOutput, calls=%fused_computation.6.clone.1 | convolution fusion | flops 1157623808 | bytes 1622020 | tf_op jit(solution)/shard_map/while/body/eval_jaxpr/dot_general | solution.py:228
  78.7 0.7 reshape.42.part
  79.4 19.5 %shard_map.78 = f32[1,64]{1,0:T(1,128)} custom-call(f32[8,8,64]{2,1,0:T(8,128)} %reshape.42.part), custom_call_target="tpu_custom_call" | custom-call | tf_op jit(solution)/shard_map/pallas_call | solution.py:211
  98.9 0.0 copy-done.5
  98.9 0.0 copy-done
  98.9 0.8 gather_fusion.1
  100.4 0.9 fusion.5
  101.2 0.0 copy-done.3
  101.2 0.0 copy-done.4
  101.2 0.6 fusion.15
  (20 shorter events, 0.2 us)
Async XLA Ops:
  40.5 1.0 %copy-start.1 = (bf16[8,8,32,128]{3,2,1,0:T(8,128)(2,1)S(1)}, bf16[8,8,32,128]{3,2,1,0:T(8,128)(2,1)}, u32[]{:S(2)}) copy-start(bf16[8,8,32,128]{3,2,1,0:T(8,128)(2,1)} %get-tuple-element.41) | copy-start | bytes 1572868
  40.5 1.5 %copy-start.2 = (bf16[8,272,128]{2,1,0:T(8,128)(2,1)S(1)}, bf16[8,272,128]{2,1,0:T(8,128)(2,1)}, u32[]{:S(2)}) copy-start(bf16[8,272,128]{2,1,0:T(8,128)(2,1)} %get-tuple-element.42) | copy-start | bytes 1671172
  42.6 56.2 %copy-start.5 = (s32[64]{0:T(128)S(1)}, s32[64]{0:T(128)}, u32[]{:S(2)}) copy-start(s32[64]{0:T(128)} %param.12) | copy-start | bytes 772
  42.6 56.3 %copy-start = (f32[512]{0:T(512)S(1)}, f32[512]{0:T(512)}, u32[]{:S(2)}) copy-start(f32[512]{0:T(512)} %get-tuple-element.80) | copy-start | bytes 6148
  42.7 58.6 %copy-start.3 = (f32[512]{0:T(512)S(1)}, f32[512]{0:T(512)}, u32[]{:S(2)}) copy-start(f32[512]{0:T(512)} %param.9) | copy-start | bytes 6148
  42.7 58.6 %copy-start.4 = (f32[512]{0:T(512)S(1)}, f32[512]{0:T(512)}, u32[]{:S(2)}) copy-start(f32[512]{0:T(512)} %param.10) | copy-start | bytes 6148

commit v14 on v12

--- a/solution.py
+++ b/solution.py
@@ -235,8 +235,8 @@
 
 
 def column_sums(row_feats, piece_points, every_coef):
-    row_sq = jnp.sum(jnp.square(row_feats.astype(jnp.float32)), axis=1)
-    neg_two_rows = row_feats * jnp.asarray(-2.0, row_feats.dtype)
+    neg_two_rows = row_feats
+    row_sq = 0.25 * jnp.sum(jnp.square(neg_two_rows.astype(jnp.float32)), axis=1)
     zeros_init = jnp.zeros((row_feats.shape[0],), jnp.float32)
     piece_len = piece_points.shape[0]
     block_len = math.gcd(piece_len, 2048)
@@ -257,7 +257,7 @@
     preview = coefficients + MOMENTUM * velocity
     slot_total = batch_rows.shape[0]
     local_size = points.shape[0]
-    picked = points.at[batch_rows].get(mode="promise_in_bounds")
+    picked = points.at[batch_rows].get(mode="promise_in_bounds") * jnp.asarray(-2.0, points.dtype)
     g = 8
     lanes = 128
     dense = lambda a: a.reshape(-1, lanes)

time: 103 us -> 102 us (level)
  other arithmetic: 5.11 us -> 3.92 us
    reshape x0 -> x1, local copies, waits for them, and re-layouts: none -> 1.71 us  [per_device(): group_rows = rows_all.reshape(-1, points.shape[1])]
    square x1 -> x0, other arithmetic: 1.17 us -> none  [column_sums(): row_sq = jnp.sum(jnp.square(row_feats.astype(jnp.float32)), axis=1)]
where the time goes in v14:
time: 102 us; the launch traced here: 101 us
  Pallas kernels  52.7 us (52%)
  matrix products  35.4 us (35%)
  local copies, waits for them, and re-layouts  7.76 us (8%)
  other arithmetic  3.92 us (4%)
  between operations  1.48 us (1%)
    dot_general x2, matrix products, matern_sums(): lax.dot_general(neg_two_rows, col_points, (((1,), (1,)), ((), ())), prefe...  35.1 us
    pallas_call x1, Pallas kernels, gather_all(): pl.pallas_call(functools.partial(gather_kernel, g), out_shape=(jax.ShapeD...  33.1 us
    pallas_call x1, Pallas kernels, scatter_all(): pl.pallas_call(functools.partial(scatter_kernel, g), out_shape=jax.ShapeD...  19.5 us

profile of v14, /device:TPU:8, one launch (start us, length us, event | category | flops | bytes accessed | tf_op | source)
XLA Modules:
  0.0 101.3 jit_solution(505203114754354687)
XLA Ops:
  0.6 0.0 copy-start
  0.6 1.0 copy.10
  1.6 0.7 reshape.26.pts
  2.4 0.7 compare_select_fusion.1
  3.0 0.6 gather_fusion
  3.7 0.7 mul.48.picked
  4.4 1.3 %multiply_add_fusion = f32[512]{0:T(512)} fusion(f32[512]{0:T(512)} %param.9, f32[512]{0:T(512)} %param.10), kind=kLoop, calls=%fused_computation.26 | loop fusion | flops 1024 | bytes 6144 | tf_op jit(solution)/shard_map/add | solution.py:257
  5.6 33.1 %shard_map.77 = (bf16[8,8,32,128]{3,2,1,0:T(8,128)(2,1)}, bf16[8,256,128]{2,1,0:T(8,128)(2,1)}, f32[8,1,512]{2,1,0:T(1,128)}) custom-call(bf16[32,128]{1,0:T(8,128)(2,1)} %mul.48.picked, bf16[256,128]{1,0:T(8,128)(2,1)} %reshape.26.pts, f32[1,512]{1,0:T(1,128)} %bitcast.36), custom_call_target="tpu_custom_call" | custom-call | tf_op jit(solution)/shard_map/pallas_call | solution.py:137
  38.8 0.0 copy-start.2
  38.8 1.7 %reshape.28 = bf16[4096,64]{1,0:T(8,128)(2,1)S(1)} reshape(bf16[8,8,32,128]{3,2,1,0:T(8,128)(2,1)} %get-tuple-element.42) | data formatting | bytes 1048576 | tf_op jit(solution)/shard_map/reshape | solution.py:270
  40.5 0.6 multiply_reduce_fusion.2
  41.1 0.0 copy-start.3
  41.1 0.0 copy-done.2
  41.2 0.4 reshape_reshape.6
  41.6 0.3 copy-done.3
  41.9 0.0 copy-start.7
  41.9 0.0 copy-start.1
  41.9 36.0 %while.11 = (s32[]{:T(128)}, f32[4096]{0:T(1024)S(1)}, f32[4096]{0:T(1024)S(1)}, bf16[2,2048,64]{2,1,0:T(8,128)(2,1)S(1)}, bf16[4096,64]{1,0:T(8,128)(2,1)S(1)},...) while((s32[]{:T(128)}, f32[4096]{0:T(1024)S(1)}, f32[4096]{0:T(1024)S(1)}, ...), condition=%wide.region_4.5_spmd.clone, body=%wide.region_1.4_spmd.clone.sunk | while | flops 1158023168 | bytes 1957995 | solution.py:252
  41.9 0.3 multiply_reduce_fusion.5
  42.3 17.6 %multiply_reduce_fusion.6 = f32[4096]{0:T(1024)S(1)} fusion(bf16[4096,64]{1,0:T(8,128)(2,1)S(1)} %get-tuple-element.139, f32[2048]{0:T(1024)S(1)} %bitcast.37, f32[2048]{0:T(1024)S(1)} %multiply_reduce_fusion.5, f32[4096]{0:T(1024)S(1)} %get-tuple-element.137, bf16[2,2048,64]{2,1,0:T(8,128)(2,1)S(1)} %get-tuple-element.138, s32[]{:T(128)} %get-tuple-element.127), kind=kOutput, calls=%fused_computation.7.clone.1 | convolution fusion | flops 1157623808 | bytes 1622020 | tf_op jit(solution)/shard_map/while/body/eval_jaxpr/dot_general | solution.py:227
  59.9 0.3 multiply_reduce_fusion.5
  60.3 17.6 %multiply_reduce_fusion.6 = f32[4096]{0:T(1024)S(1)} fusion(bf16[4096,64]{1,0:T(8,128)(2,1)S(1)} %get-tuple-element.139, f32[2048]{0:T(1024)S(1)} %bitcast.37, f32[2048]{0:T(1024)S(1)} %multiply_reduce_fusion.5, f32[4096]{0:T(1024)S(1)} %get-tuple-element.137, bf16[2,2048,64]{2,1,0:T(8,128)(2,1)S(1)} %get-tuple-element.138, s32[]{:T(128)} %get-tuple-element.127), kind=kOutput, calls=%fused_computation.7.clone.1 | convolution fusion | flops 1157623808 | bytes 1622020 | tf_op jit(solution)/shard_map/while/body/eval_jaxpr/dot_general | solution.py:227
  77.9 0.0 copy-start.4
  77.9 0.0 copy-start.5
  77.9 0.7 reshape.29.part
  78.6 19.5 %shard_map.78 = f32[1,64]{1,0:T(1,128)} custom-call(f32[8,8,64]{2,1,0:T(8,128)} %reshape.29.part), custom_call_target="tpu_custom_call" | custom-call | tf_op jit(solution)/shard_map/pallas_call | solution.py:210
  98.2 0.0 copy-done.7
  98.2 0.0 copy-start.6
  98.2 0.0 copy-done.1
  98.2 0.8 gather_fusion.1
  99.0 0.0 copy-done
  99.0 0.8 gather_fusion.2
  100.5 0.0 copy-done.6
  100.5 0.2 fusion.5
  100.7 0.0 copy-done.4
  100.7 0.0 copy-done.5
  100.7 0.6 fusion.18
  (12 shorter events, 0.1 us)
Async XLA Ops:
  0.6 98.4 %copy-start = (f32[512]{0:T(512)S(1)}, f32[512]{0:T(512)}, u32[]{:S(2)}) copy-start(f32[512]{0:T(512)} %param.11) | copy-start | bytes 6148
  38.8 2.4 %copy-start.2 = (bf16[8,256,128]{2,1,0:T(8,128)(2,1)S(1)}, bf16[8,256,128]{2,1,0:T(8,128)(2,1)}, u32[]{:S(2)}) copy-start(bf16[8,256,128]{2,1,0:T(8,128)(2,1)} %get-tuple-element.43) | copy-start | bytes 1572868
  41.1 0.7 copy-start.3
  41.9 56.2 %copy-start.7 = (s32[64]{0:T(128)S(1)}, s32[64]{0:T(128)}, u32[]{:S(2)}) copy-start(s32[64]{0:T(128)} %param.12) | copy-start | bytes 772
  41.9 56.3 %copy-start.1 = (f32[512]{0:T(512)S(1)}, f32[512]{0:T(512)}, u32[]{:S(2)}) copy-start(f32[512]{0:T(512)} %multiply_add_fusion) | copy-start | bytes 6148
  77.9 22.8 %copy-start.4 = (f32[512]{0:T(512)S(1)}, f32[512]{0:T(512)}, u32[]{:S(2)}) copy-start(f32[512]{0:T(512)} %param.9) | copy-start | bytes 6148
  77.9 22.8 %copy-start.5 = (f32[512]{0:T(512)S(1)}, f32[512]{0:T(512)}, u32[]{:S(2)}) copy-start(f32[512]{0:T(512)} %param.10) | copy-start | bytes 6148
  98.2 2.3 %copy-start.6 = (f32[1,64]{1,0:T(1,128)S(1)}, f32[1,64]{1,0:T(1,128)}, u32[]{:S(2)}) copy-start(f32[1,64]{1,0:T(1,128)} %shard_map.78) | copy-start | bytes 772

commit v15 on v14

--- a/solution.py
+++ b/solution.py
@@ -257,7 +257,9 @@
     preview = coefficients + MOMENTUM * velocity
     slot_total = batch_rows.shape[0]
     local_size = points.shape[0]
-    picked = points.at[batch_rows].get(mode="promise_in_bounds") * jnp.asarray(-2.0, points.dtype)
+    choose = (batch_rows[:, None] == jnp.arange(local_size, dtype=jnp.int32)[None, :])
+    choose = jnp.where(choose, -2.0, 0.0).astype(points.dtype)
+    picked = jnp.dot(choose, points, preferred_element_type=jnp.float32).astype(points.dtype)
     g = 8
     lanes = 128
     dense = lambda a: a.reshape(-1, lanes)

time: 102 us -> 101 us (level)
    dot_general x0 -> x1, matrix products: none -> 1.06 us  [per_device(): jnp.dot(choose, points, preferred_element_type=jnp.float32)]
where the time goes in v15:
time: 101 us
  Pallas kernels  52.7 us (52%)
  matrix products  36.4 us (36%)
  local copies, waits for them, and re-layouts  7.13 us (7%)
  other arithmetic  3.25 us (3%)
  between operations  1.48 us (1%)
    dot_general x2, matrix products, matern_sums(): lax.dot_general(neg_two_rows, col_points, (((1,), (1,)), ((), ())), prefe...  35.1 us
    pallas_call x1, Pallas kernels, gather_all(): pl.pallas_call(functools.partial(gather_kernel, g), out_shape=(jax.ShapeD...  33.1 us
    pallas_call x1, Pallas kernels, scatter_all(): pl.pallas_call(functools.partial(scatter_kernel, g), out_shape=jax.ShapeD...  19.5 us

profile of v15, /device:TPU:8, one launch (start us, length us, event | category | flops | bytes accessed | tf_op | source)
XLA Modules:
  0.0 101.0 jit_solution(10755008976896113113)
XLA Ops:
  0.6 0.0 copy-start
  0.6 1.3 %multiply_add_fusion = f32[512]{0:T(512)} fusion(f32[512]{0:T(512)} %param.9, f32[512]{0:T(512)} %param.10), kind=kLoop, calls=%fused_computation.28 | loop fusion | flops 1024 | bytes 6144 | tf_op jit(solution)/shard_map/add | solution.py:257
  1.9 1.0 copy.9
  2.9 0.7 reshape.27.pts
  3.6 1.1 %convolution_convert_fusion = bf16[64,64]{1,0:T(8,128)(2,1)S(1)} fusion(bf16[512,64]{0,1:T(8,128)(2,1)} %param.8, s32[64]{0:T(128)} %param.12), kind=kOutput, calls=%fused_computation.14 | convolution fusion | flops 4296704 | bytes 73984 | tf_op jit(solution)/shard_map/dot_general | solution.py:262
  4.7 0.7 reshape.26.picked
  5.4 33.1 %shard_map.77 = (bf16[8,8,32,128]{3,2,1,0:T(8,128)(2,1)}, bf16[8,256,128]{2,1,0:T(8,128)(2,1)}, f32[8,1,512]{2,1,0:T(1,128)}) custom-call(bf16[32,128]{1,0:T(8,128)(2,1)} %reshape.26.picked, bf16[256,128]{1,0:T(8,128)(2,1)} %reshape.27.pts, f32[1,512]{1,0:T(1,128)} %bitcast.37), custom_call_target="tpu_custom_call" | custom-call | tf_op jit(solution)/shard_map/pallas_call | solution.py:137
  38.5 0.0 copy-start.2
  38.5 1.7 %reshape.29 = bf16[4096,64]{1,0:T(8,128)(2,1)S(1)} reshape(bf16[8,8,32,128]{3,2,1,0:T(8,128)(2,1)} %get-tuple-element.42) | data formatting | bytes 1048576 | tf_op jit(solution)/shard_map/reshape | solution.py:272
  40.3 0.6 multiply_reduce_fusion.2
  40.9 0.0 copy-start.3
  40.9 0.0 copy-done.2
  40.9 0.4 reshape_reshape.6
  41.3 0.3 copy-done.3
  41.7 0.0 copy-start.7
  41.7 0.0 copy-start.1
  41.7 36.0 %while.11 = (s32[]{:T(128)}, f32[4096]{0:T(1024)S(1)}, f32[4096]{0:T(1024)S(1)}, bf16[2,2048,64]{2,1,0:T(8,128)(2,1)S(1)}, bf16[4096,64]{1,0:T(8,128)(2,1)S(1)},...) while((s32[]{:T(128)}, f32[4096]{0:T(1024)S(1)}, f32[4096]{0:T(1024)S(1)}, ...), condition=%wide.region_4.5_spmd.clone, body=%wide.region_1.4_spmd.clone.sunk | while | flops 1158023168 | bytes 1957995 | solution.py:252
  41.7 0.3 multiply_reduce_fusion.5
  42.1 17.6 %multiply_reduce_fusion.6 = f32[4096]{0:T(1024)S(1)} fusion(bf16[4096,64]{1,0:T(8,128)(2,1)S(1)} %get-tuple-element.139, f32[2048]{0:T(1024)S(1)} %bitcast.38, f32[2048]{0:T(1024)S(1)} %multiply_reduce_fusion.5, f32[4096]{0:T(1024)S(1)} %get-tuple-element.137, bf16[2,2048,64]{2,1,0:T(8,128)(2,1)S(1)} %get-tuple-element.138, s32[]{:T(128)} %get-tuple-element.127), kind=kOutput, calls=%fused_computation.6.clone.1 | convolution fusion | flops 1157623808 | bytes 1622020 | tf_op jit(solution)/shard_map/while/body/eval_jaxpr/dot_general | solution.py:227
  59.7 0.3 multiply_reduce_fusion.5
  60.1 17.6 %multiply_reduce_fusion.6 = f32[4096]{0:T(1024)S(1)} fusion(bf16[4096,64]{1,0:T(8,128)(2,1)S(1)} %get-tuple-element.139, f32[2048]{0:T(1024)S(1)} %bitcast.38, f32[2048]{0:T(1024)S(1)} %multiply_reduce_fusion.5, f32[4096]{0:T(1024)S(1)} %get-tuple-element.137, bf16[2,2048,64]{2,1,0:T(8,128)(2,1)S(1)} %get-tuple-element.138, s32[]{:T(128)} %get-tuple-element.127), kind=kOutput, calls=%fused_computation.6.clone.1 | convolution fusion | flops 1157623808 | bytes 1622020 | tf_op jit(solution)/shard_map/while/body/eval_jaxpr/dot_general | solution.py:227
  77.7 0.0 copy-start.4
  77.7 0.0 copy-start.5
  77.7 0.7 reshape.30.part
  78.4 19.5 %shard_map.78 = f32[1,64]{1,0:T(1,128)} custom-call(f32[8,8,64]{2,1,0:T(8,128)} %reshape.30.part), custom_call_target="tpu_custom_call" | custom-call | tf_op jit(solution)/shard_map/pallas_call | solution.py:210
  97.9 0.0 copy-done.7
  97.9 0.0 copy-start.6
  98.0 0.0 copy-done.1
  98.0 0.8 gather_fusion
  98.8 0.0 copy-done
  98.8 0.8 gather_fusion.1
  100.2 0.0 copy-done.6
  100.2 0.2 fusion.5
  100.4 0.0 copy-done.4
  100.5 0.0 copy-done.5
  100.5 0.6 fusion.23
  (10 shorter events, 0.1 us)
Async XLA Ops:
  0.6 98.1 %copy-start = (f32[512]{0:T(512)S(1)}, f32[512]{0:T(512)}, u32[]{:S(2)}) copy-start(f32[512]{0:T(512)} %param.11) | copy-start | bytes 6148
  38.5 2.4 %copy-start.2 = (bf16[8,256,128]{2,1,0:T(8,128)(2,1)S(1)}, bf16[8,256,128]{2,1,0:T(8,128)(2,1)}, u32[]{:S(2)}) copy-start(bf16[8,256,128]{2,1,0:T(8,128)(2,1)} %get-tuple-element.43) | copy-start | bytes 1572868
  40.9 0.7 copy-start.3
  41.7 56.2 %copy-start.7 = (s32[64]{0:T(128)S(1)}, s32[64]{0:T(128)}, u32[]{:S(2)}) copy-start(s32[64]{0:T(128)} %param.12) | copy-start | bytes 772
  41.7 56.3 %copy-start.1 = (f32[512]{0:T(512)S(1)}, f32[512]{0:T(512)}, u32[]{:S(2)}) copy-start(f32[512]{0:T(512)} %multiply_add_fusion) | copy-start | bytes 6148
  77.7 22.8 %copy-start.4 = (f32[512]{0:T(512)S(1)}, f32[512]{0:T(512)}, u32[]{:S(2)}) copy-start(f32[512]{0:T(512)} %param.9) | copy-start | bytes 6148
  77.7 22.8 %copy-start.5 = (f32[512]{0:T(512)S(1)}, f32[512]{0:T(512)}, u32[]{:S(2)}) copy-start(f32[512]{0:T(512)} %param.10) | copy-start | bytes 6148
  97.9 2.3 %copy-start.6 = (f32[1,64]{1,0:T(1,128)S(1)}, f32[1,64]{1,0:T(1,128)}, u32[]{:S(2)}) copy-start(f32[1,64]{1,0:T(1,128)} %shard_map.78) | copy-start | bytes 772

commit v16 on v15

--- a/solution.py
+++ b/solution.py
@@ -274,14 +274,12 @@
     every_coef = prev_all.reshape(-1)
     partial_value = column_sums(group_rows, piece_points, every_coef)
     kernel_rows = scatter_all(partial_value.reshape(g, g, slot_total), g).reshape(-1)
-    residual = jnp.where(
-        in_count,
-        kernel_rows + NOISE_VAR * preview.at[batch_rows].get(mode="promise_in_bounds") - targets.at[batch_rows].get(mode="promise_in_bounds"),
-        0.0,
-    )
     scatter_rows = (batch_rows[:, None] == jnp.arange(local_size, dtype=jnp.int32)[None, :]).astype(
         jnp.float32
     )
+    adjust = NOISE_VAR * preview - targets
+    looked_up = jnp.dot(scatter_rows, adjust, precision=lax.Precision.HIGHEST)
+    residual = jnp.where(in_count, kernel_rows + looked_up, 0.0)
     update_sum = jnp.dot(residual, scatter_rows, precision=lax.Precision.HIGHEST)
     new_velocity = MOMENTUM * velocity - STEP_SIZE * update_sum
     new_coefficients = coefficients + new_velocity

time: 101 us -> 101 us (level)
  local copies, waits for them, and re-layouts: 7.13 us -> 5.52 us
    gather x2 -> x0, local copies, waits for them, and re-layouts: 1.59 us -> none  [the longest x1 0.8 us: per_device(): preview.at[batch_rows].get(mode='promise_in_bounds')]
    sub x0 -> x1, other arithmetic: none -> 1.3 us  [per_device(): adjust = NOISE_VAR * preview - targets]
    add x1 -> x0, other arithmetic: 1.28 us -> none  [per_device(): preview = coefficients + MOMENTUM * velocity]
where the time goes in v16:
time: 101 us; the launch traced here: 100 us
  Pallas kernels  52.7 us (52%)
  matrix products  37.2 us (37%)
  local copies, waits for them, and re-layouts  5.52 us (5%)
  other arithmetic  3.26 us (3%)
  between operations  1.44 us (1%)
    dot_general x2, matrix products, matern_sums(): lax.dot_general(neg_two_rows, col_points, (((1,), (1,)), ((), ())), prefe...  35 us
    pallas_call x1, Pallas kernels, gather_all(): pl.pallas_call(functools.partial(gather_kernel, g), out_shape=(jax.ShapeD...  33.1 us
    pallas_call x1, Pallas kernels, scatter_all(): pl.pallas_call(functools.partial(scatter_kernel, g), out_shape=jax.ShapeD...  19.5 us

profile of v16, /device:TPU:8, one launch (start us, length us, event | category | flops | bytes accessed | tf_op | source)
XLA Modules:
  0.0 100.1 jit_solution(4623743899953642570)
XLA Ops:
  0.6 1.3 %multiply_subtract_fusion = (f32[512]{0:T(512)}, f32[512]{0:T(512)}) fusion(f32[512]{0:T(512)} %param.11, f32[512]{0:T(512)} %param.9, f32[512]{0:T(512)} %param.10), kind=kLoop, calls=%fused_computation.27 | loop fusion | flops 2048 | bytes 10240 | tf_op jit(solution)/shard_map/sub | solution.py:280
  1.9 1.0 copy.9
  2.9 0.7 reshape.27.pts
  3.6 1.1 %convolution_convert_fusion = bf16[64,64]{1,0:T(8,128)(2,1)S(1)} fusion(bf16[512,64]{0,1:T(8,128)(2,1)} %param.8, s32[64]{0:T(128)} %param.12), kind=kOutput, calls=%fused_computation.12 | convolution fusion | flops 4296704 | bytes 73984 | tf_op jit(solution)/shard_map/dot_general | solution.py:262
  4.7 0.7 reshape.26.picked
  5.4 33.1 %shard_map.77 = (bf16[8,8,32,128]{3,2,1,0:T(8,128)(2,1)}, bf16[8,256,128]{2,1,0:T(8,128)(2,1)}, f32[8,1,512]{2,1,0:T(1,128)}) custom-call(bf16[32,128]{1,0:T(8,128)(2,1)} %reshape.26.picked, bf16[256,128]{1,0:T(8,128)(2,1)} %reshape.27.pts, f32[1,512]{1,0:T(1,128)} %bitcast.43), custom_call_target="tpu_custom_call" | custom-call | tf_op jit(solution)/shard_map/pallas_call | solution.py:137
  38.5 0.0 copy-start
  38.5 1.7 %reshape.29 = bf16[4096,64]{1,0:T(8,128)(2,1)S(1)} reshape(bf16[8,8,32,128]{3,2,1,0:T(8,128)(2,1)} %get-tuple-element.42) | data formatting | bytes 1048576 | tf_op jit(solution)/shard_map/reshape | solution.py:272
  40.3 0.6 multiply_reduce_fusion.2
  40.9 0.0 copy-start.1
  40.9 0.0 copy-done
  40.9 0.4 reshape_reshape.6
  41.3 0.3 copy-done.1
  41.7 0.0 copy-start.4
  41.7 0.0 copy-start.5
  41.7 0.0 copy-start.2
  41.7 0.0 copy-start.3
  41.7 35.9 %while.11 = (s32[]{:T(128)}, f32[4096]{0:T(1024)S(1)}, f32[4096]{0:T(1024)S(1)}, bf16[2,2048,64]{2,1,0:T(8,128)(2,1)S(1)}, bf16[4096,64]{1,0:T(8,128)(2,1)S(1)},...) while((s32[]{:T(128)}, f32[4096]{0:T(1024)S(1)}, f32[4096]{0:T(1024)S(1)}, ...), condition=%wide.region_4.5_spmd.clone, body=%wide.region_1.4_spmd.clone.sunk | while | flops 1158023168 | bytes 1957995 | solution.py:252
  41.7 0.3 multiply_reduce_fusion.5
  42.1 17.5 %multiply_reduce_fusion.6 = f32[4096]{0:T(1024)S(1)} fusion(bf16[4096,64]{1,0:T(8,128)(2,1)S(1)} %get-tuple-element.141, f32[2048]{0:T(1024)S(1)} %bitcast.42, f32[2048]{0:T(1024)S(1)} %multiply_reduce_fusion.5, f32[4096]{0:T(1024)S(1)} %get-tuple-element.139, bf16[2,2048,64]{2,1,0:T(8,128)(2,1)S(1)} %get-tuple-element.140, s32[]{:T(128)} %get-tuple-element.129), kind=kOutput, calls=%fused_computation.4.clone.1 | convolution fusion | flops 1157623808 | bytes 1622020 | tf_op jit(solution)/shard_map/while/body/eval_jaxpr/dot_general | solution.py:227
  59.7 0.3 multiply_reduce_fusion.5
  60.0 17.5 %multiply_reduce_fusion.6 = f32[4096]{0:T(1024)S(1)} fusion(bf16[4096,64]{1,0:T(8,128)(2,1)S(1)} %get-tuple-element.141, f32[2048]{0:T(1024)S(1)} %bitcast.42, f32[2048]{0:T(1024)S(1)} %multiply_reduce_fusion.5, f32[4096]{0:T(1024)S(1)} %get-tuple-element.139, bf16[2,2048,64]{2,1,0:T(8,128)(2,1)S(1)} %get-tuple-element.140, s32[]{:T(128)} %get-tuple-element.129), kind=kOutput, calls=%fused_computation.4.clone.1 | convolution fusion | flops 1157623808 | bytes 1622020 | tf_op jit(solution)/shard_map/while/body/eval_jaxpr/dot_general | solution.py:227
  77.6 0.7 reshape.30.part
  78.3 19.5 %shard_map.78 = f32[1,64]{1,0:T(1,128)} custom-call(f32[8,8,64]{2,1,0:T(8,128)} %reshape.30.part), custom_call_target="tpu_custom_call" | custom-call | tf_op jit(solution)/shard_map/pallas_call | solution.py:210
  98.4 0.0 copy-done.4
  98.4 0.0 copy-done.5
  98.4 0.8 fusion.7
  99.3 0.3 fusion.8
  99.5 0.0 copy-done.2
  99.5 0.0 copy-done.3
  99.6 0.6 fusion.16
  (8 shorter events, 0.1 us)
Async XLA Ops:
  38.5 2.4 %copy-start = (bf16[8,256,128]{2,1,0:T(8,128)(2,1)S(1)}, bf16[8,256,128]{2,1,0:T(8,128)(2,1)}, u32[]{:S(2)}) copy-start(bf16[8,256,128]{2,1,0:T(8,128)(2,1)} %get-tuple-element.43) | copy-start | bytes 1572868
  40.9 0.7 copy-start.1
  41.7 56.8 %copy-start.4 = (f32[512]{0:T(512)S(1)}, f32[512]{0:T(512)}, u32[]{:S(2)}) copy-start(f32[512]{0:T(512)} %get-tuple-element.82) | copy-start | bytes 6148
  41.7 56.8 %copy-start.5 = (s32[64]{0:T(128)S(1)}, s32[64]{0:T(128)}, u32[]{:S(2)}) copy-start(s32[64]{0:T(128)} %param.12) | copy-start | bytes 772
  41.7 57.9 %copy-start.2 = (f32[512]{0:T(512)S(1)}, f32[512]{0:T(512)}, u32[]{:S(2)}) copy-start(f32[512]{0:T(512)} %param.9) | copy-start | bytes 6148
  41.7 57.8 %copy-start.3 = (f32[512]{0:T(512)S(1)}, f32[512]{0:T(512)}, u32[]{:S(2)}) copy-start(f32[512]{0:T(512)} %param.10) | copy-start | bytes 6148

commit v17 on v16

--- a/solution.py
+++ b/solution.py
@@ -101,8 +101,11 @@
     lax.fori_loop(0, g - 1, start_group, 0)
 
     def wait_inner(i, carry):
+        inner_copy(i, lax.rem(w + 2 * g - 1 - i, g)).wait_recv()
+        return carry
+
+    def wait_inner_sent(i, carry):
         inner_copy(i, w).wait_send()
-        inner_copy(i, lax.rem(w + 2 * g - 1 - i, g)).wait_recv()
         return carry
 
     lax.fori_loop(0, g - 1, wait_inner, 0)
@@ -128,6 +131,7 @@
 
     lax.fori_loop(0, g - 1, wait_group, 0)
     lax.fori_loop(0, g - 1, wait_outer, 0)
+    lax.fori_loop(0, g - 1, wait_inner_sent, 0)
     own[1].wait()
     own[2].wait()
 
@@ -177,8 +181,11 @@
     lax.fori_loop(0, g - 1, start_outer, 0)
 
     def wait_outer(i, carry):
+        outer_copy(i, lax.rem(q + 2 * g - 1 - i, g)).wait_recv()
+        return carry
+
+    def wait_outer_sent(i, carry):
         outer_copy(i, q).wait_send()
-        outer_copy(i, lax.rem(q + 2 * g - 1 - i, g)).wait_recv()
         return carry
 
     lax.fori_loop(0, g - 1, wait_outer, 0)
@@ -201,6 +208,7 @@
     lax.fori_loop(0, g - 1, wait_inner, 0)
     own2.wait()
     total_out[...] = jnp.sum(stage2[...], axis=0)
+    lax.fori_loop(0, g - 1, wait_outer_sent, 0)
 
 
 def scatter_all(part, g):

time: 101 us -> 101 us (level)
  no operation moved by 1% of the time
where the time goes in v17:
time: 101 us; the launch traced here: 100 us
  Pallas kernels  52.7 us (52%)
  matrix products  37.2 us (37%)
  local copies, waits for them, and re-layouts  5.52 us (5%)
  other arithmetic  3.26 us (3%)
  between operations  1.44 us (1%)
    dot_general x2, matrix products, matern_sums(): lax.dot_general(neg_two_rows, col_points, (((1,), (1,)), ((), ())), prefe...  35 us
    pallas_call x1, Pallas kernels, gather_all(): pl.pallas_call(functools.partial(gather_kernel, g), out_shape=(jax.ShapeD...  33.2 us
    pallas_call x1, Pallas kernels, scatter_all(): pl.pallas_call(functools.partial(scatter_kernel, g), out_shape=jax.ShapeD...  19.5 us

profile of v17, /device:TPU:8, one launch (start us, length us, event | category | flops | bytes accessed | tf_op | source)
XLA Modules:
  0.0 100.2 jit_solution(2840489331113946612)
XLA Ops:
  0.6 1.3 %multiply_subtract_fusion = (f32[512]{0:T(512)}, f32[512]{0:T(512)}) fusion(f32[512]{0:T(512)} %param.11, f32[512]{0:T(512)} %param.9, f32[512]{0:T(512)} %param.10), kind=kLoop, calls=%fused_computation.27 | loop fusion | flops 2048 | bytes 10240 | tf_op jit(solution)/shard_map/sub | solution.py:288
  1.9 1.0 copy.9
  2.9 0.7 reshape.27.pts
  3.6 1.1 %convolution_convert_fusion = bf16[64,64]{1,0:T(8,128)(2,1)S(1)} fusion(bf16[512,64]{0,1:T(8,128)(2,1)} %param.8, s32[64]{0:T(128)} %param.12), kind=kOutput, calls=%fused_computation.12 | convolution fusion | flops 4296704 | bytes 73984 | tf_op jit(solution)/shard_map/dot_general | solution.py:270
  4.7 0.7 reshape.26.picked
  5.4 33.2 %shard_map.77 = (bf16[8,8,32,128]{3,2,1,0:T(8,128)(2,1)}, bf16[8,256,128]{2,1,0:T(8,128)(2,1)}, f32[8,1,512]{2,1,0:T(1,128)}) custom-call(bf16[32,128]{1,0:T(8,128)(2,1)} %reshape.26.picked, bf16[256,128]{1,0:T(8,128)(2,1)} %reshape.27.pts, f32[1,512]{1,0:T(1,128)} %bitcast.43), custom_call_target="tpu_custom_call" | custom-call | tf_op jit(solution)/shard_map/pallas_call | solution.py:141
  38.5 0.0 copy-start
  38.6 1.7 %reshape.29 = bf16[4096,64]{1,0:T(8,128)(2,1)S(1)} reshape(bf16[8,8,32,128]{3,2,1,0:T(8,128)(2,1)} %get-tuple-element.42) | data formatting | bytes 1048576 | tf_op jit(solution)/shard_map/reshape | solution.py:280
  40.3 0.6 multiply_reduce_fusion.2
  40.9 0.0 copy-start.1
  40.9 0.0 copy-done
  40.9 0.4 reshape_reshape.6
  41.3 0.3 copy-done.1
  41.7 0.0 copy-start.4
  41.7 0.0 copy-start.5
  41.7 0.0 copy-start.2
  41.7 0.0 copy-start.3
  41.7 35.9 %while.11 = (s32[]{:T(128)}, f32[4096]{0:T(1024)S(1)}, f32[4096]{0:T(1024)S(1)}, bf16[2,2048,64]{2,1,0:T(8,128)(2,1)S(1)}, bf16[4096,64]{1,0:T(8,128)(2,1)S(1)},...) while((s32[]{:T(128)}, f32[4096]{0:T(1024)S(1)}, f32[4096]{0:T(1024)S(1)}, ...), condition=%wide.region_4.5_spmd.clone, body=%wide.region_1.4_spmd.clone.sunk | while | flops 1158023168 | bytes 1957995 | solution.py:260
  41.7 0.3 multiply_reduce_fusion.5
  42.1 17.5 %multiply_reduce_fusion.6 = f32[4096]{0:T(1024)S(1)} fusion(bf16[4096,64]{1,0:T(8,128)(2,1)S(1)} %get-tuple-element.141, f32[2048]{0:T(1024)S(1)} %bitcast.42, f32[2048]{0:T(1024)S(1)} %multiply_reduce_fusion.5, f32[4096]{0:T(1024)S(1)} %get-tuple-element.139, bf16[2,2048,64]{2,1,0:T(8,128)(2,1)S(1)} %get-tuple-element.140, s32[]{:T(128)} %get-tuple-element.129), kind=kOutput, calls=%fused_computation.4.clone.1 | convolution fusion | flops 1157623808 | bytes 1622020 | tf_op jit(solution)/shard_map/while/body/eval_jaxpr/dot_general | solution.py:235
  59.7 0.3 multiply_reduce_fusion.5
  60.1 17.5 %multiply_reduce_fusion.6 = f32[4096]{0:T(1024)S(1)} fusion(bf16[4096,64]{1,0:T(8,128)(2,1)S(1)} %get-tuple-element.141, f32[2048]{0:T(1024)S(1)} %bitcast.42, f32[2048]{0:T(1024)S(1)} %multiply_reduce_fusion.5, f32[4096]{0:T(1024)S(1)} %get-tuple-element.139, bf16[2,2048,64]{2,1,0:T(8,128)(2,1)S(1)} %get-tuple-element.140, s32[]{:T(128)} %get-tuple-element.129), kind=kOutput, calls=%fused_computation.4.clone.1 | convolution fusion | flops 1157623808 | bytes 1622020 | tf_op jit(solution)/shard_map/while/body/eval_jaxpr/dot_general | solution.py:235
  77.6 0.7 reshape.30.part
  78.3 19.5 %shard_map.78 = f32[1,64]{1,0:T(1,128)} custom-call(f32[8,8,64]{2,1,0:T(8,128)} %reshape.30.part), custom_call_target="tpu_custom_call" | custom-call | tf_op jit(solution)/shard_map/pallas_call | solution.py:218
  98.5 0.0 copy-done.4
  98.5 0.0 copy-done.5
  98.5 0.8 fusion.7
  99.3 0.3 fusion.8
  99.6 0.0 copy-done.2
  99.6 0.0 copy-done.3
  99.6 0.6 fusion.16
  (8 shorter events, 0.1 us)
Async XLA Ops:
  38.5 2.4 %copy-start = (bf16[8,256,128]{2,1,0:T(8,128)(2,1)S(1)}, bf16[8,256,128]{2,1,0:T(8,128)(2,1)}, u32[]{:S(2)}) copy-start(bf16[8,256,128]{2,1,0:T(8,128)(2,1)} %get-tuple-element.43) | copy-start | bytes 1572868
  40.9 0.7 copy-start.1
  41.7 56.8 %copy-start.4 = (f32[512]{0:T(512)S(1)}, f32[512]{0:T(512)}, u32[]{:S(2)}) copy-start(f32[512]{0:T(512)} %get-tuple-element.82) | copy-start | bytes 6148
  41.7 56.8 %copy-start.5 = (s32[64]{0:T(128)S(1)}, s32[64]{0:T(128)}, u32[]{:S(2)}) copy-start(s32[64]{0:T(128)} %param.12) | copy-start | bytes 772
  41.7 57.9 %copy-start.2 = (f32[512]{0:T(512)S(1)}, f32[512]{0:T(512)}, u32[]{:S(2)}) copy-start(f32[512]{0:T(512)} %param.9) | copy-start | bytes 6148
  41.7 57.9 %copy-start.3 = (f32[512]{0:T(512)S(1)}, f32[512]{0:T(512)}, u32[]{:S(2)}) copy-start(f32[512]{0:T(512)} %param.10) | copy-start | bytes 6148

commit v18 on v16

--- a/solution.py
+++ b/solution.py
@@ -141,7 +141,7 @@
             jax.ShapeDtypeStruct((g,) + pts.shape, pts.dtype),
             jax.ShapeDtypeStruct((g,) + prev.shape, prev.dtype),
         ),
-        in_specs=[ANY, ANY, ANY],
+        in_specs=[pl.BlockSpec(memory_space=pltpu.VMEM)] * 2 + [ANY],
         out_specs=(ANY, ANY, ANY),
         scratch_shapes=[dma((g,)) for _ in range(8)] + [dma((3,))],
         compiler_params=pltpu.CompilerParams(has_side_effects=True, collective_id=0),

time: 101 us -> 101 us (level)
  no operation moved by 1% of the time
where the time goes in v18:
time: 101 us; the launch traced here: 100 us
  Pallas kernels  52.9 us (52%)
  matrix products  37.2 us (37%)
  local copies, waits for them, and re-layouts  5.52 us (5%)
  other arithmetic  3.26 us (3%)
  between operations  1.44 us (1%)
    dot_general x2, matrix products, matern_sums(): lax.dot_general(neg_two_rows, col_points, (((1,), (1,)), ((), ())), prefe...  35 us
    pallas_call x1, Pallas kernels, gather_all(): pl.pallas_call(functools.partial(gather_kernel, g), out_shape=(jax.ShapeD...  33.6 us
    pallas_call x1, Pallas kernels, scatter_all(): pl.pallas_call(functools.partial(scatter_kernel, g), out_shape=jax.ShapeD...  19.3 us

profile of v18, /device:TPU:8, one launch (start us, length us, event | category | flops | bytes accessed | tf_op | source)
XLA Modules:
  0.0 100.4 jit_solution(4190228694749332767)
XLA Ops:
  0.6 1.3 %multiply_subtract_fusion = (f32[512]{0:T(512)}, f32[512]{0:T(512)}) fusion(f32[512]{0:T(512)} %param.11, f32[512]{0:T(512)} %param.9, f32[512]{0:T(512)} %param.10), kind=kLoop, calls=%fused_computation.27 | loop fusion | flops 2048 | bytes 10240 | tf_op jit(solution)/shard_map/sub | solution.py:280
  1.9 1.0 copy.9
  2.9 0.7 reshape.27.pts
  3.6 1.1 %convolution_convert_fusion = bf16[64,64]{1,0:T(8,128)(2,1)S(1)} fusion(bf16[512,64]{0,1:T(8,128)(2,1)} %param.8, s32[64]{0:T(128)} %param.12), kind=kOutput, calls=%fused_computation.12 | convolution fusion | flops 4296704 | bytes 73984 | tf_op jit(solution)/shard_map/dot_general | solution.py:262
  4.7 0.7 reshape.26.picked
  5.4 33.6 %shard_map.77 = (bf16[8,8,32,128]{3,2,1,0:T(8,128)(2,1)}, bf16[8,256,128]{2,1,0:T(8,128)(2,1)}, f32[8,1,512]{2,1,0:T(1,128)}) custom-call(bf16[32,128]{1,0:T(8,128)(2,1)} %reshape.26.picked, bf16[256,128]{1,0:T(8,128)(2,1)} %reshape.27.pts, f32[1,512]{1,0:T(1,128)} %bitcast.43), custom_call_target="tpu_custom_call" | custom-call | tf_op jit(solution)/shard_map/pallas_call | solution.py:137
  39.0 0.0 copy-start
  39.0 1.7 %reshape.29 = bf16[4096,64]{1,0:T(8,128)(2,1)S(1)} reshape(bf16[8,8,32,128]{3,2,1,0:T(8,128)(2,1)} %get-tuple-element.42) | data formatting | bytes 1048576 | tf_op jit(solution)/shard_map/reshape | solution.py:272
  40.7 0.6 multiply_reduce_fusion.2
  41.3 0.0 copy-start.1
  41.4 0.0 copy-done
  41.4 0.4 reshape_reshape.6
  41.8 0.3 copy-done.1
  42.1 0.0 copy-start.4
  42.1 0.0 copy-start.5
  42.1 0.0 copy-start.2
  42.2 0.0 copy-start.3
  42.2 35.9 %while.11 = (s32[]{:T(128)}, f32[4096]{0:T(1024)S(1)}, f32[4096]{0:T(1024)S(1)}, bf16[2,2048,64]{2,1,0:T(8,128)(2,1)S(1)}, bf16[4096,64]{1,0:T(8,128)(2,1)S(1)},...) while((s32[]{:T(128)}, f32[4096]{0:T(1024)S(1)}, f32[4096]{0:T(1024)S(1)}, ...), condition=%wide.region_4.5_spmd.clone, body=%wide.region_1.4_spmd.clone.sunk | while | flops 1158023168 | bytes 1957995 | solution.py:252
  42.2 0.3 multiply_reduce_fusion.5
  42.6 17.5 %multiply_reduce_fusion.6 = f32[4096]{0:T(1024)S(1)} fusion(bf16[4096,64]{1,0:T(8,128)(2,1)S(1)} %get-tuple-element.141, f32[2048]{0:T(1024)S(1)} %bitcast.42, f32[2048]{0:T(1024)S(1)} %multiply_reduce_fusion.5, f32[4096]{0:T(1024)S(1)} %get-tuple-element.139, bf16[2,2048,64]{2,1,0:T(8,128)(2,1)S(1)} %get-tuple-element.140, s32[]{:T(128)} %get-tuple-element.129), kind=kOutput, calls=%fused_computation.4.clone.1 | convolution fusion | flops 1157623808 | bytes 1622020 | tf_op jit(solution)/shard_map/while/body/eval_jaxpr/dot_general | solution.py:227
  60.1 0.3 multiply_reduce_fusion.5
  60.5 17.5 %multiply_reduce_fusion.6 = f32[4096]{0:T(1024)S(1)} fusion(bf16[4096,64]{1,0:T(8,128)(2,1)S(1)} %get-tuple-element.141, f32[2048]{0:T(1024)S(1)} %bitcast.42, f32[2048]{0:T(1024)S(1)} %multiply_reduce_fusion.5, f32[4096]{0:T(1024)S(1)} %get-tuple-element.139, bf16[2,2048,64]{2,1,0:T(8,128)(2,1)S(1)} %get-tuple-element.140, s32[]{:T(128)} %get-tuple-element.129), kind=kOutput, calls=%fused_computation.4.clone.1 | convolution fusion | flops 1157623808 | bytes 1622020 | tf_op jit(solution)/shard_map/while/body/eval_jaxpr/dot_general | solution.py:227
  78.0 0.7 reshape.30.part
  78.7 19.3 %shard_map.78 = f32[1,64]{1,0:T(1,128)} custom-call(f32[8,8,64]{2,1,0:T(8,128)} %reshape.30.part), custom_call_target="tpu_custom_call" | custom-call | tf_op jit(solution)/shard_map/pallas_call | solution.py:210
  98.7 0.0 copy-done.4
  98.7 0.0 copy-done.5
  98.7 0.8 fusion.7
  99.5 0.3 fusion.8
  99.8 0.0 copy-done.2
  99.8 0.0 copy-done.3
  99.8 0.6 fusion.16
  (8 shorter events, 0.1 us)
Async XLA Ops:
  39.0 2.4 %copy-start = (bf16[8,256,128]{2,1,0:T(8,128)(2,1)S(1)}, bf16[8,256,128]{2,1,0:T(8,128)(2,1)}, u32[]{:S(2)}) copy-start(bf16[8,256,128]{2,1,0:T(8,128)(2,1)} %get-tuple-element.43) | copy-start | bytes 1572868
  41.3 0.7 copy-start.1
  42.1 56.6 %copy-start.4 = (f32[512]{0:T(512)S(1)}, f32[512]{0:T(512)}, u32[]{:S(2)}) copy-start(f32[512]{0:T(512)} %get-tuple-element.82) | copy-start | bytes 6148
  42.1 56.6 %copy-start.5 = (s32[64]{0:T(128)S(1)}, s32[64]{0:T(128)}, u32[]{:S(2)}) copy-start(s32[64]{0:T(128)} %param.12) | copy-start | bytes 772
  42.1 57.7 %copy-start.2 = (f32[512]{0:T(512)S(1)}, f32[512]{0:T(512)}, u32[]{:S(2)}) copy-start(f32[512]{0:T(512)} %param.9) | copy-start | bytes 6148
  42.2 57.7 %copy-start.3 = (f32[512]{0:T(512)S(1)}, f32[512]{0:T(512)}, u32[]{:S(2)}) copy-start(f32[512]{0:T(512)} %param.10) | copy-start | bytes 6148

commit v19 on v16

--- a/solution.py
+++ b/solution.py
@@ -148,75 +148,68 @@
     )(picked, pts, prev)
 
 
-def scatter_kernel(g, part, total_out, stage1, mid, stage2,
-                   out_send, out_recv, in_send, in_recv, local_sem):
+def exchange(src_of, dst, my, n, peer_dev, send_sem, recv_sem, local_sem):
+    own = pltpu.make_async_copy(src_of(my), dst.at[my], local_sem)
+    own.start()
+
+    def copy(i, src):
+        peer = lax.rem(my + 1 + i, n)
+        return pltpu.make_async_remote_copy(
+            src_ref=src_of(peer), dst_ref=dst.at[src], send_sem=send_sem.at[i],
+            recv_sem=recv_sem.at[src], device_id=peer_dev(peer), device_id_type=MESH_ID)
+
+    def start(i, carry):
+        copy(i, my).start()
+        return carry
+
+    lax.fori_loop(0, n - 1, start, 0)
+
+    def wait(i, carry):
+        copy(i, my).wait_send()
+        copy(i, lax.rem(my + 2 * n - 1 - i, n)).wait_recv()
+        return carry
+
+    lax.fori_loop(0, n - 1, wait, 0)
+    own.wait()
+
+
+def scatter_kernel(n, part, total_out, s1, m1, s2, m2, s3, sems, local_sem):
     c, q, w = coords()
+    a, bb, cc = q // 2, lax.rem(q, 2) * 2 + lax.rem(w, 2), w // 2
+    at = lambda a2, b2, c2: dev(c, a2 * 2 + b2 // 2, c2 * 2 + lax.rem(b2, 2))
     barrier = pltpu.get_barrier_semaphore()
-    n = greet_all(barrier, lambda i: dev(c, q, lax.rem(w + 1 + i, g)), g - 1, 0)
-    n = greet_all(barrier, lambda i: dev(c, lax.rem(q + 1 + i, g), w), g - 1, n)
-    pl.semaphore_wait(barrier, n)
-    own1 = pltpu.make_async_copy(part.at[q], stage1.at[q], local_sem.at[0])
-    own1.start()
-
-    def outer_copy(i, src):
-        peer = lax.rem(q + 1 + i, g)
-        return pltpu.make_async_remote_copy(
-            src_ref=part.at[peer], dst_ref=stage1.at[src], send_sem=out_send.at[i],
-            recv_sem=out_recv.at[src], device_id=dev(c, peer, w), device_id_type=MESH_ID)
-
-    def inner_copy(i, src):
-        peer = lax.rem(w + 1 + i, g)
-        return pltpu.make_async_remote_copy(
-            src_ref=mid.at[peer], dst_ref=stage2.at[src], send_sem=in_send.at[i],
-            recv_sem=in_recv.at[src], device_id=dev(c, q, peer), device_id_type=MESH_ID)
-
-    def start_outer(i, carry):
-        outer_copy(i, q).start()
-        return carry
-
-    lax.fori_loop(0, g - 1, start_outer, 0)
-
-    def wait_outer(i, carry):
-        outer_copy(i, q).wait_send()
-        outer_copy(i, lax.rem(q + 2 * g - 1 - i, g)).wait_recv()
-        return carry
-
-    lax.fori_loop(0, g - 1, wait_outer, 0)
-    own1.wait()
-    mid[...] = jnp.sum(stage1[...], axis=0)[:, None, :]
-    own2 = pltpu.make_async_copy(mid.at[w], stage2.at[w], local_sem.at[1])
-    own2.start()
-
-    def start_inner(i, carry):
-        inner_copy(i, w).start()
-        return carry
-
-    lax.fori_loop(0, g - 1, start_inner, 0)
-
-    def wait_inner(i, carry):
-        inner_copy(i, w).wait_send()
-        inner_copy(i, lax.rem(w + 2 * g - 1 - i, g)).wait_recv()
-        return carry
-
-    lax.fori_loop(0, g - 1, wait_inner, 0)
-    own2.wait()
-    total_out[...] = jnp.sum(stage2[...], axis=0)
-
-
-def scatter_all(part, g):
-    dma = pltpu.SemaphoreType.DMA
+    k = greet_all(barrier, lambda i: at(lax.rem(a + 1 + i, n), bb, cc), n - 1, 0)
+    k = greet_all(barrier, lambda i: at(a, lax.rem(bb + 1 + i, n), cc), n - 1, k)
+    k = greet_all(barrier, lambda i: at(a, bb, lax.rem(cc + 1 + i, n)), n - 1, k)
+    pl.semaphore_wait(barrier, k)
+    exchange(lambda p: part.at[p], s1, a, n, lambda p: at(p, bb, cc),
+             sems.at[0], sems.at[1], local_sem.at[0])
+    m1[...] = jnp.sum(s1[...], axis=0)
+    exchange(lambda p: m1.at[p], s2, bb, n, lambda p: at(a, p, cc),
+             sems.at[2], sems.at[3], local_sem.at[1])
+    m2[...] = jnp.sum(s2[...], axis=0)[:, None, :]
+    exchange(lambda p: m2.at[p], s3, cc, n, lambda p: at(a, bb, p),
+             sems.at[4], sems.at[5], local_sem.at[2])
+    total_out[...] = jnp.sum(s3[...], axis=0)
+
+
+def scatter_all(part, n):
     vmem = pl.BlockSpec(memory_space=pltpu.VMEM)
     width = part.shape[-1]
+    f32 = jnp.float32
     return pl.pallas_call(
-        functools.partial(scatter_kernel, g),
+        functools.partial(scatter_kernel, n),
         out_shape=jax.ShapeDtypeStruct((1, width), part.dtype),
         in_specs=[vmem],
         out_specs=vmem,
         scratch_shapes=[
-            pltpu.VMEM((g, g, width), jnp.float32),
-            pltpu.VMEM((g, 1, width), jnp.float32),
-            pltpu.VMEM((g, 1, width), jnp.float32),
-            dma((g,)), dma((g,)), dma((g,)), dma((g,)), dma((2,)),
+            pltpu.VMEM((n, n, n, width), f32),
+            pltpu.VMEM((n, n, width), f32),
+            pltpu.VMEM((n, n, width), f32),
+            pltpu.VMEM((n, 1, width), f32),
+            pltpu.VMEM((n, 1, width), f32),
+            pltpu.SemaphoreType.DMA((6, n)),
+            pltpu.SemaphoreType.DMA((3,)),
         ],
         compiler_params=pltpu.CompilerParams(has_side_effects=True, collective_id=1),
     )(part)
@@ -273,7 +266,8 @@
     piece_points = pts_all.reshape(-1, points.shape[1])
     every_coef = prev_all.reshape(-1)
     partial_value = column_sums(group_rows, piece_points, every_coef)
-    kernel_rows = scatter_all(partial_value.reshape(g, g, slot_total), g).reshape(-1)
+    split = partial_value.reshape(4, 2, 4, 2, slot_total).transpose(0, 1, 3, 2, 4)
+    kernel_rows = scatter_all(split.reshape(4, 4, 4, slot_total), 4).reshape(-1)
     scatter_rows = (batch_rows[:, None] == jnp.arange(local_size, dtype=jnp.int32)[None, :]).astype(
         jnp.float32
     )

time: 101 us -> 108 us (1.069)
  the two profiles are of different devices: /device:TPU:8 before, /device:TPU:32 now
where the time goes in v19:
time: 108 us; the launch traced here: 107 us
  Pallas kernels  59.7 us (55%)
  matrix products  37.2 us (34%)
  local copies, waits for them, and re-layouts  5.54 us (5%)
  other arithmetic  3.26 us (3%)
  between operations  1.44 us (1%)
    dot_general x2, matrix products, matern_sums(): lax.dot_general(neg_two_rows, col_points, (((1,), (1,)), ((), ())), prefe...  35 us
    pallas_call x1, Pallas kernels, gather_all(): pl.pallas_call(functools.partial(gather_kernel, g), out_shape=(jax.ShapeD...  32.5 us
    pallas_call x1, Pallas kernels, scatter_all(): pl.pallas_call(functools.partial(scatter_kernel, n), out_shape=jax.ShapeD...  27.2 us

profile of v19, /device:TPU:32, one launch (start us, length us, event | category | flops | bytes accessed | tf_op | source)
XLA Modules:
  0.0 107.2 jit_solution(215268681914847337)
XLA Ops:
  0.6 1.3 %multiply_subtract_fusion = (f32[512]{0:T(512)}, f32[512]{0:T(512)}) fusion(f32[512]{0:T(512)} %param.11, f32[512]{0:T(512)} %param.9, f32[512]{0:T(512)} %param.10), kind=kLoop, calls=%fused_computation.27 | loop fusion | flops 2048 | bytes 10240 | tf_op jit(solution)/shard_map/sub | solution.py:274
  1.9 1.0 copy.9
  2.9 0.7 reshape.30.pts
  3.6 1.1 convolution_convert_fusion
  4.7 0.7 reshape.29.picked
  5.4 32.5 %shard_map.77 = (bf16[8,8,32,128]{3,2,1,0:T(8,128)(2,1)}, bf16[8,256,128]{2,1,0:T(8,128)(2,1)}, f32[8,1,512]{2,1,0:T(1,128)}) custom-call(bf16[32,128]{1,0:T(8,128)(2,1)} %reshape.29.picked, bf16[256,128]{1,0:T(8,128)(2,1)} %reshape.30.pts, f32[1,512]{1,0:T(1,128)} %bitcast.47), custom_call_target="tpu_custom_call" | custom-call | tf_op jit(solution)/shard_map/pallas_call | solution.py:137
  37.9 0.0 copy-start
  37.9 1.7 %reshape.32 = bf16[4096,64]{1,0:T(8,128)(2,1)S(1)} reshape(bf16[8,8,32,128]{3,2,1,0:T(8,128)(2,1)} %get-tuple-element.42) | data formatting | bytes 1048576 | tf_op jit(solution)/shard_map/reshape | solution.py:265
  39.6 0.6 multiply_reduce_fusion.2
  40.2 0.0 copy-start.1
  40.2 0.0 copy-done
  40.3 0.4 reshape_reshape.6
  40.7 0.3 copy-done.1
  41.0 0.0 copy-start.4
  41.0 0.0 copy-start.5
  41.0 0.0 copy-start.2
  41.1 0.0 copy-start.3
  41.1 35.9 %while.11 = (s32[]{:T(128)}, f32[4096]{0:T(1024)S(1)}, f32[4096]{0:T(1024)S(1)}, bf16[2,2048,64]{2,1,0:T(8,128)(2,1)S(1)}, bf16[4096,64]{1,0:T(8,128)(2,1)S(1)},...) while((s32[]{:T(128)}, f32[4096]{0:T(1024)S(1)}, f32[4096]{0:T(1024)S(1)}, ...), condition=%wide.region_4.5_spmd.clone, body=%wide.region_1.4_spmd.clone.sunk | while | flops 1158023168 | bytes 1957995 | solution.py:245
  41.1 0.3 multiply_reduce_fusion.5
  41.5 17.5 %multiply_reduce_fusion.6 = f32[4096]{0:T(1024)S(1)} fusion(bf16[4096,64]{1,0:T(8,128)(2,1)S(1)} %get-tuple-element.141, f32[2048]{0:T(1024)S(1)} %bitcast.44, f32[2048]{0:T(1024)S(1)} %multiply_reduce_fusion.5, f32[4096]{0:T(1024)S(1)} %get-tuple-element.139, bf16[2,2048,64]{2,1,0:T(8,128)(2,1)S(1)} %get-tuple-element.140, s32[]{:T(128)} %get-tuple-element.129), kind=kOutput, calls=%fused_computation.4.clone.1 | convolution fusion | flops 1157623808 | bytes 1622020 | tf_op jit(solution)/shard_map/while/body/eval_jaxpr/dot_general | solution.py:220
  59.0 0.3 multiply_reduce_fusion.5
  59.4 17.5 %multiply_reduce_fusion.6 = f32[4096]{0:T(1024)S(1)} fusion(bf16[4096,64]{1,0:T(8,128)(2,1)S(1)} %get-tuple-element.141, f32[2048]{0:T(1024)S(1)} %bitcast.44, f32[2048]{0:T(1024)S(1)} %multiply_reduce_fusion.5, f32[4096]{0:T(1024)S(1)} %get-tuple-element.139, bf16[2,2048,64]{2,1,0:T(8,128)(2,1)S(1)} %get-tuple-element.140, s32[]{:T(128)} %get-tuple-element.129), kind=kOutput, calls=%fused_computation.4.clone.1 | convolution fusion | flops 1157623808 | bytes 1622020 | tf_op jit(solution)/shard_map/while/body/eval_jaxpr/dot_general | solution.py:220
  76.9 0.1 reshape.33
  77.0 0.6 copy.10
  77.6 27.2 %shard_map.78 = f32[1,64]{1,0:T(1,128)} custom-call(f32[4,4,4,64]{3,2,1,0:T(4,128)} %bitcast.46), custom_call_target="tpu_custom_call" | custom-call | tf_op jit(solution)/shard_map/pallas_call | solution.py:200
  105.5 0.0 copy-done.4
  105.5 0.0 copy-done.5
  105.5 0.8 fusion.7
  106.3 0.3 fusion.8
  106.6 0.0 copy-done.2
  106.6 0.0 copy-done.3
  106.6 0.6 fusion.16
  (8 shorter events, 0.1 us)
Async XLA Ops:
  37.9 2.4 %copy-start = (bf16[8,256,128]{2,1,0:T(8,128)(2,1)S(1)}, bf16[8,256,128]{2,1,0:T(8,128)(2,1)}, u32[]{:S(2)}) copy-start(bf16[8,256,128]{2,1,0:T(8,128)(2,1)} %get-tuple-element.43) | copy-start | bytes 1572868
  40.2 0.7 copy-start.1
  41.0 64.4 %copy-start.4 = (f32[512]{0:T(512)S(1)}, f32[512]{0:T(512)}, u32[]{:S(2)}) copy-start(f32[512]{0:T(512)} %get-tuple-element.82) | copy-start | bytes 6148
  41.0 64.4 %copy-start.5 = (s32[64]{0:T(128)S(1)}, s32[64]{0:T(128)}, u32[]{:S(2)}) copy-start(s32[64]{0:T(128)} %param.12) | copy-start | bytes 772
  41.0 65.5 %copy-start.2 = (f32[512]{0:T(512)S(1)}, f32[512]{0:T(512)}, u32[]{:S(2)}) copy-start(f32[512]{0:T(512)} %param.9) | copy-start | bytes 6148
  41.1 65.5 %copy-start.3 = (f32[512]{0:T(512)S(1)}, f32[512]{0:T(512)}, u32[]{:S(2)}) copy-start(f32[512]{0:T(512)} %param.10) | copy-start | bytes 6148

commit v20 on v16

--- a/solution.py
+++ b/solution.py
@@ -249,7 +249,7 @@
             None,
         )
 
-    result, unused = lax.scan(advance, zeros_init, (point_blocks, coef_blocks))
+    result, unused = lax.scan(advance, zeros_init, (point_blocks, coef_blocks), unroll=True)
     return result
 
 

time: 101 us -> 100 us (0.990)
  no operation moved by 1% of the time
where the time goes in v20:
time: 100 us; the launch traced here: 99.9 us
  Pallas kernels  52.6 us (53%)
  matrix products  37.3 us (37%)
  local copies, waits for them, and re-layouts  5.37 us (5%)
  other arithmetic  3.2 us (3%)
  between operations  1.45 us (1%)
    dot_general x2, matrix products, matern_sums(): lax.dot_general(neg_two_rows, col_points, (((1,), (1,)), ((), ())), prefe...  35.1 us
    pallas_call x1, Pallas kernels, gather_all(): pl.pallas_call(functools.partial(gather_kernel, g), out_shape=(jax.ShapeD...  33.1 us
    pallas_call x1, Pallas kernels, scatter_all(): pl.pallas_call(functools.partial(scatter_kernel, g), out_shape=jax.ShapeD...  19.5 us

profile of v20, /device:TPU:8, one launch (start us, length us, event | category | flops | bytes accessed | tf_op | source)
XLA Modules:
  0.0 99.9 jit_solution(13417721036789121759)
XLA Ops:
  0.6 1.3 %multiply_subtract_fusion = (f32[512]{0:T(512)S(1)}, f32[512]{0:T(512)}) fusion(f32[512]{0:T(512)} %param.9, f32[512]{0:T(512)} %param.7, f32[512]{0:T(512)} %param.8), kind=kLoop, calls=%fused_computation.28 | loop fusion | flops 2048 | bytes 10240 | tf_op jit(solution)/shard_map/sub | solution.py:280
  1.9 1.0 copy.9
  2.9 0.7 reshape.39.pts
  3.6 1.1 %convolution_convert_fusion = bf16[64,64]{1,0:T(8,128)(2,1)S(1)} fusion(bf16[512,64]{0,1:T(8,128)(2,1)} %param.6, s32[64]{0:T(128)} %param.10), kind=kOutput, calls=%fused_computation.11 | convolution fusion | flops 4296704 | bytes 73984 | tf_op jit(solution)/shard_map/dot_general | solution.py:262
  4.7 0.7 reshape.38.picked
  5.4 33.1 %shard_map.77 = (bf16[8,8,32,128]{3,2,1,0:T(8,128)(2,1)}, bf16[8,256,128]{2,1,0:T(8,128)(2,1)}, f32[8,1,512]{2,1,0:T(1,128)}) custom-call(bf16[32,128]{1,0:T(8,128)(2,1)} %reshape.38.picked, bf16[256,128]{1,0:T(8,128)(2,1)} %reshape.39.pts, f32[1,512]{1,0:T(1,128)} %bitcast.28), custom_call_target="tpu_custom_call" | custom-call | tf_op jit(solution)/shard_map/pallas_call | solution.py:137
  38.5 0.0 copy-start
  38.5 1.7 %reshape.41 = bf16[4096,64]{1,0:T(8,128)(2,1)S(1)} reshape(bf16[8,8,32,128]{3,2,1,0:T(8,128)(2,1)} %get-tuple-element.10) | data formatting | bytes 1048576 | tf_op jit(solution)/shard_map/reshape | solution.py:272
  40.2 0.6 multiply_reduce_fusion.2
  40.9 0.0 copy-done
  40.9 0.0 copy-start.1
  40.9 0.2 squeeze.7
  41.2 0.3 multiply_reduce_fusion.3
  41.5 0.1 copy-done.1
  41.6 17.6 %multiply_reduce_fusion = f32[4096]{0:T(1024)S(1)} fusion(f32[2048]{0:T(1024)S(1)} %bitcast.30, f32[2048]{0:T(1024)S(1)} %multiply_reduce_fusion.3, f32[4096]{0:T(1024)S(1)} %broadcast_multiply_fusion, bf16[4096,64]{1,0:T(8,128)(2,1)S(1)} %reshape.41, bf16[2048,64]{1,0:T(8,128)(2,1)S(1)} %squeeze.7), kind=kOutput, calls=%fused_computation.6 | convolution fusion | flops 1157623808 | bytes 835584 | tf_op jit(solution)/shard_map/eval_jaxpr/dot_general | solution.py:227
  59.2 0.2 squeeze.6
  59.4 0.3 multiply_reduce_fusion.4
  59.8 0.0 copy-start.4
  59.8 0.0 copy-start.2
  59.8 0.0 copy-start.3
  59.8 17.6 %multiply_reduce_fusion.1 = f32[4096]{0:T(1024)S(1)} fusion(f32[2048]{0:T(1024)S(1)} %bitcast.29, f32[2048]{0:T(1024)S(1)} %multiply_reduce_fusion.4, f32[4096]{0:T(1024)S(1)} %broadcast_multiply_fusion, bf16[4096,64]{1,0:T(8,128)(2,1)S(1)} %reshape.41, bf16[2048,64]{1,0:T(8,128)(2,1)S(1)} %squeeze.6), kind=kOutput, calls=%fused_computation.8 | convolution fusion | flops 1157623808 | bytes 835584 | tf_op jit(solution)/shard_map/eval_jaxpr/dot_general | solution.py:227
  77.4 0.7 add.55.part
  78.1 19.5 %shard_map.78 = f32[1,64]{1,0:T(1,128)} custom-call(f32[8,8,64]{2,1,0:T(8,128)} %add.55.part), custom_call_target="tpu_custom_call" | custom-call | tf_op jit(solution)/shard_map/pallas_call | solution.py:210
  98.2 0.0 copy-done.4
  98.2 0.8 fusion.6
  99.0 0.3 fusion.7
  99.3 0.0 copy-done.2
  99.3 0.0 copy-done.3
  99.3 0.6 fusion.15
  (4 shorter events, 0.0 us)
Async XLA Ops:
  38.5 2.4 %copy-start = (bf16[8,256,128]{2,1,0:T(8,128)(2,1)S(1)}, bf16[8,256,128]{2,1,0:T(8,128)(2,1)}, u32[]{:S(2)}) copy-start(bf16[8,256,128]{2,1,0:T(8,128)(2,1)} %get-tuple-element.11) | copy-start | bytes 1572868
  40.9 0.7 copy-start.1
  59.8 38.4 %copy-start.4 = (s32[64]{0:T(128)S(1)}, s32[64]{0:T(128)}, u32[]{:S(2)}) copy-start(s32[64]{0:T(128)} %param.10) | copy-start | bytes 772
  59.8 39.5 %copy-start.2 = (f32[512]{0:T(512)S(1)}, f32[512]{0:T(512)}, u32[]{:S(2)}) copy-start(f32[512]{0:T(512)} %param.7) | copy-start | bytes 6148
  59.8 39.5 %copy-start.3 = (f32[512]{0:T(512)S(1)}, f32[512]{0:T(512)}, u32[]{:S(2)}) copy-start(f32[512]{0:T(512)} %param.8) | copy-start | bytes 6148

commit v21 on v20

--- a/solution.py
+++ b/solution.py
@@ -222,8 +222,7 @@
     )(part)
 
 
-def matern_sums(neg_two_rows, row_sq, col_points, col_coef):
-    col_sq = jnp.sum(jnp.square(col_points.astype(jnp.float32)), axis=1)
+def matern_sums(neg_two_rows, row_sq, col_points, col_coef, col_sq):
     neg_two_dot = lax.dot_general(
         neg_two_rows, col_points, (((1,), (1,)), ((), ())), preferred_element_type=jnp.float32
     )
@@ -242,14 +241,16 @@
     block_len = math.gcd(piece_len, 2048)
     point_blocks = piece_points.reshape(-1, block_len, piece_points.shape[1])
     coef_blocks = every_coef.reshape(-1, block_len)
+    sq_blocks = jnp.sum(jnp.square(piece_points.astype(jnp.float32)), axis=1).reshape(-1, block_len)
 
     def advance(partial_sum, column_block):
         return (
-            partial_sum + matern_sums(neg_two_rows, row_sq, column_block[0], column_block[1]),
+            partial_sum
+            + matern_sums(neg_two_rows, row_sq, column_block[0], column_block[1], column_block[2]),
             None,
         )
 
-    result, unused = lax.scan(advance, zeros_init, (point_blocks, coef_blocks), unroll=True)
+    result, unused = lax.scan(advance, zeros_init, (point_blocks, coef_blocks, sq_blocks))
     return result
 
 

time: 100 us -> 102 us (1.020)
  local copies, waits for them, and re-layouts: 5.37 us -> 7.24 us
    another operation x0 -> x2, local copies, waits for them, and re-layouts: none -> 1.67 us  [the longest x1 1.65 us: column_sums(): point_blocks = piece_points.reshape(-1, block_len, piece_points.shape[1])]
where the time goes in v21:
time: 102 us
  Pallas kernels  52.7 us (52%)
  matrix products  37.2 us (36%)
  local copies, waits for them, and re-layouts  7.24 us (7%)
  other arithmetic  3.24 us (3%)
  between operations  1.49 us (1%)
    dot_general x2, matrix products, matern_sums(): lax.dot_general(neg_two_rows, col_points, (((1,), (1,)), ((), ())), prefe...  35 us
    pallas_call x1, Pallas kernels, gather_all(): pl.pallas_call(functools.partial(gather_kernel, g), out_shape=(jax.ShapeD...  33.1 us
    pallas_call x1, Pallas kernels, scatter_all(): pl.pallas_call(functools.partial(scatter_kernel, g), out_shape=jax.ShapeD...  19.6 us

profile of v21, /device:TPU:8, one launch (start us, length us, event | category | flops | bytes accessed | tf_op | source)
XLA Modules:
  0.0 101.9 jit_solution(5856384222217216188)
XLA Ops:
  0.6 1.3 %multiply_subtract_fusion = (f32[512]{0:T(512)}, f32[512]{0:T(512)}) fusion(f32[512]{0:T(512)} %param.11, f32[512]{0:T(512)} %param.9, f32[512]{0:T(512)} %param.10), kind=kLoop, calls=%fused_computation.28 | loop fusion | flops 2048 | bytes 10240 | tf_op jit(solution)/shard_map/sub | solution.py:281
  1.9 1.0 copy.9
  2.9 0.8 reshape.32.pts
  3.7 1.1 %convolution_convert_fusion = bf16[64,64]{1,0:T(8,128)(2,1)S(1)} fusion(bf16[512,64]{0,1:T(8,128)(2,1)} %param.8, s32[64]{0:T(128)} %param.12), kind=kOutput, calls=%fused_computation.12 | convolution fusion | flops 4296704 | bytes 73984 | tf_op jit(solution)/shard_map/dot_general | solution.py:263
  4.7 0.7 reshape.31.picked
  5.4 33.1 %shard_map.77 = (bf16[8,8,32,128]{3,2,1,0:T(8,128)(2,1)}, bf16[8,256,128]{2,1,0:T(8,128)(2,1)}, f32[8,1,512]{2,1,0:T(1,128)}) custom-call(bf16[32,128]{1,0:T(8,128)(2,1)} %reshape.31.picked, bf16[256,128]{1,0:T(8,128)(2,1)} %reshape.32.pts, f32[1,512]{1,0:T(1,128)} %bitcast.44), custom_call_target="tpu_custom_call" | custom-call | tf_op jit(solution)/shard_map/pallas_call | solution.py:137
  38.5 0.0 copy-start.2
  38.6 1.7 %reshape.34 = bf16[4096,64]{1,0:T(8,128)(2,1)S(1)} reshape(bf16[8,8,32,128]{3,2,1,0:T(8,128)(2,1)} %get-tuple-element.47) | data formatting | bytes 1048576 | tf_op jit(solution)/shard_map/reshape | solution.py:273
  40.3 0.0 copy-start
  40.3 0.6 multiply_reduce_fusion.1
  40.9 0.3 copy-done
  41.3 0.0 copy-done.2
  41.3 0.1 convert_multiply_fusion
  41.3 0.3 square.11
  41.7 0.0 copy-start.3
  41.7 0.0 copy-start.1
  41.7 0.6 reduce_sum.28
  42.3 1.6 %reshape_reshape.6 = bf16[2,2048,64]{2,1,0:T(8,128)(2,1)S(1)} reshape(bf16[8,256,128]{2,1,0:T(8,128)(2,1)} %get-tuple-element.48) | data formatting | bytes 1048576 | tf_op jit(solution)/shard_map/reshape;reshape | solution.py:242
  44.0 0.0 copy-done.3
  44.1 0.0 copy-done.1
  44.1 0.0 copy-start.6
  44.1 0.0 copy-start.7
  44.1 0.0 copy-start.4
  44.1 0.0 copy-start.5
  44.1 35.1 %while.11 = (s32[]{:T(128)}, f32[4096]{0:T(1024)S(1)}, f32[4096]{0:T(1024)S(1)}, f32[2,2048]{1,0:T(2,128)S(1)}, bf16[2,2048,64]{2,1,0:T(8,128)(2,1)S(1)}, /*inde...) while((s32[]{:T(128)}, f32[4096]{0:T(1024)S(1)}, ...), condition=%wide.region_4.5_spmd.clone, body=%wide.region_2.4_spmd.clone.sunk | while | flops 1157632000 | bytes 1704047 | solution.py:253
  44.2 17.5 %multiply_reduce_fusion.3 = f32[4096]{0:T(1024)S(1)} fusion(bf16[4096,64]{1,0:T(8,128)(2,1)S(1)} %get-tuple-element.166, f32[2048]{0:T(1024)S(1)} %bitcast.42, f32[2048]{0:T(1024)S(1)} %bitcast.43, f32[4096]{0:T(1024)S(1)} %get-tuple-element.163, bf16[2,2048,64]{2,1,0:T(8,128)(2,1)S(1)} %get-tuple-element.165, s32[]{:T(128)} %get-tuple-element.152), kind=kOutput, calls=%fused_computation.4.clone.1 | convolution fusion | flops 1157623808 | bytes 1622020 | tf_op jit(solution)/shard_map/while/body/eval_jaxpr/dot_general | solution.py:226
  61.7 17.5 %multiply_reduce_fusion.3 = f32[4096]{0:T(1024)S(1)} fusion(bf16[4096,64]{1,0:T(8,128)(2,1)S(1)} %get-tuple-element.166, f32[2048]{0:T(1024)S(1)} %bitcast.42, f32[2048]{0:T(1024)S(1)} %bitcast.43, f32[4096]{0:T(1024)S(1)} %get-tuple-element.163, bf16[2,2048,64]{2,1,0:T(8,128)(2,1)S(1)} %get-tuple-element.165, s32[]{:T(128)} %get-tuple-element.152), kind=kOutput, calls=%fused_computation.4.clone.1 | convolution fusion | flops 1157623808 | bytes 1622020 | tf_op jit(solution)/shard_map/while/body/eval_jaxpr/dot_general | solution.py:226
  79.3 0.7 reshape.36.part
  79.9 19.6 %shard_map.78 = f32[1,64]{1,0:T(1,128)} custom-call(f32[8,8,64]{2,1,0:T(8,128)} %reshape.36.part), custom_call_target="tpu_custom_call" | custom-call | tf_op jit(solution)/shard_map/pallas_call | solution.py:210
  100.1 0.0 copy-done.6
  100.2 0.0 copy-done.7
  100.2 0.9 fusion.7
  101.0 0.3 fusion.8
  101.3 0.0 copy-done.4
  101.3 0.0 copy-done.5
  101.3 0.6 fusion.16
  (9 shorter events, 0.1 us)
Async XLA Ops:
  38.5 2.7 %copy-start.2 = (bf16[8,256,128]{2,1,0:T(8,128)(2,1)S(1)}, bf16[8,256,128]{2,1,0:T(8,128)(2,1)}, u32[]{:S(2)}) copy-start(bf16[8,256,128]{2,1,0:T(8,128)(2,1)} %get-tuple-element.48) | copy-start | bytes 1572868
  40.3 1.0 copy-start
  41.7 2.3 %copy-start.3 = (f32[8,1,512]{2,1,0:T(1,128)S(1)}, f32[8,1,512]{2,1,0:T(1,128)}, u32[]{:S(2)}) copy-start(f32[8,1,512]{2,1,0:T(1,128)} %get-tuple-element.49) | copy-start | bytes 49156
  41.7 2.4 %copy-start.1 = (bf16[4096,64]{1,0:T(8,128)(2,1)S(1)}, bf16[4096,64]{1,0:T(8,128)(2,1)}, u32[]{:S(2)}) copy-start(bf16[4096,64]{1,0:T(8,128)(2,1)} %copy-done) | copy-start | bytes 1572868
  44.1 56.1 %copy-start.6 = (f32[512]{0:T(512)S(1)}, f32[512]{0:T(512)}, u32[]{:S(2)}) copy-start(f32[512]{0:T(512)} %get-tuple-element.92) | copy-start | bytes 6148
  44.1 56.1 %copy-start.7 = (s32[64]{0:T(128)S(1)}, s32[64]{0:T(128)}, u32[]{:S(2)}) copy-start(s32[64]{0:T(128)} %param.12) | copy-start | bytes 772
  44.1 57.2 %copy-start.4 = (f32[512]{0:T(512)S(1)}, f32[512]{0:T(512)}, u32[]{:S(2)}) copy-start(f32[512]{0:T(512)} %param.9) | copy-start | bytes 6148
  44.1 57.2 %copy-start.5 = (f32[512]{0:T(512)S(1)}, f32[512]{0:T(512)}, u32[]{:S(2)}) copy-start(f32[512]{0:T(512)} %param.10) | copy-start | bytes 6148

commit v22 on v16

--- a/solution.py
+++ b/solution.py
@@ -155,20 +155,37 @@
     n = greet_all(barrier, lambda i: dev(c, q, lax.rem(w + 1 + i, g)), g - 1, 0)
     n = greet_all(barrier, lambda i: dev(c, lax.rem(q + 1 + i, g), w), g - 1, n)
     pl.semaphore_wait(barrier, n)
-    own1 = pltpu.make_async_copy(part.at[q], stage1.at[q], local_sem.at[0])
+    own1 = pltpu.make_async_copy(part.at[w], stage1.at[w], local_sem.at[0])
     own1.start()
+
+    def inner_copy(i, src):
+        peer = lax.rem(w + 1 + i, g)
+        return pltpu.make_async_remote_copy(
+            src_ref=part.at[peer], dst_ref=stage1.at[src], send_sem=in_send.at[i],
+            recv_sem=in_recv.at[src], device_id=dev(c, q, peer), device_id_type=MESH_ID)
 
     def outer_copy(i, src):
         peer = lax.rem(q + 1 + i, g)
         return pltpu.make_async_remote_copy(
-            src_ref=part.at[peer], dst_ref=stage1.at[src], send_sem=out_send.at[i],
+            src_ref=mid.at[peer], dst_ref=stage2.at[src], send_sem=out_send.at[i],
             recv_sem=out_recv.at[src], device_id=dev(c, peer, w), device_id_type=MESH_ID)
 
-    def inner_copy(i, src):
-        peer = lax.rem(w + 1 + i, g)
-        return pltpu.make_async_remote_copy(
-            src_ref=mid.at[peer], dst_ref=stage2.at[src], send_sem=in_send.at[i],
-            recv_sem=in_recv.at[src], device_id=dev(c, q, peer), device_id_type=MESH_ID)
+    def start_inner(i, carry):
+        inner_copy(i, w).start()
+        return carry
+
+    lax.fori_loop(0, g - 1, start_inner, 0)
+
+    def wait_inner(i, carry):
+        inner_copy(i, w).wait_send()
+        inner_copy(i, lax.rem(w + 2 * g - 1 - i, g)).wait_recv()
+        return carry
+
+    lax.fori_loop(0, g - 1, wait_inner, 0)
+    own1.wait()
+    mid[...] = jnp.sum(stage1[...], axis=0)[:, None, :]
+    own2 = pltpu.make_async_copy(mid.at[q], stage2.at[q], local_sem.at[1])
+    own2.start()
 
     def start_outer(i, carry):
         outer_copy(i, q).start()
@@ -182,23 +199,6 @@
         return carry
 
     lax.fori_loop(0, g - 1, wait_outer, 0)
-    own1.wait()
-    mid[...] = jnp.sum(stage1[...], axis=0)[:, None, :]
-    own2 = pltpu.make_async_copy(mid.at[w], stage2.at[w], local_sem.at[1])
-    own2.start()
-
-    def start_inner(i, carry):
-        inner_copy(i, w).start()
-        return carry
-
-    lax.fori_loop(0, g - 1, start_inner, 0)
-
-    def wait_inner(i, carry):
-        inner_copy(i, w).wait_send()
-        inner_copy(i, lax.rem(w + 2 * g - 1 - i, g)).wait_recv()
-        return carry
-
-    lax.fori_loop(0, g - 1, wait_inner, 0)
     own2.wait()
     total_out[...] = jnp.sum(stage2[...], axis=0)
 
@@ -273,7 +273,8 @@
     piece_points = pts_all.reshape(-1, points.shape[1])
     every_coef = prev_all.reshape(-1)
     partial_value = column_sums(group_rows, piece_points, every_coef)
-    kernel_rows = scatter_all(partial_value.reshape(g, g, slot_total), g).reshape(-1)
+    by_w = partial_value.reshape(g, g, slot_total).transpose(1, 0, 2)
+    kernel_rows = scatter_all(by_w, g).reshape(-1)
     scatter_rows = (batch_rows[:, None] == jnp.arange(local_size, dtype=jnp.int32)[None, :]).astype(
         jnp.float32
     )

time: 101 us -> 101 us (level)
  no operation moved by 1% of the time
where the time goes in v22:
time: 101 us; the launch traced here: 100 us
  Pallas kernels  52.7 us (52%)
  matrix products  37.2 us (37%)
  local copies, waits for them, and re-layouts  5.53 us (5%)
  other arithmetic  3.26 us (3%)
  between operations  1.44 us (1%)
    dot_general x2, matrix products, matern_sums(): lax.dot_general(neg_two_rows, col_points, (((1,), (1,)), ((), ())), prefe...  35 us
    pallas_call x1, Pallas kernels, gather_all(): pl.pallas_call(functools.partial(gather_kernel, g), out_shape=(jax.ShapeD...  33.1 us
    pallas_call x1, Pallas kernels, scatter_all(): pl.pallas_call(functools.partial(scatter_kernel, g), out_shape=jax.ShapeD...  19.5 us

profile of v22, /device:TPU:8, one launch (start us, length us, event | category | flops | bytes accessed | tf_op | source)
XLA Modules:
  0.0 100.2 jit_solution(8011686682250566188)
XLA Ops:
  0.6 1.3 %multiply_subtract_fusion = (f32[512]{0:T(512)}, f32[512]{0:T(512)}) fusion(f32[512]{0:T(512)} %param.11, f32[512]{0:T(512)} %param.9, f32[512]{0:T(512)} %param.10), kind=kLoop, calls=%fused_computation.28 | loop fusion | flops 2048 | bytes 10240 | tf_op jit(solution)/shard_map/sub | solution.py:281
  1.9 1.0 copy.9
  2.9 0.7 reshape.27.pts
  3.6 1.1 %convolution_convert_fusion = bf16[64,64]{1,0:T(8,128)(2,1)S(1)} fusion(bf16[512,64]{0,1:T(8,128)(2,1)} %param.8, s32[64]{0:T(128)} %param.12), kind=kOutput, calls=%fused_computation.12 | convolution fusion | flops 4296704 | bytes 73984 | tf_op jit(solution)/shard_map/dot_general | solution.py:262
  4.7 0.7 reshape.26.picked
  5.4 33.1 %shard_map.77 = (bf16[8,8,32,128]{3,2,1,0:T(8,128)(2,1)}, bf16[8,256,128]{2,1,0:T(8,128)(2,1)}, f32[8,1,512]{2,1,0:T(1,128)}) custom-call(bf16[32,128]{1,0:T(8,128)(2,1)} %reshape.26.picked, bf16[256,128]{1,0:T(8,128)(2,1)} %reshape.27.pts, f32[1,512]{1,0:T(1,128)} %bitcast.47), custom_call_target="tpu_custom_call" | custom-call | tf_op jit(solution)/shard_map/pallas_call | solution.py:137
  38.5 0.0 copy-start
  38.5 1.7 %reshape.29 = bf16[4096,64]{1,0:T(8,128)(2,1)S(1)} reshape(bf16[8,8,32,128]{3,2,1,0:T(8,128)(2,1)} %get-tuple-element.42) | data formatting | bytes 1048576 | tf_op jit(solution)/shard_map/reshape | solution.py:272
  40.3 0.6 multiply_reduce_fusion.2
  40.9 0.0 copy-start.1
  40.9 0.0 copy-done
  40.9 0.4 reshape_reshape.6
  41.3 0.3 copy-done.1
  41.7 0.0 copy-start.4
  41.7 0.0 copy-start.5
  41.7 0.0 copy-start.2
  41.7 0.0 copy-start.3
  41.7 35.9 %while.11 = (s32[]{:T(128)}, f32[4096]{0:T(1024)S(1)}, f32[4096]{0:T(1024)S(1)}, bf16[2,2048,64]{2,1,0:T(8,128)(2,1)S(1)}, bf16[4096,64]{1,0:T(8,128)(2,1)S(1)},...) while((s32[]{:T(128)}, f32[4096]{0:T(1024)S(1)}, f32[4096]{0:T(1024)S(1)}, ...), condition=%wide.region_4.5_spmd.clone, body=%wide.region_1.4_spmd.clone.sunk | while | flops 1158023168 | bytes 1957995 | solution.py:252
  41.7 0.3 multiply_reduce_fusion.5
  42.1 17.5 %multiply_reduce_fusion.6 = f32[4096]{0:T(1024)S(1)} fusion(bf16[4096,64]{1,0:T(8,128)(2,1)S(1)} %get-tuple-element.141, f32[2048]{0:T(1024)S(1)} %bitcast.45, f32[2048]{0:T(1024)S(1)} %multiply_reduce_fusion.5, f32[4096]{0:T(1024)S(1)} %get-tuple-element.139, bf16[2,2048,64]{2,1,0:T(8,128)(2,1)S(1)} %get-tuple-element.140, s32[]{:T(128)} %get-tuple-element.129), kind=kOutput, calls=%fused_computation.4.clone.1 | convolution fusion | flops 1157623808 | bytes 1622020 | tf_op jit(solution)/shard_map/while/body/eval_jaxpr/dot_general | solution.py:227
  59.7 0.3 multiply_reduce_fusion.5
  60.0 17.5 %multiply_reduce_fusion.6 = f32[4096]{0:T(1024)S(1)} fusion(bf16[4096,64]{1,0:T(8,128)(2,1)S(1)} %get-tuple-element.141, f32[2048]{0:T(1024)S(1)} %bitcast.45, f32[2048]{0:T(1024)S(1)} %multiply_reduce_fusion.5, f32[4096]{0:T(1024)S(1)} %get-tuple-element.139, bf16[2,2048,64]{2,1,0:T(8,128)(2,1)S(1)} %get-tuple-element.140, s32[]{:T(128)} %get-tuple-element.129), kind=kOutput, calls=%fused_computation.4.clone.1 | convolution fusion | flops 1157623808 | bytes 1622020 | tf_op jit(solution)/shard_map/while/body/eval_jaxpr/dot_general | solution.py:227
  77.6 0.1 reshape.30
  77.7 0.6 copy.12
  78.3 19.5 %shard_map.78 = f32[1,64]{1,0:T(1,128)} custom-call(f32[8,8,64]{2,1,0:T(8,128)} %bitcast.46), custom_call_target="tpu_custom_call" | custom-call | tf_op jit(solution)/shard_map/pallas_call | solution.py:210
  98.5 0.0 copy-done.4
  98.5 0.0 copy-done.5
  98.5 0.8 fusion.7
  99.3 0.3 fusion.8
  99.6 0.0 copy-done.2
  99.6 0.0 copy-done.3
  99.6 0.6 fusion.16
  (8 shorter events, 0.1 us)
Async XLA Ops:
  38.5 2.4 %copy-start = (bf16[8,256,128]{2,1,0:T(8,128)(2,1)S(1)}, bf16[8,256,128]{2,1,0:T(8,128)(2,1)}, u32[]{:S(2)}) copy-start(bf16[8,256,128]{2,1,0:T(8,128)(2,1)} %get-tuple-element.43) | copy-start | bytes 1572868
  40.9 0.7 copy-start.1
  41.7 56.8 %copy-start.4 = (f32[512]{0:T(512)S(1)}, f32[512]{0:T(512)}, u32[]{:S(2)}) copy-start(f32[512]{0:T(512)} %get-tuple-element.82) | copy-start | bytes 6148
  41.7 56.8 %copy-start.5 = (s32[64]{0:T(128)S(1)}, s32[64]{0:T(128)}, u32[]{:S(2)}) copy-start(s32[64]{0:T(128)} %param.12) | copy-start | bytes 772
  41.7 57.9 %copy-start.2 = (f32[512]{0:T(512)S(1)}, f32[512]{0:T(512)}, u32[]{:S(2)}) copy-start(f32[512]{0:T(512)} %param.9) | copy-start | bytes 6148
  41.7 57.9 %copy-start.3 = (f32[512]{0:T(512)S(1)}, f32[512]{0:T(512)}, u32[]{:S(2)}) copy-start(f32[512]{0:T(512)} %param.10) | copy-start | bytes 6148
